TPU v7x, 128 devices: a whole 4x4x4 slice. The times are simulated.
128 devices in a mesh: dom: 16 (over z, x), band: 8 (over y, core).
Axes of the slice: x: 4, y: 4, z: 4, core: 2. Of those that a mesh axis runs over, the one named last changes fastest.
Arguments:
- orbitals_now: bfloat16 [256, 512, 512], P('dom', 'band'), may hold values from -6 to 6
- orbitals_prev: bfloat16 [256, 512, 512], P('dom', 'band'), may hold values from -6 to 6
- interp: bfloat16 [8, 512, 512], replicated, may hold values from -0.25 to 0.25
- owner_map: int32 [256], replicated, may hold values from 0 to 15, as said below
- child_oct: int32 [256, 2], replicated, may hold values from 0 to 7, all different within a row
Outputs:
- predicted: bfloat16 [1024, 512, 512], P(('dom', 'band'))
Inputs may be any that keep to these rules, and one draw needn't show every extreme that they name: `owner_map`: among the 16 cells of one domain at most 2 have the same owner; in every draw one owner receives exactly 2 cells from every domain.
All inputs are finite; a program needn't handle non-finite values.
Results may differ from a plain program's by a relative error of at most 0.0059.
Values may be sent and summed in bfloat16 or wider, within the bound.
No kernel may reach another device: no remote copies, remote signals or barrier semaphores. Data moves between devices by JAX's collectives and lax.ppermute only.
A program may use at most 128 MiB of HBM per device.

v0:
```python
import functools
import math

import jax
import jax.numpy as jnp
from jax import lax
from jax.experimental import pallas as pl
from jax.experimental.pallas import tpu as pltpu
from jax.sharding import Mesh
from jax.sharding import PartitionSpec as P


Z, X, Y, C = "dom_0", "dom_1", "band_0", "band_1"
DOM = (Z, X)
BAND = (Y, C)
DOM_BAND = (Z, X, Y, C)
CHIPS = (Z, X, Y)

BF16 = jnp.bfloat16
F32 = jnp.float32
RING = 4
CORES = 2
OFFSETS = tuple((q, l) for q in range(RING) for l in range(CORES))


SMEM = pl.BlockSpec(memory_space=pltpu.SMEM)
ANY = pl.BlockSpec(memory_space=pl.ANY)


def band_pairs(q, l):
    return [
        (y * CORES + c, ((y + q) % RING) * CORES + (c + l) % CORES)
        for y in range(RING)
        for c in range(CORES)
    ]


def over_band(pieces):
    return [
        lax.ppermute(piece, BAND, band_pairs(q, l)) for (q, l), piece in zip(OFFSETS[1:], pieces)
    ]


def run_copies(copies):
    for copy in copies:
        copy.start()
    for copy in copies:
        copy.wait()


def sized(shape, dtype=BF16):
    return jax.ShapeDtypeStruct(shape, dtype)


def moved(read, written, flops=0):
    return pl.CostEstimate(flops=flops, bytes_accessed=read + written, transcendentals=0)


def cells_kernel(at, now, prev, *refs):
    outs, (buf, in_sem, out_sem) = refs[:7], refs[7:]
    y, c = at[2], at[3]
    loads, stores = [], []
    for n, (q, l) in enumerate(OFFSETS[1:]):
        first = (((y + q) & 3) * CORES + ((c + l) & 1)) * 2
        loads.append(
            [
                pltpu.make_async_copy(src.at[pl.ds(first, 2)], buf.at[n, a], in_sem.at[n, a])
                for a, src in enumerate((now, prev))
            ]
        )
        stores.append(pltpu.make_async_copy(buf.at[n], outs[n], out_sem.at[n]))
    for pair in loads:
        for copy in pair:
            copy.start()
    for pair, store in zip(loads, stores):
        for copy in pair:
            copy.wait()
        store.start()
    for store in stores:
        store.wait()


def cells_for_band(at, now, prev):
    _, rows, nodes = now.shape
    piece = (2, 2, rows, nodes)
    size = 4 * rows * nodes * 2
    return pl.pallas_call(
        cells_kernel,
        out_shape=[sized(piece)] * 7,
        in_specs=[SMEM, ANY, ANY],
        out_specs=[ANY] * 7,
        scratch_shapes=[
            pltpu.VMEM((7, *piece), BF16),
            pltpu.SemaphoreType.DMA((7, 2)),
            pltpu.SemaphoreType.DMA((7,)),
        ],
        cost_estimate=moved(7 * size, 7 * size),
        name="cells_for_band",
    )(at, now, prev)


def product_kernel(at, octants, now, prev, *refs):
    pieces, interp, mine, other = refs[:7], refs[7], refs[8], refs[9]
    parents, matrices, kids, out, in_sem, mat_sem, out_sem = refs[10:]
    z, x, y, c = at[0], at[1], at[2], at[3]
    rows = now.shape[1]
    nodes = now.shape[2]
    states = parents.shape[2]
    half = states // 2
    first = (y * CORES + c) * 2
    cell0 = (z * RING + x) * now.shape[0] + first
    copies = []
    for e in range(2):
        for j in range(2):
            o = octants[(cell0 + e) * 2 + j]
            copies.append(
                pltpu.make_async_copy(interp.at[o], matrices.at[e, j], mat_sem.at[e, j])
            )
    own = pl.ds(pl.multiple_of((y * CORES + c) * rows, rows), rows)
    for a, src in enumerate((now, prev)):
        copies.append(
            pltpu.make_async_copy(
                src.at[pl.ds(first, 2)], parents.at[a, :, own], in_sem.at[7 + a]
            )
        )
    for n, (q, l) in enumerate(OFFSETS[1:]):
        b = ((y - q) & 3) * CORES + ((c - l) & 1)
        to = pl.ds(pl.multiple_of(b * rows, rows), rows)
        copies.append(
            pltpu.make_async_copy(pieces[n], parents.at[:, :, to], in_sem.at[n])
        )
    run_copies(copies)
    for a in range(2):
        for e in range(2):
            for j in range(2):
                kids[a, :, pl.ds((e * 2 + j) * nodes, nodes)] = lax.dot_general(
                    parents[a, e],
                    matrices[e, j],
                    (((1,), (1,)), ((), ())),
                    preferred_element_type=F32,
                ).astype(BF16)
    stores = []
    for n, (side, dst) in enumerate(((c, mine), (1 - c, other))):
        u = pl.ds(pl.multiple_of(side * half, half), half)
        part = lax.dot_general(
            kids[1, u, :], kids[0], (((1,), (1,)), ((), ())), preferred_element_type=F32
        )
        for t in range(states // 128):
            out[n, t] = part[:, t * 128 : (t + 1) * 128]
        stores.append(pltpu.make_async_copy(out.at[n], dst, out_sem.at[n]))
        stores[-1].start()
    for store in stores:
        store.wait()


def product_of_cells(at, octants, now, prev, pieces, interp):
    _, rows, nodes = now.shape
    states = rows * RING * CORES
    lanes = (states // 128, states // 2, 128)
    return pl.pallas_call(
        product_kernel,
        out_shape=[sized(lanes, F32)] * 2,
        in_specs=[SMEM, SMEM] + [ANY] * 10,
        out_specs=[ANY] * 2,
        scratch_shapes=[
            pltpu.VMEM((2, 2, states, nodes), BF16),
            pltpu.VMEM((2, 2, nodes, nodes), BF16),
            pltpu.VMEM((2, states, 4 * nodes), BF16),
            pltpu.VMEM((2, *lanes), F32),
            pltpu.SemaphoreType.DMA((9,)),
            pltpu.SemaphoreType.DMA((2, 2)),
            pltpu.SemaphoreType.DMA((2,)),
        ],
        cost_estimate=moved(4 << 20, 1 << 20, 24 * states * nodes * nodes),
        name="product_of_cells",
    )(at, octants, now, prev, *pieces, interp)


def summed_over_all(mine, other, scaling):
    swap = [(0, 1), (1, 0)]
    half = mine + lax.ppermute(other, C, swap)
    chips = lax.axis_size(CHIPS)
    shape = half.shape
    blocks = half.reshape(chips, -1, 128)
    tiles = lax.all_to_all(blocks, CHIPS, 0, 0, tiled=True)
    own = (jnp.sum(tiles, axis=0) * scaling).astype(BF16)
    own = jnp.broadcast_to(own[None], (chips, *own.shape))
    own = lax.all_to_all(own, CHIPS, 0, 0, tiled=True)
    own = own.reshape(shape)
    return own, lax.ppermute(own, C, swap)


def slots_kernel(rank, at, owners, now, prev, out, cells, slot, seen, in_sem, out_sem):
    z, x = at[0], at[1]
    old = now.shape[0]
    first = (z * RING + x) * old
    loads = [
        pltpu.make_async_copy(src, cells.at[a], in_sem.at[a]) for a, src in enumerate((now, prev))
    ]
    for load in loads:
        load.start()
    for d in range(RING * RING):
        seen[d] = 0
        slot[d] = 0

    def place(i, carry):
        owner = owners[first + i]
        slot[owner] = jnp.where(seen[owner] == rank, i, slot[owner])
        seen[owner] = seen[owner] + 1
        return carry

    lax.fori_loop(0, old, place, 0)
    stores = []
    for a in range(2):
        loads[a].wait()
        for d in range(RING * RING):
            stores.append(
                pltpu.make_async_copy(cells.at[a, slot[d]], out.at[d, a], out_sem.at[a, d])
            )
            stores[-1].start()
    for store in stores:
        store.wait()


def slots_for_owners(rank, at, owners, now, prev):
    old, rows, nodes = now.shape
    doms = RING * RING
    size = 2 * old * rows * nodes * 2
    return pl.pallas_call(
        functools.partial(slots_kernel, rank),
        out_shape=sized((doms, 2, rows, nodes)),
        in_specs=[SMEM, SMEM, ANY, ANY],
        out_specs=ANY,
        scratch_shapes=[
            pltpu.VMEM((2, old, rows, nodes), BF16),
            pltpu.SMEM((doms,), jnp.int32),
            pltpu.SMEM((doms,), jnp.int32),
            pltpu.SemaphoreType.DMA((2,)),
            pltpu.SemaphoreType.DMA((2, doms)),
        ],
        cost_estimate=moved(size, size),
    )(at, owners, now, prev)


def route_kernel(at, slots, *refs):
    outs, (buf, in_sem, out_sem) = refs[:7], refs[7:]
    y, c = at[2], at[3]
    loads, stores = [], []
    for n, (q, l) in enumerate(OFFSETS[1:]):
        first = (((y + q) & 3) * CORES + ((c + l) & 1)) * 2
        loads.append(pltpu.make_async_copy(slots.at[pl.ds(first, 2)], buf.at[n], in_sem.at[n]))
        stores.append(pltpu.make_async_copy(buf.at[n], outs[n], out_sem.at[n]))
    for load in loads:
        load.start()
    for load, store in zip(loads, stores):
        load.wait()
        store.start()
    for store in stores:
        store.wait()


def routed(at, slots):
    piece = (2, *slots.shape[1:])
    size = 7 * math.prod(piece) * 2
    return pl.pallas_call(
        route_kernel,
        out_shape=[sized(piece)] * 7,
        in_specs=[SMEM, ANY],
        out_specs=[ANY] * 7,
        scratch_shapes=[
            pltpu.VMEM((7, *piece), BF16),
            pltpu.SemaphoreType.DMA((7,)),
            pltpu.SemaphoreType.DMA((7,)),
        ],
        cost_estimate=moved(size, size),
    )(at, slots)


def predict_kernel(rank, old, at, owners, octants, *refs):
    slots, pieces, mine, other, interp = refs[0], refs[1:8], refs[8], refs[9], refs[10]
    predicted = refs[11 + rank]
    parents, matrices, mix, out, in_sem, mat_sem, mix_sem, out_sem = refs[12 + rank :]
    z, x, y, c = at[0], at[1], at[2], at[3]
    rows = pieces[0].shape[2]
    blocks, half, _ = mine.shape
    owner = z * RING + x
    copies, filled = [], []
    for e in range(2):
        first = (RING * y + 2 * c + e) * old

        def look(i, carry, first=first):
            count, cell = carry
            match = owners[first + i] == owner
            cell = jnp.where(match & (count == rank), i, cell)
            return count + match.astype(jnp.int32), cell

        count, cell = lax.fori_loop(0, old, look, (jnp.int32(0), jnp.int32(0)))
        filled.append(count > rank)
        for j in range(2):
            o = octants[(first + cell) * 2 + j]
            copies.append(
                pltpu.make_async_copy(interp.at[o], matrices.at[e, j], mat_sem.at[e, j])
            )
    for n, (q, l) in enumerate(OFFSETS):
        b = ((y - q) & 3) * CORES + ((c - l) & 1)
        to = pl.ds(pl.multiple_of(b * rows, rows), rows)
        src = pieces[n - 1] if n else slots.at[pl.ds(b * 2, 2)]
        copies.append(pltpu.make_async_copy(src, parents.at[:, :, to], in_sem.at[n]))
    for n, (side, src) in enumerate(((c, mine), (1 - c, other))):
        u = pl.ds(pl.multiple_of(side * half, half), half)
        for t in range(blocks):
            copies.append(
                pltpu.make_async_copy(
                    src.at[t], mix.at[u, pl.ds(t * 128, 128)], mix_sem.at[n, t]
                )
            )
    run_copies(copies)
    stores = []
    for e in range(2):

        @pl.when(filled[e])
        def _(e=e):
            mixed = jnp.dot(mix[...], parents[e, 0], preferred_element_type=F32)
            value = (parents[e, 1].astype(F32) + mixed).astype(BF16)
            for j in range(2):
                out[e, j] = lax.dot_general(
                    value, matrices[e, j], (((1,), (1,)), ((), ())), preferred_element_type=F32
                ).astype(BF16)

        @pl.when(jnp.logical_not(filled[e]))
        def _(e=e):
            out[e] = jnp.zeros(out.shape[1:], BF16)

        stores.append(
            pltpu.make_async_copy(
                out.at[e], predicted.at[pl.ds(e * 4 + rank * 2, 2)], out_sem.at[e]
            )
        )
        stores[-1].start()
    for store in stores:
        store.wait()


def predict(rank, old, at, owners, octants, slots, pieces, mine, other, interp, earlier=None):
    _, _, rows, nodes = pieces[0].shape
    states = rows * RING * CORES
    operands = [at, owners, octants, slots, *pieces, mine, other, interp]
    if earlier is not None:
        operands.append(earlier)
    return pl.pallas_call(
        functools.partial(predict_kernel, rank, old),
        out_shape=sized((8, states, nodes)),
        in_specs=[SMEM] * 3 + [ANY] * (len(operands) - 3),
        out_specs=ANY,
        scratch_shapes=[
            pltpu.VMEM((2, 2, states, nodes), BF16),
            pltpu.VMEM((2, 2, nodes, nodes), BF16),
            pltpu.VMEM((states, states), BF16),
            pltpu.VMEM((2, 2, states, nodes), BF16),
            pltpu.SemaphoreType.DMA((8,)),
            pltpu.SemaphoreType.DMA((2, 2)),
            pltpu.SemaphoreType.DMA((2, states // 128)),
            pltpu.SemaphoreType.DMA((2,)),
        ],
        input_output_aliases={} if earlier is None else {len(operands) - 1: 0},
        cost_estimate=moved(5 << 20, 2 << 20, 12 * states * nodes * nodes),
    )(*operands)


def refined(orbitals_now, orbitals_prev, interp, owner_map, child_oct):
    old, rows, nodes = orbitals_now.shape
    states = rows * lax.axis_size(BAND)
    at = jnp.stack([lax.axis_index(a) for a in DOM_BAND]).astype(jnp.int32)
    octants = child_oct.reshape(-1)
    scaling = 1.0 / math.sqrt(2.0 * states * owner_map.shape[0] * nodes)

    slots, pieces = [], []
    for rank in range(2):
        slots.append(slots_for_owners(rank, at, owner_map, orbitals_now, orbitals_prev))
        slots[rank] = lax.all_to_all(slots[rank], DOM, 0, 0, tiled=True)
        pieces.append(routed(at, slots[rank]))
        pieces[rank] = over_band(pieces[rank])

    cells = cells_for_band(at, orbitals_now, orbitals_prev)
    cells = over_band(cells)
    mine, other = product_of_cells(at, octants, orbitals_now, orbitals_prev, cells, interp)
    mine, other = summed_over_all(mine, other, scaling)

    out = predict(0, old, at, owner_map, octants, slots[0], pieces[0], mine, other, interp)
    return predict(1, old, at, owner_map, octants, slots[1], pieces[1], mine, other, interp, out)


def solution(mesh):
    split = Mesh(mesh.devices.reshape(4, 4, 4, 2), DOM_BAND)
    placed = (P(DOM, BAND, None), P(DOM, BAND, None), P(), P(), P())
    return jax.shard_map(
        refined, mesh=split, in_specs=placed, out_specs=P(DOM_BAND, None, None), check_vma=False
    )
```

profile of v0, /device:TPU:1, one launch (start us, length us, event | category | flops | bytes accessed | tf_op | source)
XLA Modules:
  0.0 215.4 jit_solution(16280504158930423564)
XLA Ops:
  0.0 0.6 pad_add_fusion.at
  0.6 3.1 %cells_for_band.1 = (bf16[2,2,64,512]{3,2,1,0:T(8,128)(2,1)}, bf16[2,2,64,512]{3,2,1,0:T(8,128)(2,1)}, bf16[2,2,64,512]{3,2,1,0:T(8,128)(2,1)}, bf16[2,2,64,512]...) custom-call(s32[4]{0:T(128)} %pad_add_fusion.at, ...), custom_call_target="tpu_custom_call" | custom-call | bytes 3670016 | tf_op jit(solution)/shard_map/cells_for_band/pallas_call | solution.py:87
  3.7 1.5 collective-permute-start.7
  5.2 1.4 collective-permute-start.8
  6.6 1.5 collective-permute-start.9
  8.1 1.2 collective-permute-start.10
  9.3 2.1 collective-permute-start.11
  11.4 0.0 collective-permute-done.7.refs_0_
  11.4 1.4 collective-permute-start.12
  12.8 1.9 collective-permute-done.8.refs_1_
  14.7 2.7 %collective-permute-start.13 = (bf16[2,2,64,512]{3,2,1,0:T(8,128)(2,1)}, bf16[2,2,64,512]{3,2,1,0:T(8,128)(2,1)S(1)}, u32[]{:S(2)}, u32[]{:S(2)}) collective-permute-start(bf16[2,2,64,512]{3,2,1,0:T(8,128)(2,1)} %get-tuple-element.41), channel_id=1, source_target_pairs={{0,7},{1,6},{2,1},{3,0},{4,3},{5,2},{6,5},{7,4},{8,15},{9,14},{10,... | collective-permute-start | bytes 786440 | tf_op jit(solution)/shard_map/ppermute | solution.py:40
  17.4 0.1 copy.7
  17.5 0.7 reshape.13.octants
  18.2 2.2 %collective-permute-done.9.refs_2_ = bf16[2,2,64,512]{3,2,1,0:T(8,128)(2,1)S(1)} collective-permute-done((bf16[2,2,64,512]{3,2,1,0:T(8,128)(2,1)}, bf16[2,2,64,512]{3,2,1,0:T(8,128)(2,1)S(1)}, u32[]{:S(2)}, u32[]{:S(2)}) %collective-permute-start.9) | collective-permute-done | bytes 262176 | tf_op jit(solution)/shard_map/ppermute | solution.py:40
  20.4 6.5 %collective-permute-done.10.refs_3_ = bf16[2,2,64,512]{3,2,1,0:T(8,128)(2,1)S(1)} collective-permute-done((bf16[2,2,64,512]{3,2,1,0:T(8,128)(2,1)}, bf16[2,2,64,512]{3,2,1,0:T(8,128)(2,1)S(1)}, u32[]{:S(2)}, u32[]{:S(2)}) %collective-permute-start.10) | collective-permute-done | bytes 262176 | tf_op jit(solution)/shard_map/ppermute | solution.py:40
  27.0 5.9 %collective-permute-done.11.refs_4_ = bf16[2,2,64,512]{3,2,1,0:T(8,128)(2,1)S(1)} collective-permute-done((bf16[2,2,64,512]{3,2,1,0:T(8,128)(2,1)}, bf16[2,2,64,512]{3,2,1,0:T(8,128)(2,1)S(1)}, u32[]{:S(2)}, u32[]{:S(2)}) %collective-permute-start.11) | collective-permute-done | bytes 262176 | tf_op jit(solution)/shard_map/ppermute | solution.py:40
  32.8 0.9 collective-permute-done.13.refs_6_
  33.8 0.7 copy-done.25
  34.5 7.4 %product_of_cells.1 = (f32[4,256,128]{2,1,0:T(8,128)}, f32[4,256,128]{2,1,0:T(8,128)}) custom-call(s32[4]{0:T(128)} %pad_add_fusion.at, s32[512]{0:T(512)} %reshape.13.octants, bf16[16,64,512]{2,1,0:T(8,128)(2,1)} %now.7, bf16[16,64,512]{2,1,0:T(8,128)(2,1)} %prev.7, bf16[2,2,64,512]{3,2,1,0:T(8,128)(2,1)} %copy-done.19, bf16[2,2,64,512]{3,2,1,0:T(8,128)(2,1)} %copy-done.20, ...), custom_call_target="tpu_custom_call" | custom-call | flops 3221225472 | bytes 5242880 | tf_op jit(solution)/shard_map/product_of_cells/pallas_call | solution.py:160
  41.9 0.2 collective-permute-start.14
  42.1 2.0 collective-permute-done.14
  44.1 1.1 add.3
  45.3 22.9 %all_to_all.20 = f32[64,16,128]{2,1,0:T(8,128)S(1)} all-to-all(f32[64,16,128]{2,1,0:T(8,128)S(1)} %bitcast.9), channel_id=1, replica_groups=mesh['dom_0'=4,'dom_1'=4,'band_0'=4,'band_1'=2] {'dom_0','dom_1','band_0'}, dimensions={0} | all-to-all | bytes 1048576 | tf_op jit(solution)/shard_map/all_to_all | solution.py:185
  68.1 0.1 reduce_sum.9
  68.2 0.7 broadcast_in_dim.2
  69.0 4.7 %all-to-all-start.2 = ((bf16[64,16,128]{2,1,0:T(8,128)(2,1)}), bf16[64,16,128]{2,1,0:T(8,128)(2,1)S(1)}, u32[]{:S(2)}, u32[]{:S(2)}) async-start(bf16[64,16,128]{2,1,0:T(8,128)(2,1)} %broadcast_in_dim.2), calls=%async_computation.2 | async-start | bytes 524288 | tf_op jit(solution)/shard_map/all_to_all | solution.py:188
  73.7 3.5 %shard_map.55 = bf16[16,2,64,512]{3,2,1,0:T(8,128)(2,1)} custom-call(s32[4]{0:T(128)} %pad_add_fusion.at, s32[256]{0:T(256)} %owners.7, bf16[16,64,512]{2,1,0:T(8,128)(2,1)} %now.7, bf16[16,64,512]{2,1,0:T(8,128)(2,1)} %prev.7), custom_call_target="tpu_custom_call" | custom-call | bytes 4194304 | tf_op jit(solution)/shard_map/pallas_call | solution.py:229
  77.2 5.9 %all-to-all-done.2 = bf16[64,16,128]{2,1,0:T(8,128)(2,1)S(1)} async-done(((bf16[64,16,128]{2,1,0:T(8,128)(2,1)}), bf16[64,16,128]{2,1,0:T(8,128)(2,1)S(1)}, u32[]{:S(2)}, u32[]{:S(2)}) %all-to-all-start.2) | async-done | bytes 262176 | tf_op jit(solution)/shard_map/all_to_all | solution.py:188
  83.1 3.7 %all-to-all-start = ((bf16[16,2,64,512]{3,2,1,0:T(8,128)(2,1)}), bf16[16,2,64,512]{3,2,1,0:T(8,128)(2,1)S(1)}, u32[]{:S(2)}, u32[]{:S(2)}) async-start(bf16[16,2,64,512]{3,2,1,0:T(8,128)(2,1)} %shard_map.55), calls=%async_computation | async-start | bytes 4194304 | tf_op jit(solution)/shard_map/all_to_all | solution.py:380
  86.8 3.6 %shard_map.57 = bf16[16,2,64,512]{3,2,1,0:T(8,128)(2,1)} custom-call(s32[4]{0:T(128)} %pad_add_fusion.at, s32[256]{0:T(256)} %owners.7, bf16[16,64,512]{2,1,0:T(8,128)(2,1)} %now.7, bf16[16,64,512]{2,1,0:T(8,128)(2,1)} %prev.7), custom_call_target="tpu_custom_call" | custom-call | bytes 4194304 | tf_op jit(solution)/shard_map/pallas_call | solution.py:229
  90.4 21.4 %all-to-all-done.slots.refs_0_ = bf16[16,2,64,512]{3,2,1,0:T(8,128)(2,1)S(1)} async-done(((bf16[16,2,64,512]{3,2,1,0:T(8,128)(2,1)}), bf16[16,2,64,512]{3,2,1,0:T(8,128)(2,1)S(1)}, u32[]{:S(2)}, u32[]{:S(2)}) %all-to-all-start) | async-done | bytes 2097184 | tf_op jit(solution)/shard_map/all_to_all | solution.py:380
  111.8 1.3 copy-done.1
  113.2 7.1 %all-to-all-start.3 = ((bf16[16,2,64,512]{3,2,1,0:T(8,128)(2,1)}), bf16[16,2,64,512]{3,2,1,0:T(8,128)(2,1)S(1)}, u32[]{:S(2)}, u32[]{:S(2)}) async-start(bf16[16,2,64,512]{3,2,1,0:T(8,128)(2,1)} %shard_map.57), calls=%async_computation.3 | async-start | bytes 4194304 | tf_op jit(solution)/shard_map/all_to_all | solution.py:380
  120.3 2.3 %collective-permute-start.15 = (bf16[4,256,128]{2,1,0:T(8,128)(2,1)S(1)}, bf16[4,256,128]{2,1,0:T(8,128)(2,1)S(1)}, u32[]{:S(2)}, u32[]{:S(2)}) collective-permute-start(bf16[4,256,128]{2,1,0:T(8,128)(2,1)S(1)} %bitcast.6), channel_id=1, source_target_pairs={{0,1},{1,0},{2,3},{3,2},{4,5},{5,4},{6,7},{7,6},{8,9},{9,8},{10,11... | collective-permute-start | bytes 786440 | tf_op jit(solution)/shard_map/ppermute | solution.py:190
  122.6 3.0 %shard_map.56 = (bf16[2,2,64,512]{3,2,1,0:T(8,128)(2,1)}, bf16[2,2,64,512]{3,2,1,0:T(8,128)(2,1)}, bf16[2,2,64,512]{3,2,1,0:T(8,128)(2,1)}, bf16[2,2,64,512]{3,2...) custom-call(s32[4]{0:T(128)} %pad_add_fusion.at, ...), custom_call_target="tpu_custom_call" | custom-call | bytes 3670016 | tf_op jit(solution)/shard_map/pallas_call | solution.py:265
  125.6 0.1 collective-permute-start
  125.7 0.4 collective-permute-start.1
  126.1 21.0 %all-to-all-done.3.slots.refs_0_ = bf16[16,2,64,512]{3,2,1,0:T(8,128)(2,1)S(1)} async-done(((bf16[16,2,64,512]{3,2,1,0:T(8,128)(2,1)}), bf16[16,2,64,512]{3,2,1,0:T(8,128)(2,1)S(1)}, u32[]{:S(2)}, u32[]{:S(2)}) %all-to-all-start.3) | async-done | bytes 2097184 | tf_op jit(solution)/shard_map/all_to_all | solution.py:380
  147.1 1.4 copy-done
  148.4 3.0 %shard_map.58 = (bf16[2,2,64,512]{3,2,1,0:T(8,128)(2,1)}, bf16[2,2,64,512]{3,2,1,0:T(8,128)(2,1)}, bf16[2,2,64,512]{3,2,1,0:T(8,128)(2,1)}, bf16[2,2,64,512]{3,2...) custom-call(s32[4]{0:T(128)} %pad_add_fusion.at, ...), custom_call_target="tpu_custom_call" | custom-call | bytes 3670016 | tf_op jit(solution)/shard_map/pallas_call | solution.py:265
  151.4 4.8 %collective-permute-start.16 = (bf16[2,2,64,512]{3,2,1,0:T(8,128)(2,1)}, bf16[2,2,64,512]{3,2,1,0:T(8,128)(2,1)S(1)}, u32[]{:S(2)}, u32[]{:S(2)}) collective-permute-start(bf16[2,2,64,512]{3,2,1,0:T(8,128)(2,1)} %get-tuple-element.44), channel_id=1, source_target_pairs={{0,1},{1,0},{2,3},{3,2},{4,5},{5,4},{6,7},{7,6},{8,9},{9,8},{10,11... | collective-permute-start | bytes 786440 | tf_op jit(solution)/shard_map/ppermute | solution.py:40
  156.3 0.3 collective-permute-start.17
  156.6 0.3 collective-permute-start.18
  156.9 0.0 collective-permute-done.refs_1_
  156.9 3.5 %collective-permute-start.19 = (bf16[2,2,64,512]{3,2,1,0:T(8,128)(2,1)}, bf16[2,2,64,512]{3,2,1,0:T(8,128)(2,1)S(1)}, u32[]{:S(2)}, u32[]{:S(2)}) collective-permute-start(bf16[2,2,64,512]{3,2,1,0:T(8,128)(2,1)} %get-tuple-element.47), channel_id=1, source_target_pairs={{0,4},{1,5},{2,6},{3,7},{4,0},{5,1},{6,2},{7,3},{8,12},{9,13},{10,... | collective-permute-start | bytes 786440 | tf_op jit(solution)/shard_map/ppermute | solution.py:40
  160.4 0.1 collective-permute-start.20
  160.5 2.3 %collective-permute-start.21 = (bf16[2,2,64,512]{3,2,1,0:T(8,128)(2,1)}, bf16[2,2,64,512]{3,2,1,0:T(8,128)(2,1)S(1)}, u32[]{:S(2)}, u32[]{:S(2)}) collective-permute-start(bf16[2,2,64,512]{3,2,1,0:T(8,128)(2,1)} %get-tuple-element.49), channel_id=1, source_target_pairs={{0,6},{1,7},{2,0},{3,1},{4,2},{5,3},{6,4},{7,5},{8,14},{9,15},{10,... | collective-permute-start | bytes 786440 | tf_op jit(solution)/shard_map/ppermute | solution.py:40
  162.8 2.6 %collective-permute-done.17.refs_2_ = bf16[2,2,64,512]{3,2,1,0:T(8,128)(2,1)S(1)} collective-permute-done((bf16[2,2,64,512]{3,2,1,0:T(8,128)(2,1)}, bf16[2,2,64,512]{3,2,1,0:T(8,128)(2,1)S(1)}, u32[]{:S(2)}, u32[]{:S(2)}) %collective-permute-start.17) | collective-permute-done | bytes 262176 | tf_op jit(solution)/shard_map/ppermute | solution.py:40
  165.5 0.7 collective-permute-start.22
  166.2 16.4 %collective-permute-done.18.refs_3_ = bf16[2,2,64,512]{3,2,1,0:T(8,128)(2,1)S(1)} collective-permute-done((bf16[2,2,64,512]{3,2,1,0:T(8,128)(2,1)}, bf16[2,2,64,512]{3,2,1,0:T(8,128)(2,1)S(1)}, u32[]{:S(2)}, u32[]{:S(2)}) %collective-permute-start.18) | collective-permute-done | bytes 262176 | tf_op jit(solution)/shard_map/ppermute | solution.py:40
  182.6 0.0 collective-permute-done.19.refs_4_
  182.6 1.1 collective-permute-start.3
  183.8 2.2 %collective-permute-start.4 = (bf16[2,2,64,512]{3,2,1,0:T(8,128)(2,1)}, bf16[2,2,64,512]{3,2,1,0:T(8,128)(2,1)S(1)}, u32[]{:S(2)}, u32[]{:S(2)}) collective-permute-start(bf16[2,2,64,512]{3,2,1,0:T(8,128)(2,1)} %get-tuple-element.32), channel_id=1, source_target_pairs={{0,5},{1,4},{2,7},{3,6},{4,1},{5,0},{6,3},{7,2},{8,13},{9,12},{10,... | collective-permute-start | bytes 786440 | tf_op jit(solution)/shard_map/ppermute | solution.py:40
  186.0 0.7 copy-done.16
  186.7 2.8 %collective-permute-start.5 = (bf16[2,2,64,512]{3,2,1,0:T(8,128)(2,1)}, bf16[2,2,64,512]{3,2,1,0:T(8,128)(2,1)S(1)}, u32[]{:S(2)}, u32[]{:S(2)}) collective-permute-start(bf16[2,2,64,512]{3,2,1,0:T(8,128)(2,1)} %get-tuple-element.33), channel_id=1, source_target_pairs={{0,6},{1,7},{2,0},{3,1},{4,2},{5,3},{6,4},{7,5},{8,14},{9,15},{10,... | collective-permute-start | bytes 786440 | tf_op jit(solution)/shard_map/ppermute | solution.py:40
  189.5 0.0 collective-permute-done.22.refs_7_
  189.5 0.7 copy-done.17
  190.3 6.6 %shard_map.59.refs_11_ = bf16[8,512,512]{2,1,0:T(8,128)(2,1)} custom-call(s32[4]{0:T(128)} %pad_add_fusion.at, s32[256]{0:T(256)} %owners.7, s32[512]{0:T(512)} %reshape.13.octants, bf16[16,2,64,512]{3,2,1,0:T(8,128)(2,1)} %copy-done, bf16[2,2,64,512]{3,2,1,0:T(8,128)(2,1)} %copy-done.11, bf16[2,2,64,512]{3,2,1,0:T(8,128)(2,1)} %copy-done.12, ...), custom_call_target="tpu_custom_call" | custom-call | flops 1610612736 | bytes 7340032 | tf_op jit(solution)/shard_map/pallas_call | solution.py:350
  196.9 6.4 %collective-permute-done.2.refs_3_ = bf16[2,2,64,512]{3,2,1,0:T(8,128)(2,1)S(1)} collective-permute-done((bf16[2,2,64,512]{3,2,1,0:T(8,128)(2,1)}, bf16[2,2,64,512]{3,2,1,0:T(8,128)(2,1)S(1)}, u32[]{:S(2)}, u32[]{:S(2)}) %collective-permute-start.2) | collective-permute-done | bytes 262176 | tf_op jit(solution)/shard_map/ppermute | solution.py:40
  203.3 0.0 collective-permute-done.4.refs_5_
  203.3 0.1 collective-permute-done.5.refs_6_
  203.4 6.1 %collective-permute-done.6.refs_7_ = bf16[2,2,64,512]{3,2,1,0:T(8,128)(2,1)S(1)} collective-permute-done((bf16[2,2,64,512]{3,2,1,0:T(8,128)(2,1)}, bf16[2,2,64,512]{3,2,1,0:T(8,128)(2,1)S(1)}, u32[]{:S(2)}, u32[]{:S(2)}) %collective-permute-start.6) | collective-permute-done | bytes 262176 | tf_op jit(solution)/shard_map/ppermute | solution.py:40
  209.6 0.7 copy-done.10
  210.3 5.0 %shard_map.60 = bf16[8,512,512]{2,1,0:T(8,128)(2,1)} custom-call(s32[4]{0:T(128)} %pad_add_fusion.at, s32[256]{0:T(256)} %owners.7, s32[512]{0:T(512)} %reshape.13.octants, bf16[16,2,64,512]{3,2,1,0:T(8,128)(2,1)} %copy-done.1, bf16[2,2,64,512]{3,2,1,0:T(8,128)(2,1)} %copy-done.4, ...), custom_call_target="tpu_custom_call", output_to_operand_aliasing={{}: (14, {})} | custom-call | flops 1610612736 | bytes 7340032 | tf_op jit(solution)/shard_map/pallas_call | solution.py:350
  (56 shorter events, 0.1 us)
Async XLA Ops:
  0.0 17.4 %copy-start.18 = (s32[256,2]{0,1:T(2,128)S(1)}, s32[256,2]{0,1:T(2,128)}, u32[]{:S(2)}) copy-start(s32[256,2]{0,1:T(2,128)} %param.9) | copy-start | bytes 6148
  3.7 7.7 %collective-permute-start.7 = (bf16[2,2,64,512]{3,2,1,0:T(8,128)(2,1)}, bf16[2,2,64,512]{3,2,1,0:T(8,128)(2,1)S(1)}, u32[]{:S(2)}, u32[]{:S(2)}) collective-permute-start(bf16[2,2,64,512]{3,2,1,0:T(8,128)(2,1)} %get-tuple-element.35), channel_id=1, source_target_pairs={{0,1},{1,0},{2,3},{3,2},{4,5},{5,4},{6,7},{7,6},{8,9},{9,8},{10,11... | collective-permute-start | bytes 786440 | tf_op jit(solution)/shard_map/ppermute | solution.py:40
  5.2 9.5 %collective-permute-start.8 = (bf16[2,2,64,512]{3,2,1,0:T(8,128)(2,1)}, bf16[2,2,64,512]{3,2,1,0:T(8,128)(2,1)S(1)}, u32[]{:S(2)}, u32[]{:S(2)}) collective-permute-start(bf16[2,2,64,512]{3,2,1,0:T(8,128)(2,1)} %get-tuple-element.36), channel_id=1, source_target_pairs={{0,2},{1,3},{2,4},{3,5},{4,6},{5,7},{6,0},{7,1},{8,10},{9,11},{10,... | collective-permute-start | bytes 786440 | tf_op jit(solution)/shard_map/ppermute | solution.py:40
  6.6 13.8 %collective-permute-start.9 = (bf16[2,2,64,512]{3,2,1,0:T(8,128)(2,1)}, bf16[2,2,64,512]{3,2,1,0:T(8,128)(2,1)S(1)}, u32[]{:S(2)}, u32[]{:S(2)}) collective-permute-start(bf16[2,2,64,512]{3,2,1,0:T(8,128)(2,1)} %get-tuple-element.37), channel_id=1, source_target_pairs={{0,3},{1,2},{2,5},{3,4},{4,7},{5,6},{6,1},{7,0},{8,11},{9,10},{10,... | collective-permute-start | bytes 786440 | tf_op jit(solution)/shard_map/ppermute | solution.py:40
  8.1 18.8 %collective-permute-start.10 = (bf16[2,2,64,512]{3,2,1,0:T(8,128)(2,1)}, bf16[2,2,64,512]{3,2,1,0:T(8,128)(2,1)S(1)}, u32[]{:S(2)}, u32[]{:S(2)}) collective-permute-start(bf16[2,2,64,512]{3,2,1,0:T(8,128)(2,1)} %get-tuple-element.38), channel_id=1, source_target_pairs={{0,4},{1,5},{2,6},{3,7},{4,0},{5,1},{6,2},{7,3},{8,12},{9,13},{10,... | collective-permute-start | bytes 786440 | tf_op jit(solution)/shard_map/ppermute | solution.py:40
  9.3 23.6 %collective-permute-start.11 = (bf16[2,2,64,512]{3,2,1,0:T(8,128)(2,1)}, bf16[2,2,64,512]{3,2,1,0:T(8,128)(2,1)S(1)}, u32[]{:S(2)}, u32[]{:S(2)}) collective-permute-start(bf16[2,2,64,512]{3,2,1,0:T(8,128)(2,1)} %get-tuple-element.39), channel_id=1, source_target_pairs={{0,5},{1,4},{2,7},{3,6},{4,1},{5,0},{6,3},{7,2},{8,13},{9,12},{10,... | collective-permute-start | bytes 786440 | tf_op jit(solution)/shard_map/ppermute | solution.py:40
  11.4 22.3 %copy-start.19 = (bf16[2,2,64,512]{3,2,1,0:T(8,128)(2,1)}, bf16[2,2,64,512]{3,2,1,0:T(8,128)(2,1)S(1)}, u32[]{:S(2)}) copy-start(bf16[2,2,64,512]{3,2,1,0:T(8,128)(2,1)S(1)} %collective-permute-done.7.refs_0_) | copy-start | bytes 786436
  11.4 21.4 %collective-permute-start.12 = (bf16[2,2,64,512]{3,2,1,0:T(8,128)(2,1)}, bf16[2,2,64,512]{3,2,1,0:T(8,128)(2,1)S(1)}, u32[]{:S(2)}, u32[]{:S(2)}) collective-permute-start(bf16[2,2,64,512]{3,2,1,0:T(8,128)(2,1)} %get-tuple-element.40), channel_id=1, source_target_pairs={{0,6},{1,7},{2,0},{3,1},{4,2},{5,3},{6,4},{7,5},{8,14},{9,15},{10,... | collective-permute-start | bytes 786440 | tf_op jit(solution)/shard_map/ppermute | solution.py:40
  14.7 19.0 %copy-start.20 = (bf16[2,2,64,512]{3,2,1,0:T(8,128)(2,1)}, bf16[2,2,64,512]{3,2,1,0:T(8,128)(2,1)S(1)}, u32[]{:S(2)}) copy-start(bf16[2,2,64,512]{3,2,1,0:T(8,128)(2,1)S(1)} %collective-permute-done.8.refs_1_) | copy-start | bytes 786436
  14.7 19.0 %collective-permute-start.13 = (bf16[2,2,64,512]{3,2,1,0:T(8,128)(2,1)}, bf16[2,2,64,512]{3,2,1,0:T(8,128)(2,1)S(1)}, u32[]{:S(2)}, u32[]{:S(2)}) collective-permute-start(bf16[2,2,64,512]{3,2,1,0:T(8,128)(2,1)} %get-tuple-element.41), channel_id=1, source_target_pairs={{0,7},{1,6},{2,1},{3,0},{4,3},{5,2},{6,5},{7,4},{8,15},{9,14},{10,... | collective-permute-start | bytes 786440 | tf_op jit(solution)/shard_map/ppermute | solution.py:40
  20.4 13.3 %copy-start.21 = (bf16[2,2,64,512]{3,2,1,0:T(8,128)(2,1)}, bf16[2,2,64,512]{3,2,1,0:T(8,128)(2,1)S(1)}, u32[]{:S(2)}) copy-start(bf16[2,2,64,512]{3,2,1,0:T(8,128)(2,1)S(1)} %collective-permute-done.9.refs_2_) | copy-start | bytes 786436
  27.0 6.8 %copy-start.22 = (bf16[2,2,64,512]{3,2,1,0:T(8,128)(2,1)}, bf16[2,2,64,512]{3,2,1,0:T(8,128)(2,1)S(1)}, u32[]{:S(2)}) copy-start(bf16[2,2,64,512]{3,2,1,0:T(8,128)(2,1)S(1)} %collective-permute-done.10.refs_3_) | copy-start | bytes 786436
  32.8 0.9 copy-start.23
  32.8 1.0 copy-start.24
  33.8 0.7 copy-start.25
  41.9 2.2 %collective-permute-start.14 = (f32[4,256,128]{2,1,0:T(8,128)}, f32[4,256,128]{2,1,0:T(8,128)S(1)}, u32[]{:S(2)}, u32[]{:S(2)}) collective-permute-start(f32[4,256,128]{2,1,0:T(8,128)} %get-tuple-element.43), channel_id=1, source_target_pairs={{0,1},{1,0},{2,3},{3,2},{4,5},{5,4},{6,7},{7,6},{8,9},{9,8},{10,11... | collective-permute-start | bytes 1572872 | tf_op jit(solution)/shard_map/ppermute | solution.py:181
  69.0 14.1 %all-to-all-start.2 = ((bf16[64,16,128]{2,1,0:T(8,128)(2,1)}), bf16[64,16,128]{2,1,0:T(8,128)(2,1)S(1)}, u32[]{:S(2)}, u32[]{:S(2)}) async-start(bf16[64,16,128]{2,1,0:T(8,128)(2,1)} %broadcast_in_dim.2), calls=%async_computation.2 | async-start | bytes 524288 | tf_op jit(solution)/shard_map/all_to_all | solution.py:188
  83.1 37.2 %copy-start.2 = (bf16[64,16,128]{2,1,0:T(8,128)(2,1)}, bf16[64,16,128]{2,1,0:T(8,128)(2,1)S(1)}, u32[]{:S(2)}) copy-start(bf16[64,16,128]{2,1,0:T(8,128)(2,1)S(1)} %all-to-all-done.2) | copy-start | bytes 786436
  83.1 28.7 %all-to-all-start = ((bf16[16,2,64,512]{3,2,1,0:T(8,128)(2,1)}), bf16[16,2,64,512]{3,2,1,0:T(8,128)(2,1)S(1)}, u32[]{:S(2)}, u32[]{:S(2)}) async-start(bf16[16,2,64,512]{3,2,1,0:T(8,128)(2,1)} %shard_map.55), calls=%async_computation | async-start | bytes 4194304 | tf_op jit(solution)/shard_map/all_to_all | solution.py:380
  111.8 1.4 copy-start.1
  113.2 33.9 %all-to-all-start.3 = ((bf16[16,2,64,512]{3,2,1,0:T(8,128)(2,1)}), bf16[16,2,64,512]{3,2,1,0:T(8,128)(2,1)S(1)}, u32[]{:S(2)}, u32[]{:S(2)}) async-start(bf16[16,2,64,512]{3,2,1,0:T(8,128)(2,1)} %shard_map.57), calls=%async_computation.3 | async-start | bytes 4194304 | tf_op jit(solution)/shard_map/all_to_all | solution.py:380
  120.3 36.3 %collective-permute-start.15 = (bf16[4,256,128]{2,1,0:T(8,128)(2,1)S(1)}, bf16[4,256,128]{2,1,0:T(8,128)(2,1)S(1)}, u32[]{:S(2)}, u32[]{:S(2)}) collective-permute-start(bf16[4,256,128]{2,1,0:T(8,128)(2,1)S(1)} %bitcast.6), channel_id=1, source_target_pairs={{0,1},{1,0},{2,3},{3,2},{4,5},{5,4},{6,7},{7,6},{8,9},{9,8},{10,11... | collective-permute-start | bytes 786440 | tf_op jit(solution)/shard_map/ppermute | solution.py:190
  125.6 31.3 %collective-permute-start = (bf16[2,2,64,512]{3,2,1,0:T(8,128)(2,1)}, bf16[2,2,64,512]{3,2,1,0:T(8,128)(2,1)S(1)}, u32[]{:S(2)}, u32[]{:S(2)}) collective-permute-start(bf16[2,2,64,512]{3,2,1,0:T(8,128)(2,1)} %get-tuple-element.28), channel_id=1, source_target_pairs={{0,1},{1,0},{2,3},{3,2},{4,5},{5,4},{6,7},{7,6},{8,9},{9,8},{10,11... | collective-permute-start | bytes 786440 | tf_op jit(solution)/shard_map/ppermute | solution.py:40
  125.7 34.7 %collective-permute-start.1 = (bf16[2,2,64,512]{3,2,1,0:T(8,128)(2,1)}, bf16[2,2,64,512]{3,2,1,0:T(8,128)(2,1)S(1)}, u32[]{:S(2)}, u32[]{:S(2)}) collective-permute-start(bf16[2,2,64,512]{3,2,1,0:T(8,128)(2,1)} %get-tuple-element.29), channel_id=1, source_target_pairs={{0,2},{1,3},{2,4},{3,5},{4,6},{5,7},{6,0},{7,1},{8,10},{9,11},{10,... | collective-permute-start | bytes 786440 | tf_op jit(solution)/shard_map/ppermute | solution.py:40
  147.1 1.4 copy-start
  151.4 9.1 %collective-permute-start.16 = (bf16[2,2,64,512]{3,2,1,0:T(8,128)(2,1)}, bf16[2,2,64,512]{3,2,1,0:T(8,128)(2,1)S(1)}, u32[]{:S(2)}, u32[]{:S(2)}) collective-permute-start(bf16[2,2,64,512]{3,2,1,0:T(8,128)(2,1)} %get-tuple-element.44), channel_id=1, source_target_pairs={{0,1},{1,0},{2,3},{3,2},{4,5},{5,4},{6,7},{7,6},{8,9},{9,8},{10,11... | collective-permute-start | bytes 786440 | tf_op jit(solution)/shard_map/ppermute | solution.py:40
  156.3 9.2 %collective-permute-start.17 = (bf16[2,2,64,512]{3,2,1,0:T(8,128)(2,1)}, bf16[2,2,64,512]{3,2,1,0:T(8,128)(2,1)S(1)}, u32[]{:S(2)}, u32[]{:S(2)}) collective-permute-start(bf16[2,2,64,512]{3,2,1,0:T(8,128)(2,1)} %get-tuple-element.45), channel_id=1, source_target_pairs={{0,2},{1,3},{2,4},{3,5},{4,6},{5,7},{6,0},{7,1},{8,10},{9,11},{10,... | collective-permute-start | bytes 786440 | tf_op jit(solution)/shard_map/ppermute | solution.py:40
  156.6 33.6 %copy-start.3 = (bf16[4,256,128]{2,1,0:T(8,128)(2,1)}, bf16[4,256,128]{2,1,0:T(8,128)(2,1)S(1)}, u32[]{:S(2)}) copy-start(bf16[4,256,128]{2,1,0:T(8,128)(2,1)S(1)} %collective-permute-done.15.refs_9_) | copy-start | bytes 786436
  156.6 26.0 %collective-permute-start.18 = (bf16[2,2,64,512]{3,2,1,0:T(8,128)(2,1)}, bf16[2,2,64,512]{3,2,1,0:T(8,128)(2,1)S(1)}, u32[]{:S(2)}, u32[]{:S(2)}) collective-permute-start(bf16[2,2,64,512]{3,2,1,0:T(8,128)(2,1)} %get-tuple-element.46), channel_id=1, source_target_pairs={{0,3},{1,2},{2,5},{3,4},{4,7},{5,6},{6,1},{7,0},{8,11},{9,10},{10,... | collective-permute-start | bytes 786440 | tf_op jit(solution)/shard_map/ppermute | solution.py:40
  156.9 39.9 %copy-start.4 = (bf16[2,2,64,512]{3,2,1,0:T(8,128)(2,1)}, bf16[2,2,64,512]{3,2,1,0:T(8,128)(2,1)S(1)}, u32[]{:S(2)}) copy-start(bf16[2,2,64,512]{3,2,1,0:T(8,128)(2,1)S(1)} %collective-permute-done.refs_1_) | copy-start | bytes 786436
  156.9 25.7 %collective-permute-start.19 = (bf16[2,2,64,512]{3,2,1,0:T(8,128)(2,1)}, bf16[2,2,64,512]{3,2,1,0:T(8,128)(2,1)S(1)}, u32[]{:S(2)}, u32[]{:S(2)}) collective-permute-start(bf16[2,2,64,512]{3,2,1,0:T(8,128)(2,1)} %get-tuple-element.47), channel_id=1, source_target_pairs={{0,4},{1,5},{2,6},{3,7},{4,0},{5,1},{6,2},{7,3},{8,12},{9,13},{10,... | collective-permute-start | bytes 786440 | tf_op jit(solution)/shard_map/ppermute | solution.py:40
  160.4 36.5 %copy-start.5 = (bf16[2,2,64,512]{3,2,1,0:T(8,128)(2,1)}, bf16[2,2,64,512]{3,2,1,0:T(8,128)(2,1)S(1)}, u32[]{:S(2)}) copy-start(bf16[2,2,64,512]{3,2,1,0:T(8,128)(2,1)S(1)} %collective-permute-done.1.refs_2_) | copy-start | bytes 786436
  160.4 23.4 %collective-permute-start.20 = (bf16[2,2,64,512]{3,2,1,0:T(8,128)(2,1)}, bf16[2,2,64,512]{3,2,1,0:T(8,128)(2,1)S(1)}, u32[]{:S(2)}, u32[]{:S(2)}) collective-permute-start(bf16[2,2,64,512]{3,2,1,0:T(8,128)(2,1)} %get-tuple-element.48), channel_id=1, source_target_pairs={{0,5},{1,4},{2,7},{3,6},{4,1},{5,0},{6,3},{7,2},{8,13},{9,12},{10,... | collective-permute-start | bytes 786440 | tf_op jit(solution)/shard_map/ppermute | solution.py:40
  160.5 29.7 %copy-start.11 = (bf16[2,2,64,512]{3,2,1,0:T(8,128)(2,1)}, bf16[2,2,64,512]{3,2,1,0:T(8,128)(2,1)S(1)}, u32[]{:S(2)}) copy-start(bf16[2,2,64,512]{3,2,1,0:T(8,128)(2,1)S(1)} %collective-permute-done.16.refs_1_) | copy-start | bytes 786436
  160.5 25.4 %collective-permute-start.21 = (bf16[2,2,64,512]{3,2,1,0:T(8,128)(2,1)}, bf16[2,2,64,512]{3,2,1,0:T(8,128)(2,1)S(1)}, u32[]{:S(2)}, u32[]{:S(2)}) collective-permute-start(bf16[2,2,64,512]{3,2,1,0:T(8,128)(2,1)} %get-tuple-element.49), channel_id=1, source_target_pairs={{0,6},{1,7},{2,0},{3,1},{4,2},{5,3},{6,4},{7,5},{8,14},{9,15},{10,... | collective-permute-start | bytes 786440 | tf_op jit(solution)/shard_map/ppermute | solution.py:40
  165.5 24.7 %copy-start.12 = (bf16[2,2,64,512]{3,2,1,0:T(8,128)(2,1)}, bf16[2,2,64,512]{3,2,1,0:T(8,128)(2,1)S(1)}, u32[]{:S(2)}) copy-start(bf16[2,2,64,512]{3,2,1,0:T(8,128)(2,1)S(1)} %collective-permute-done.17.refs_2_) | copy-start | bytes 786436
  165.5 24.0 %collective-permute-start.22 = (bf16[2,2,64,512]{3,2,1,0:T(8,128)(2,1)}, bf16[2,2,64,512]{3,2,1,0:T(8,128)(2,1)S(1)}, u32[]{:S(2)}, u32[]{:S(2)}) collective-permute-start(bf16[2,2,64,512]{3,2,1,0:T(8,128)(2,1)} %get-tuple-element.50), channel_id=1, source_target_pairs={{0,7},{1,6},{2,1},{3,0},{4,3},{5,2},{6,5},{7,4},{8,15},{9,14},{10,... | collective-permute-start | bytes 786440 | tf_op jit(solution)/shard_map/ppermute | solution.py:40
  182.6 7.6 %copy-start.13 = (bf16[2,2,64,512]{3,2,1,0:T(8,128)(2,1)}, bf16[2,2,64,512]{3,2,1,0:T(8,128)(2,1)S(1)}, u32[]{:S(2)}) copy-start(bf16[2,2,64,512]{3,2,1,0:T(8,128)(2,1)S(1)} %collective-permute-done.18.refs_3_) | copy-start | bytes 786436
  182.6 20.7 %collective-permute-start.2 = (bf16[2,2,64,512]{3,2,1,0:T(8,128)(2,1)}, bf16[2,2,64,512]{3,2,1,0:T(8,128)(2,1)S(1)}, u32[]{:S(2)}, u32[]{:S(2)}) collective-permute-start(bf16[2,2,64,512]{3,2,1,0:T(8,128)(2,1)} %get-tuple-element.30), channel_id=1, source_target_pairs={{0,3},{1,2},{2,5},{3,4},{4,7},{5,6},{6,1},{7,0},{8,11},{9,10},{10,... | collective-permute-start | bytes 786440 | tf_op jit(solution)/shard_map/ppermute | solution.py:40
  182.6 7.6 %copy-start.14 = (bf16[2,2,64,512]{3,2,1,0:T(8,128)(2,1)}, bf16[2,2,64,512]{3,2,1,0:T(8,128)(2,1)S(1)}, u32[]{:S(2)}) copy-start(bf16[2,2,64,512]{3,2,1,0:T(8,128)(2,1)S(1)} %collective-permute-done.19.refs_4_) | copy-start | bytes 786436
  182.6 20.7 %collective-permute-start.3 = (bf16[2,2,64,512]{3,2,1,0:T(8,128)(2,1)}, bf16[2,2,64,512]{3,2,1,0:T(8,128)(2,1)S(1)}, u32[]{:S(2)}, u32[]{:S(2)}) collective-permute-start(bf16[2,2,64,512]{3,2,1,0:T(8,128)(2,1)} %get-tuple-element.31), channel_id=1, source_target_pairs={{0,4},{1,5},{2,6},{3,7},{4,0},{5,1},{6,2},{7,3},{8,12},{9,13},{10,... | collective-permute-start | bytes 786440 | tf_op jit(solution)/shard_map/ppermute | solution.py:40
  183.8 6.5 %copy-start.15 = (bf16[2,2,64,512]{3,2,1,0:T(8,128)(2,1)}, bf16[2,2,64,512]{3,2,1,0:T(8,128)(2,1)S(1)}, u32[]{:S(2)}) copy-start(bf16[2,2,64,512]{3,2,1,0:T(8,128)(2,1)S(1)} %collective-permute-done.20.refs_5_) | copy-start | bytes 786436
  183.8 19.6 %collective-permute-start.4 = (bf16[2,2,64,512]{3,2,1,0:T(8,128)(2,1)}, bf16[2,2,64,512]{3,2,1,0:T(8,128)(2,1)S(1)}, u32[]{:S(2)}, u32[]{:S(2)}) collective-permute-start(bf16[2,2,64,512]{3,2,1,0:T(8,128)(2,1)} %get-tuple-element.32), channel_id=1, source_target_pairs={{0,5},{1,4},{2,7},{3,6},{4,1},{5,0},{6,3},{7,2},{8,13},{9,12},{10,... | collective-permute-start | bytes 786440 | tf_op jit(solution)/shard_map/ppermute | solution.py:40
  186.0 0.7 copy-start.16
  186.7 16.7 %collective-permute-start.5 = (bf16[2,2,64,512]{3,2,1,0:T(8,128)(2,1)}, bf16[2,2,64,512]{3,2,1,0:T(8,128)(2,1)S(1)}, u32[]{:S(2)}, u32[]{:S(2)}) collective-permute-start(bf16[2,2,64,512]{3,2,1,0:T(8,128)(2,1)} %get-tuple-element.33), channel_id=1, source_target_pairs={{0,6},{1,7},{2,0},{3,1},{4,2},{5,3},{6,4},{7,5},{8,14},{9,15},{10,... | collective-permute-start | bytes 786440 | tf_op jit(solution)/shard_map/ppermute | solution.py:40
  189.5 0.7 copy-start.17
  190.2 19.3 %collective-permute-start.6 = (bf16[2,2,64,512]{3,2,1,0:T(8,128)(2,1)}, bf16[2,2,64,512]{3,2,1,0:T(8,128)(2,1)S(1)}, u32[]{:S(2)}, u32[]{:S(2)}) collective-permute-start(bf16[2,2,64,512]{3,2,1,0:T(8,128)(2,1)} %get-tuple-element.34), channel_id=1, source_target_pairs={{0,7},{1,6},{2,1},{3,0},{4,3},{5,2},{6,5},{7,4},{8,15},{9,14},{10,... | collective-permute-start | bytes 786440 | tf_op jit(solution)/shard_map/ppermute | solution.py:40
  203.3 6.2 %copy-start.6 = (bf16[2,2,64,512]{3,2,1,0:T(8,128)(2,1)}, bf16[2,2,64,512]{3,2,1,0:T(8,128)(2,1)S(1)}, u32[]{:S(2)}) copy-start(bf16[2,2,64,512]{3,2,1,0:T(8,128)(2,1)S(1)} %collective-permute-done.2.refs_3_) | copy-start | bytes 786436
  203.3 6.2 %copy-start.7 = (bf16[2,2,64,512]{3,2,1,0:T(8,128)(2,1)}, bf16[2,2,64,512]{3,2,1,0:T(8,128)(2,1)S(1)}, u32[]{:S(2)}) copy-start(bf16[2,2,64,512]{3,2,1,0:T(8,128)(2,1)S(1)} %collective-permute-done.3.refs_4_) | copy-start | bytes 786436
  203.3 6.2 %copy-start.8 = (bf16[2,2,64,512]{3,2,1,0:T(8,128)(2,1)}, bf16[2,2,64,512]{3,2,1,0:T(8,128)(2,1)S(1)}, u32[]{:S(2)}) copy-start(bf16[2,2,64,512]{3,2,1,0:T(8,128)(2,1)S(1)} %collective-permute-done.4.refs_5_) | copy-start | bytes 786436
  203.4 6.2 %copy-start.9 = (bf16[2,2,64,512]{3,2,1,0:T(8,128)(2,1)}, bf16[2,2,64,512]{3,2,1,0:T(8,128)(2,1)S(1)}, u32[]{:S(2)}) copy-start(bf16[2,2,64,512]{3,2,1,0:T(8,128)(2,1)S(1)} %collective-permute-done.5.refs_6_) | copy-start | bytes 786436
  209.6 0.7 copy-start.10
where the time goes:
time: 216 us; the launch traced here: 215 us
  waiting for transfers between devices  99.5 us (46%)
  starting transfers between devices  48.5 us (22%)
  Pallas kernels  35.2 us (16%)
  blocking collectives  22.9 us (11%)
  local copies, waits for them, and re-layouts  7.15 us (3%)
    ppermute x21, waiting for transfers between devices, over_band(): lax.ppermute(piece, BAND, band_pairs(q, l))  49.2 us
    all_to_all x2, waiting for transfers between devices, refined(): slots[rank] = lax.all_to_all(slots[rank], DOM, 0, 0, tiled=True)  42.4 us
    ppermute x21, starting transfers between devices, over_band(): lax.ppermute(piece, BAND, band_pairs(q, l))  30.5 us
    all_to_all x1, blocking collectives, summed_over_all(): tiles = lax.all_to_all(blocks, CHIPS, 0, 0, tiled=True)  22.9 us
    pallas_call x2, Pallas kernels, predict(): pl.pallas_call(functools.partial(predict_kernel, rank, old), out_shape=si...  11.6 us
    all_to_all x2, starting transfers between devices, refined(): slots[rank] = lax.all_to_all(slots[rank], DOM, 0, 0, tiled=True)  10.8 us
    pallas_call x1, Pallas kernels, product_of_cells(): pl.pallas_call(product_kernel, out_shape=[sized(lanes, F32)] * 2, in_spec...  7.42 us
    pallas_call x2, Pallas kernels, slots_for_owners(): pl.pallas_call(functools.partial(slots_kernel, rank), out_shape=sized((do...  7.09 us
  transfers between devices with their start and end apart: 26, of which 14 were waited for; matrix products, arithmetic and copies ran while one was open for 0% of the time, Pallas kernels for 9%

commit v1 on v0

v1 whole, which is shorter than its diff:
```python
import functools
import math

import jax
import jax.numpy as jnp
from jax import lax
from jax.experimental import pallas as pl
from jax.experimental.pallas import tpu as pltpu
from jax.sharding import Mesh
from jax.sharding import PartitionSpec as P


Z, X, Y, C = "dom_0", "dom_1", "band_0", "band_1"
DOM = (Z, X)
BAND = (Y, C)
DOM_BAND = (Z, X, Y, C)
CHIPS = (Z, X, Y)

BF16 = jnp.bfloat16
F32 = jnp.float32
RING = 4
CORES = 2
OFFSETS = tuple((q, l) for q in range(RING) for l in range(CORES))


WHOLE_VMEM = pltpu.CompilerParams(vmem_limit_bytes=67_043_328)

SMEM = pl.BlockSpec(memory_space=pltpu.SMEM)
HBM = pl.BlockSpec(memory_space=pltpu.HBM)


def band_pairs(q, l):
    return [
        (y * CORES + c, ((y + q) % RING) * CORES + (c + l) % CORES)
        for y in range(RING)
        for c in range(CORES)
    ]


def over_band(pieces):
    return [
        lax.ppermute(piece, BAND, band_pairs(q, l)) for (q, l), piece in zip(OFFSETS[1:], pieces)
    ]


def sized(shape, dtype=BF16):
    return jax.ShapeDtypeStruct(shape, dtype)


def moved(read, written, flops=0):
    return pl.CostEstimate(flops=flops, bytes_accessed=read + written, transcendentals=0)


def cells_kernel(at, now, prev, *refs):
    outs, (buf, in_sem, out_sem) = refs[:7], refs[7:]
    y, c = at[2], at[3]
    loads, stores = [], []
    for n, (q, l) in enumerate(OFFSETS[1:]):
        first = (((y + q) & 3) * CORES + ((c + l) & 1)) * 2
        loads.append(
            [
                pltpu.make_async_copy(src.at[pl.ds(first, 2)], buf.at[n, a], in_sem.at[n, a])
                for a, src in enumerate((now, prev))
            ]
        )
        stores.append(pltpu.make_async_copy(buf.at[n], outs[n], out_sem.at[n]))
    for pair in loads:
        for copy in pair:
            copy.start()
    for pair, store in zip(loads, stores):
        for copy in pair:
            copy.wait()
        store.start()
    for store in stores:
        store.wait()


def cells_for_band(at, now, prev):
    _, rows, nodes = now.shape
    piece = (2, 2, rows, nodes)
    size = 4 * rows * nodes * 2
    return pl.pallas_call(
        cells_kernel,
        out_shape=[sized(piece)] * 7,
        in_specs=[SMEM, HBM, HBM],
        out_specs=[HBM] * 7,
        scratch_shapes=[
            pltpu.VMEM((7, *piece), BF16),
            pltpu.SemaphoreType.DMA((7, 2)),
            pltpu.SemaphoreType.DMA((7,)),
        ],
        compiler_params=WHOLE_VMEM,
        cost_estimate=moved(7 * size, 7 * size),
        name="cells_for_band",
    )(at, now, prev)


def product_kernel(at, octants, now, prev, *refs):
    pieces, interp, mine, other = refs[:7], refs[7], refs[8:12], refs[12]
    parents, matrices, kids, out, in_sem, mat_sem, out_sem = refs[13:]
    z, x, y, c = at[0], at[1], at[2], at[3]
    rows = now.shape[1]
    nodes = now.shape[2]
    states = parents.shape[2]
    half = states // 2
    first = (y * CORES + c) * 2
    cell0 = (z * RING + x) * now.shape[0] + first
    loads = []
    for e in range(2):
        copies = []
        for a, src in enumerate((now, prev)):
            own = pl.ds(pl.multiple_of((y * CORES + c) * rows, rows), rows)
            copies.append(
                pltpu.make_async_copy(
                    src.at[first + e], parents.at[a, e, own], in_sem.at[e, 7 + a]
                )
            )
        for n, (q, l) in enumerate(OFFSETS[1:]):
            b = ((y - q) & 3) * CORES + ((c - l) & 1)
            to = pl.ds(pl.multiple_of(b * rows, rows), rows)
            copies.append(
                pltpu.make_async_copy(
                    pieces[n].at[:, e], parents.at[:, e, to], in_sem.at[e, n]
                )
            )
        for j in range(2):
            o = octants[(cell0 + e) * 2 + j]
            copies.append(
                pltpu.make_async_copy(interp.at[o], matrices.at[e, j], mat_sem.at[e, j])
            )
        for copy in copies:
            copy.start()
        loads.append(copies)
    for e in range(2):
        for copy in loads[e]:
            copy.wait()
        for a in range(2):
            for j in range(2):
                kids[a, :, pl.ds((e * 2 + j) * nodes, nodes)] = lax.dot_general(
                    parents[a, e],
                    matrices[e, j],
                    (((1,), (1,)), ((), ())),
                    preferred_element_type=F32,
                ).astype(BF16)
    stores = []
    for n, side in enumerate((1 - c, c)):
        u = pl.ds(pl.multiple_of(side * half, half), half)
        part = lax.dot_general(
            kids[1, u, :], kids[0], (((1,), (1,)), ((), ())), preferred_element_type=F32
        )
        for t in range(RING):
            out[n, t] = part[:, t * 128 : (t + 1) * 128]
        for k in range(RING):
            dst = mine[k] if n else other.at[k]
            stores.append(pltpu.make_async_copy(out.at[n, (y + k) & 3], dst, out_sem.at[n, k]))
            stores[-1].start()
    for store in stores:
        store.wait()


def product_of_cells(at, octants, now, prev, pieces, interp):
    _, rows, nodes = now.shape
    states = rows * RING * CORES
    block = (states // 2, 128)
    return pl.pallas_call(
        product_kernel,
        out_shape=[sized(block, F32)] * RING + [sized((RING, *block), F32)],
        in_specs=[SMEM, SMEM] + [HBM] * 10,
        out_specs=[HBM] * 5,
        scratch_shapes=[
            pltpu.VMEM((2, 2, states, nodes), BF16),
            pltpu.VMEM((2, 2, nodes, nodes), BF16),
            pltpu.VMEM((2, states, 4 * nodes), BF16),
            pltpu.VMEM((2, RING, *block), F32),
            pltpu.SemaphoreType.DMA((2, 9)),
            pltpu.SemaphoreType.DMA((2, 2)),
            pltpu.SemaphoreType.DMA((2, RING)),
        ],
        compiler_params=WHOLE_VMEM,
        cost_estimate=moved(4 << 20, 1 << 20, 24 * states * nodes * nodes),
        name="product_of_cells",
    )(at, octants, now, prev, *pieces, interp)


def summed_over_all(mine, other, scaling):
    swap = [(0, 1), (1, 0)]
    other = lax.ppermute(other, C, swap)
    blocks = [block + other[k] for k, block in enumerate(mine)]
    blocks[1:] = [
        lax.ppermute(blocks[k], Y, [(i, (i + k) % RING) for i in range(RING)])
        for k in range(1, RING)
    ]
    block = (blocks[0] + blocks[1]) + (blocks[2] + blocks[3])
    doms = lax.axis_size(DOM)
    tiles = lax.all_to_all(block.reshape(doms, -1, 128), DOM, 0, 0, tiled=True)
    own = (jnp.sum(tiles, axis=0) * scaling).astype(BF16)
    own = jnp.broadcast_to(own[None], (doms * RING, *own.shape))
    own = lax.all_to_all(own, CHIPS, 0, 0, tiled=True)
    own = own.reshape(doms, RING, -1, 128)
    return own, lax.ppermute(own, C, swap)


def slots_kernel(rank, at, owners, now, prev, out, cells, slot, seen, in_sem, out_sem):
    z, x = at[0], at[1]
    old = now.shape[0]
    first = (z * RING + x) * old
    loads = [
        pltpu.make_async_copy(src, cells.at[a], in_sem.at[a]) for a, src in enumerate((now, prev))
    ]
    for load in loads:
        load.start()
    for d in range(RING * RING):
        seen[d] = 0
        slot[d] = 0

    def place(i, carry):
        owner = owners[first + i]
        slot[owner] = jnp.where(seen[owner] == rank, i, slot[owner])
        seen[owner] = seen[owner] + 1
        return carry

    lax.fori_loop(0, old, place, 0)
    stores = []
    for a in range(2):
        loads[a].wait()
        for d in range(RING * RING):
            stores.append(
                pltpu.make_async_copy(cells.at[a, slot[d]], out.at[d, a], out_sem.at[a, d])
            )
            stores[-1].start()
    for store in stores:
        store.wait()


def slots_for_owners(rank, at, owners, now, prev):
    old, rows, nodes = now.shape
    doms = RING * RING
    size = 2 * old * rows * nodes * 2
    return pl.pallas_call(
        functools.partial(slots_kernel, rank),
        out_shape=sized((doms, 2, rows, nodes)),
        in_specs=[SMEM, SMEM, HBM, HBM],
        out_specs=HBM,
        scratch_shapes=[
            pltpu.VMEM((2, old, rows, nodes), BF16),
            pltpu.SMEM((doms,), jnp.int32),
            pltpu.SMEM((doms,), jnp.int32),
            pltpu.SemaphoreType.DMA((2,)),
            pltpu.SemaphoreType.DMA((2, doms)),
        ],
        compiler_params=WHOLE_VMEM,
        cost_estimate=moved(size, size),
    )(at, owners, now, prev)


def route_kernel(at, slots, *refs):
    outs, (buf, in_sem, out_sem) = refs[:7], refs[7:]
    y, c = at[2], at[3]
    loads, stores = [], []
    for n, (q, l) in enumerate(OFFSETS[1:]):
        first = (((y + q) & 3) * CORES + ((c + l) & 1)) * 2
        loads.append(pltpu.make_async_copy(slots.at[pl.ds(first, 2)], buf.at[n], in_sem.at[n]))
        stores.append(pltpu.make_async_copy(buf.at[n], outs[n], out_sem.at[n]))
    for load in loads:
        load.start()
    for load, store in zip(loads, stores):
        load.wait()
        store.start()
    for store in stores:
        store.wait()


def routed(at, slots):
    piece = (2, *slots.shape[1:])
    size = 7 * math.prod(piece) * 2
    return pl.pallas_call(
        route_kernel,
        out_shape=[sized(piece)] * 7,
        in_specs=[SMEM, HBM],
        out_specs=[HBM] * 7,
        scratch_shapes=[
            pltpu.VMEM((7, *piece), BF16),
            pltpu.SemaphoreType.DMA((7,)),
            pltpu.SemaphoreType.DMA((7,)),
        ],
        compiler_params=WHOLE_VMEM,
        cost_estimate=moved(size, size),
    )(at, slots)


def predict_kernel(old, at, owners, octants, *refs):
    slots, mine, other, interp, predicted = (refs[0], refs[8]), *refs[16:20]
    pieces = (refs[1:8], refs[9:16])
    parents, matrices, mix, out, in_sem, mat_sem, mix_sem, out_sem = refs[20:]
    z, x, y, c = at[0], at[1], at[2], at[3]
    rows = slots[0].shape[2]
    states = parents.shape[2]
    blocks = mine.shape[0]
    owner = z * RING + x
    mixing = []
    for n, (side, src) in enumerate(((c, mine), (1 - c, other))):
        u = pl.ds(side * blocks, blocks)
        for t in range(RING):
            mixing.append(
                pltpu.make_async_copy(
                    src.at[:, t], mix.at[u, :, pl.ds(t * 128, 128)], mix_sem.at[n, t]
                )
            )
    for copy in mixing:
        copy.start()
    loads, filled = [], []
    for k in range(4):
        rank, e = k // 2, k % 2
        first = (RING * y + 2 * c + e) * old

        def look(i, carry, first=first, rank=rank):
            count, cell = carry
            match = owners[first + i] == owner
            cell = jnp.where(match & (count == rank), i, cell)
            return count + match.astype(jnp.int32), cell

        count, cell = lax.fori_loop(0, old, look, (jnp.int32(0), jnp.int32(0)))
        filled.append(count > rank)
        copies = []
        for n, (q, l) in enumerate(OFFSETS):
            b = ((y - q) & 3) * CORES + ((c - l) & 1)
            to = pl.ds(pl.multiple_of(b * rows, rows), rows)
            src = pieces[rank][n - 1].at[e] if n else slots[rank].at[b * 2 + e]
            copies.append(pltpu.make_async_copy(src, parents.at[k, :, to], in_sem.at[k, n]))
        for j in range(2):
            o = octants[(first + cell) * 2 + j]
            copies.append(
                pltpu.make_async_copy(interp.at[o], matrices.at[k, j], mat_sem.at[k, j])
            )
        for copy in copies:
            copy.start()
        loads.append(copies)
    for copy in mixing:
        copy.wait()
    stores = []
    for k in range(4):
        rank, e = k // 2, k % 2
        for copy in loads[k]:
            copy.wait()

        @pl.when(filled[k])
        def _(k=k):
            mixed = jnp.dot(
                mix[...].reshape(states, states), parents[k, 0], preferred_element_type=F32
            )
            value = (parents[k, 1].astype(F32) + mixed).astype(BF16)
            for j in range(2):
                out[k, j] = lax.dot_general(
                    value, matrices[k, j], (((1,), (1,)), ((), ())), preferred_element_type=F32
                ).astype(BF16)

        @pl.when(jnp.logical_not(filled[k]))
        def _(k=k):
            out[k] = jnp.zeros(out.shape[1:], BF16)

        stores.append(
            pltpu.make_async_copy(
                out.at[k], predicted.at[pl.ds(e * 4 + rank * 2, 2)], out_sem.at[k]
            )
        )
        stores[-1].start()
    for store in stores:
        store.wait()


def predict(old, at, owners, octants, slots, pieces, mine, other, interp):
    _, _, rows, nodes = slots[0].shape
    states = rows * RING * CORES
    return pl.pallas_call(
        functools.partial(predict_kernel, old),
        out_shape=sized((8, states, nodes)),
        in_specs=[SMEM] * 3 + [HBM] * 19,
        out_specs=HBM,
        scratch_shapes=[
            pltpu.VMEM((4, 2, states, nodes), BF16),
            pltpu.VMEM((4, 2, nodes, nodes), BF16),
            pltpu.VMEM((states // 16, 16, states), BF16),
            pltpu.VMEM((4, 2, states, nodes), BF16),
            pltpu.SemaphoreType.DMA((4, 8)),
            pltpu.SemaphoreType.DMA((4, 2)),
            pltpu.SemaphoreType.DMA((2, RING)),
            pltpu.SemaphoreType.DMA((4,)),
        ],
        compiler_params=WHOLE_VMEM,
        cost_estimate=moved(9 << 20, 4 << 20, 24 * states * nodes * nodes),
        name="predict",
    )(at, owners, octants, slots[0], *pieces[0], slots[1], *pieces[1], mine, other, interp)


def refined(orbitals_now, orbitals_prev, interp, owner_map, child_oct):
    old, rows, nodes = orbitals_now.shape
    states = rows * lax.axis_size(BAND)
    at = jnp.stack([lax.axis_index(a) for a in DOM_BAND]).astype(jnp.int32)
    octants = child_oct.reshape(-1)
    scaling = 1.0 / math.sqrt(2.0 * states * owner_map.shape[0] * nodes)

    slots, pieces = [], []
    for rank in range(2):
        slots.append(slots_for_owners(rank, at, owner_map, orbitals_now, orbitals_prev))
        slots[rank] = lax.all_to_all(slots[rank], DOM, 0, 0, tiled=True)
        pieces.append(routed(at, slots[rank]))
        pieces[rank] = over_band(pieces[rank])

    cells = cells_for_band(at, orbitals_now, orbitals_prev)
    cells = over_band(cells)
    *mine, other = product_of_cells(at, octants, orbitals_now, orbitals_prev, cells, interp)
    mine, other = summed_over_all(mine, other, scaling)

    return predict(old, at, owner_map, octants, slots, pieces, mine, other, interp)


def solution(mesh):
    split = Mesh(mesh.devices.reshape(4, 4, 4, 2), DOM_BAND)
    placed = (P(DOM, BAND, None), P(DOM, BAND, None), P(), P(), P())
    return jax.shard_map(
        refined, mesh=split, in_specs=placed, out_specs=P(DOM_BAND, None, None), check_vma=False
    )
```

time: 216 us -> 208 us (0.963)
  starting transfers between devices: 48.5 us -> 62 us
  blocking collectives: 22.9 us -> 14.3 us
  waiting for transfers between devices: 99.5 us -> 94.6 us
  Pallas kernels: 35.2 us -> 30.6 us
  local copies, waits for them, and re-layouts: 7.15 us -> 2.97 us
    all_to_all x1, blocking collectives: 22.9 us -> 14.3 us  [summed_over_all(): tiles = lax.all_to_all(block.reshape(doms, -1, 128), DOM, 0, 0, tiled=True)]
    ppermute x1 -> x4, waiting for transfers between devices: 2.04 us -> 10 us  [the longest x3 8 us: summed_over_all(): lax.ppermute(blocks[k], Y, [(i, (i + k) % RING) for i in range(RING)])]
    ppermute x21, waiting for transfers between devices: 49.2 us -> 42.2 us  [over_band(): lax.ppermute(piece, BAND, band_pairs(q, l))]
    ppermute x21, starting transfers between devices: 30.5 us -> 37.1 us  [over_band(): lax.ppermute(piece, BAND, band_pairs(q, l))]
    all_to_all x2, waiting for transfers between devices: 42.4 us -> 36.6 us  [refined(): slots[rank] = lax.all_to_all(slots[rank], DOM, 0, 0, tiled=True)]
    pallas_call x3 -> x2, Pallas kernels: 19 us -> 14.4 us  [the longest x1 7.45 us: product_of_cells(): pl.pallas_call(product_kernel, out_shape=[sized(block, F32)] * RING + [si...]
    unnamed x53 -> x5, local copies, waits for them, and re-layouts: 5.73 us -> 1.51 us
    ppermute x1 -> x4, starting transfers between devices: 0.16 us -> 4.26 us  [the longest x3 4.1 us: summed_over_all(): lax.ppermute(blocks[k], Y, [(i, (i + k) % RING) for i in range(RING)])]
  transfers between devices with their start and end apart: 26 -> 29, of which waited for: 14 -> 18; matrix products, arithmetic and copies ran while one was open for 0% -> 1% of each run, Pallas kernels for 9% -> 6%
where the time goes in v1:
time: 208 us; the launch traced here: 207 us
  waiting for transfers between devices  94.6 us (45%)
  starting transfers between devices  62 us (30%)
  Pallas kernels  30.6 us (15%)
  blocking collectives  14.3 us (7%)
  local copies, waits for them, and re-layouts  2.97 us (1%)
  other arithmetic  2.7 us (1%)
    ppermute x21, waiting for transfers between devices, over_band(): lax.ppermute(piece, BAND, band_pairs(q, l))  42.2 us
    ppermute x21, starting transfers between devices, over_band(): lax.ppermute(piece, BAND, band_pairs(q, l))  37.1 us
    all_to_all x2, waiting for transfers between devices, refined(): slots[rank] = lax.all_to_all(slots[rank], DOM, 0, 0, tiled=True)  36.6 us
    all_to_all x1, blocking collectives, summed_over_all(): tiles = lax.all_to_all(block.reshape(doms, -1, 128), DOM, 0, 0, tiled=True)  14.3 us
    all_to_all x2, starting transfers between devices, refined(): slots[rank] = lax.all_to_all(slots[rank], DOM, 0, 0, tiled=True)  11.8 us
    ppermute x3, waiting for transfers between devices, summed_over_all(): lax.ppermute(blocks[k], Y, [(i, (i + k) % RING) for i in range(RING)])  8 us
    pallas_call x1, Pallas kernels, product_of_cells(): pl.pallas_call(product_kernel, out_shape=[sized(block, F32)] * RING + [si...  7.45 us
    pallas_call x2, Pallas kernels, slots_for_owners(): pl.pallas_call(functools.partial(slots_kernel, rank), out_shape=sized((do...  7.08 us
  transfers between devices with their start and end apart: 29, of which 18 were waited for; matrix products, arithmetic and copies ran while one was open for 1% of the time, Pallas kernels for 6%

profile of v1, /device:TPU:1, one launch (start us, length us, event | category | flops | bytes accessed | tf_op | source)
XLA Modules:
  0.0 207.5 jit_solution(14766592838179564995)
XLA Ops:
  0.0 0.7 pad_add_fusion.at
  0.7 3.1 %cells_for_band.1 = (bf16[2,2,64,512]{3,2,1,0:T(8,128)(2,1)}, bf16[2,2,64,512]{3,2,1,0:T(8,128)(2,1)}, bf16[2,2,64,512]{3,2,1,0:T(8,128)(2,1)}, bf16[2,2,64,512]...) custom-call(s32[4]{0:T(128)} %pad_add_fusion.at, ...), custom_call_target="tpu_custom_call" | custom-call | bytes 3670016 | tf_op jit(solution)/shard_map/cells_for_band/pallas_call | solution.py:82
  3.7 1.5 collective-permute-start.14
  5.2 1.4 collective-permute-start.15
  6.6 1.5 collective-permute-start.16
  8.2 1.2 collective-permute-start.17
  9.3 2.1 %collective-permute-start.18 = (bf16[2,2,64,512]{3,2,1,0:T(8,128)(2,1)}, bf16[2,2,64,512]{3,2,1,0:T(8,128)(2,1)}, u32[]{:S(2)}, u32[]{:S(2)}) collective-permute-start(bf16[2,2,64,512]{3,2,1,0:T(8,128)(2,1)} %get-tuple-element.49), channel_id=1, source_target_pairs={{0,5},{1,4},{2,7},{3,6},{4,1},{5,0},{6,3},{7,2},{8,13},{9,12},{10,... | collective-permute-start | bytes 786440 | tf_op jit(solution)/shard_map/ppermute | solution.py:42
  11.4 0.0 collective-permute-done.14.refs_0_
  11.4 1.4 collective-permute-start.19
  12.8 1.9 collective-permute-done.15.refs_1_
  14.8 0.7 copy-done.1
  15.5 2.7 %collective-permute-start.20 = (bf16[2,2,64,512]{3,2,1,0:T(8,128)(2,1)}, bf16[2,2,64,512]{3,2,1,0:T(8,128)(2,1)}, u32[]{:S(2)}, u32[]{:S(2)}) collective-permute-start(bf16[2,2,64,512]{3,2,1,0:T(8,128)(2,1)} %get-tuple-element.51), channel_id=1, source_target_pairs={{0,7},{1,6},{2,1},{3,0},{4,3},{5,2},{6,5},{7,4},{8,15},{9,14},{10,... | collective-permute-start | bytes 786440 | tf_op jit(solution)/shard_map/ppermute | solution.py:42
  18.1 0.8 copy.6
  18.9 0.7 reshape.13.octants
  19.7 0.9 collective-permute-done.16.refs_2_
  20.6 6.5 %collective-permute-done.17.refs_3_ = bf16[2,2,64,512]{3,2,1,0:T(8,128)(2,1)} collective-permute-done((bf16[2,2,64,512]{3,2,1,0:T(8,128)(2,1)}, bf16[2,2,64,512]{3,2,1,0:T(8,128)(2,1)}, u32[]{:S(2)}, u32[]{:S(2)}) %collective-permute-start.17) | collective-permute-done | bytes 262176 | tf_op jit(solution)/shard_map/ppermute | solution.py:42
  27.1 5.9 %collective-permute-done.18.refs_4_ = bf16[2,2,64,512]{3,2,1,0:T(8,128)(2,1)} collective-permute-done((bf16[2,2,64,512]{3,2,1,0:T(8,128)(2,1)}, bf16[2,2,64,512]{3,2,1,0:T(8,128)(2,1)}, u32[]{:S(2)}, u32[]{:S(2)}) %collective-permute-start.18) | collective-permute-done | bytes 262176 | tf_op jit(solution)/shard_map/ppermute | solution.py:42
  33.0 0.9 collective-permute-done.20.refs_6_
  33.9 7.5 %product_of_cells.1 = (f32[256,128]{1,0:T(8,128)}, f32[256,128]{1,0:T(8,128)}, f32[256,128]{1,0:T(8,128)}, f32[256,128]{1,0:T(8,128)}, f32[4,256,128]{2,1,0:T(8,128)}) custom-call(s32[4]{0:T(128)} %pad_add_fusion.at, s32[512]{0:T(512)} %reshape.13.octants, bf16[16,64,512]{2,1,0:T(8,128)(2,1)} %now.7, bf16[16,64,512]{2,1,0:T(8,128)(2,1)} %prev.7, ...), custom_call_target="tpu_custom_call" | custom-call | flops 3221225472 | bytes 5242880 | tf_op jit(solution)/shard_map/product_of_cells/pallas_call | solution.py:165
  41.4 0.2 collective-permute-start.21
  41.5 2.0 collective-permute-done.21
  43.6 1.1 fusion
  44.6 2.7 %collective-permute-start.24 = (f32[256,128]{1,0:T(8,128)S(1)}, f32[256,128]{1,0:T(8,128)S(1)}, u32[]{:S(2)}, u32[]{:S(2)}) collective-permute-start(f32[256,128]{1,0:T(8,128)S(1)} %get-tuple-element.57), channel_id=1, source_target_pairs={{0,6},{2,0},{4,2},{6,4},{1,7},{3,1},{5,3},{7,5},{8,14},{10,8},{12,... | collective-permute-start | bytes 393224 | tf_op jit(solution)/shard_map/ppermute | solution.py:190
  47.3 1.4 collective-permute-start.23
  48.7 0.0 collective-permute-start.22
  48.7 1.7 collective-permute-done.24
  50.5 2.8 %collective-permute-done.23 = f32[256,128]{1,0:T(8,128)S(1)} collective-permute-done((f32[256,128]{1,0:T(8,128)S(1)}, f32[256,128]{1,0:T(8,128)S(1)}, u32[]{:S(2)}, u32[]{:S(2)}) %collective-permute-start.23) | collective-permute-done | bytes 131104 | tf_op jit(solution)/shard_map/ppermute | solution.py:190
  53.2 3.5 %collective-permute-done.22 = f32[256,128]{1,0:T(8,128)S(1)} collective-permute-done((f32[256,128]{1,0:T(8,128)S(1)}, f32[256,128]{1,0:T(8,128)S(1)}, u32[]{:S(2)}, u32[]{:S(2)}) %collective-permute-start.22) | collective-permute-done | bytes 131104 | tf_op jit(solution)/shard_map/ppermute | solution.py:190
  56.7 0.9 fusion.5
  57.7 14.3 %all_to_all.20 = f32[16,16,128]{2,1,0:T(8,128)S(1)} all-to-all(f32[16,16,128]{2,1,0:T(8,128)S(1)} %bitcast.26), channel_id=1, replica_groups=mesh['dom_0'=4,'dom_1'=4,'band_0'=4,'band_1'=2] {'dom_0','dom_1'}, dimensions={0} | all-to-all | bytes 262144 | tf_op jit(solution)/shard_map/all_to_all | solution.py:195
  72.0 0.7 broadcast_in_dim.2
  72.7 5.9 %all-to-all-start.3 = ((bf16[64,16,128]{2,1,0:T(8,128)(2,1)}), bf16[64,16,128]{2,1,0:T(8,128)(2,1)}, u32[]{:S(2)}, u32[]{:S(2)}) async-start(bf16[64,16,128]{2,1,0:T(8,128)(2,1)} %broadcast_in_dim.2), calls=%async_computation.3 | async-start | bytes 524288 | tf_op jit(solution)/shard_map/all_to_all | solution.py:198
  78.6 3.5 %shard_map.55 = bf16[16,2,64,512]{3,2,1,0:T(8,128)(2,1)} custom-call(s32[4]{0:T(128)} %pad_add_fusion.at, s32[256]{0:T(256)} %owners.5, bf16[16,64,512]{2,1,0:T(8,128)(2,1)} %now.7, bf16[16,64,512]{2,1,0:T(8,128)(2,1)} %prev.7), custom_call_target="tpu_custom_call" | custom-call | bytes 4194304 | tf_op jit(solution)/shard_map/pallas_call | solution.py:239
  82.1 5.8 %all-to-all-done.3 = bf16[64,16,128]{2,1,0:T(8,128)(2,1)} async-done(((bf16[64,16,128]{2,1,0:T(8,128)(2,1)}), bf16[64,16,128]{2,1,0:T(8,128)(2,1)}, u32[]{:S(2)}, u32[]{:S(2)}) %all-to-all-start.3) | async-done | bytes 262176 | tf_op jit(solution)/shard_map/all_to_all | solution.py:198
  87.9 4.4 %all-to-all-start = ((bf16[16,2,64,512]{3,2,1,0:T(8,128)(2,1)}), bf16[16,2,64,512]{3,2,1,0:T(8,128)(2,1)}, u32[]{:S(2)}, u32[]{:S(2)}) async-start(bf16[16,2,64,512]{3,2,1,0:T(8,128)(2,1)} %shard_map.55), calls=%async_computation | async-start | bytes 4194304 | tf_op jit(solution)/shard_map/all_to_all | solution.py:405
  92.4 3.6 %shard_map.57 = bf16[16,2,64,512]{3,2,1,0:T(8,128)(2,1)} custom-call(s32[4]{0:T(128)} %pad_add_fusion.at, s32[256]{0:T(256)} %owners.5, bf16[16,64,512]{2,1,0:T(8,128)(2,1)} %now.7, bf16[16,64,512]{2,1,0:T(8,128)(2,1)} %prev.7), custom_call_target="tpu_custom_call" | custom-call | bytes 4194304 | tf_op jit(solution)/shard_map/pallas_call | solution.py:239
  95.9 21.7 %all-to-all-done.slots.refs_0_ = bf16[16,2,64,512]{3,2,1,0:T(8,128)(2,1)} async-done(((bf16[16,2,64,512]{3,2,1,0:T(8,128)(2,1)}), bf16[16,2,64,512]{3,2,1,0:T(8,128)(2,1)}, u32[]{:S(2)}, u32[]{:S(2)}) %all-to-all-start) | async-done | bytes 2097184 | tf_op jit(solution)/shard_map/all_to_all | solution.py:405
  117.6 7.3 %all-to-all-start.1 = ((bf16[16,2,64,512]{3,2,1,0:T(8,128)(2,1)}), bf16[16,2,64,512]{3,2,1,0:T(8,128)(2,1)}, u32[]{:S(2)}, u32[]{:S(2)}) async-start(bf16[16,2,64,512]{3,2,1,0:T(8,128)(2,1)} %shard_map.57), calls=%async_computation.1 | async-start | bytes 4194304 | tf_op jit(solution)/shard_map/all_to_all | solution.py:405
  124.9 2.9 %collective-permute-start.25 = (bf16[16,4,16,128]{3,2,1,0:T(8,128)(2,1)}, bf16[16,4,16,128]{3,2,1,0:T(8,128)(2,1)}, u32[]{:S(2)}, u32[]{:S(2)}) collective-permute-start(bf16[16,4,16,128]{3,2,1,0:T(8,128)(2,1)} %bitcast.9.refs_16_), channel_id=1, source_target_pairs={{0,1},{1,0},{2,3},{3,2},{4,5},{5,4},{6,7},{7,6},{8,9},{9,8},{10,11... | collective-permute-start | bytes 786440 | tf_op jit(solution)/shard_map/ppermute | solution.py:200
  127.8 3.0 %shard_map.56 = (bf16[2,2,64,512]{3,2,1,0:T(8,128)(2,1)}, bf16[2,2,64,512]{3,2,1,0:T(8,128)(2,1)}, bf16[2,2,64,512]{3,2,1,0:T(8,128)(2,1)}, bf16[2,2,64,512]{3,2...) custom-call(s32[4]{0:T(128)} %pad_add_fusion.at, ...), custom_call_target="tpu_custom_call" | custom-call | bytes 3670016 | tf_op jit(solution)/shard_map/pallas_call | solution.py:276
  130.9 0.1 collective-permute-start
  131.0 0.3 collective-permute-start.1
  131.3 0.6 collective-permute-start.2
  131.9 3.6 %collective-permute-start.3 = (bf16[2,2,64,512]{3,2,1,0:T(8,128)(2,1)}, bf16[2,2,64,512]{3,2,1,0:T(8,128)(2,1)}, u32[]{:S(2)}, u32[]{:S(2)}) collective-permute-start(bf16[2,2,64,512]{3,2,1,0:T(8,128)(2,1)} %get-tuple-element.34), channel_id=1, source_target_pairs={{0,4},{1,5},{2,6},{3,7},{4,0},{5,1},{6,2},{7,3},{8,12},{9,13},{10,... | collective-permute-start | bytes 786440 | tf_op jit(solution)/shard_map/ppermute | solution.py:42
  135.5 15.0 %all-to-all-done.1.slots.refs_8_ = bf16[16,2,64,512]{3,2,1,0:T(8,128)(2,1)} async-done(((bf16[16,2,64,512]{3,2,1,0:T(8,128)(2,1)}), bf16[16,2,64,512]{3,2,1,0:T(8,128)(2,1)}, u32[]{:S(2)}, u32[]{:S(2)}) %all-to-all-start.1) | async-done | bytes 2097184 | tf_op jit(solution)/shard_map/all_to_all | solution.py:405
  150.4 3.0 %shard_map.58 = (bf16[2,2,64,512]{3,2,1,0:T(8,128)(2,1)}, bf16[2,2,64,512]{3,2,1,0:T(8,128)(2,1)}, bf16[2,2,64,512]{3,2,1,0:T(8,128)(2,1)}, bf16[2,2,64,512]{3,2...) custom-call(s32[4]{0:T(128)} %pad_add_fusion.at, ...), custom_call_target="tpu_custom_call" | custom-call | bytes 3670016 | tf_op jit(solution)/shard_map/pallas_call | solution.py:276
  153.5 6.3 %collective-permute-start.4 = (bf16[2,2,64,512]{3,2,1,0:T(8,128)(2,1)}, bf16[2,2,64,512]{3,2,1,0:T(8,128)(2,1)}, u32[]{:S(2)}, u32[]{:S(2)}) collective-permute-start(bf16[2,2,64,512]{3,2,1,0:T(8,128)(2,1)} %get-tuple-element.35), channel_id=1, source_target_pairs={{0,5},{1,4},{2,7},{3,6},{4,1},{5,0},{6,3},{7,2},{8,13},{9,12},{10,... | collective-permute-start | bytes 786440 | tf_op jit(solution)/shard_map/ppermute | solution.py:42
  159.8 2.1 collective-permute-start.5
  161.8 0.0 collective-permute-start.6
  161.8 1.0 collective-permute-start.7
  162.9 0.8 collective-permute-start.8
  163.7 2.6 %collective-permute-done.4.refs_5_ = bf16[2,2,64,512]{3,2,1,0:T(8,128)(2,1)} collective-permute-done((bf16[2,2,64,512]{3,2,1,0:T(8,128)(2,1)}, bf16[2,2,64,512]{3,2,1,0:T(8,128)(2,1)}, u32[]{:S(2)}, u32[]{:S(2)}) %collective-permute-start.4) | collective-permute-done | bytes 262176 | tf_op jit(solution)/shard_map/ppermute | solution.py:42
  166.3 3.6 %collective-permute-start.9 = (bf16[2,2,64,512]{3,2,1,0:T(8,128)(2,1)}, bf16[2,2,64,512]{3,2,1,0:T(8,128)(2,1)}, u32[]{:S(2)}, u32[]{:S(2)}) collective-permute-start(bf16[2,2,64,512]{3,2,1,0:T(8,128)(2,1)} %get-tuple-element.40), channel_id=1, source_target_pairs={{0,3},{1,2},{2,5},{3,4},{4,7},{5,6},{6,1},{7,0},{8,11},{9,10},{10,... | collective-permute-start | bytes 786440 | tf_op jit(solution)/shard_map/ppermute | solution.py:42
  169.9 3.1 %collective-permute-done.5.refs_6_ = bf16[2,2,64,512]{3,2,1,0:T(8,128)(2,1)} collective-permute-done((bf16[2,2,64,512]{3,2,1,0:T(8,128)(2,1)}, bf16[2,2,64,512]{3,2,1,0:T(8,128)(2,1)}, u32[]{:S(2)}, u32[]{:S(2)}) %collective-permute-start.5) | collective-permute-done | bytes 262176 | tf_op jit(solution)/shard_map/ppermute | solution.py:42
  173.0 2.8 %collective-permute-start.10 = (bf16[2,2,64,512]{3,2,1,0:T(8,128)(2,1)}, bf16[2,2,64,512]{3,2,1,0:T(8,128)(2,1)}, u32[]{:S(2)}, u32[]{:S(2)}) collective-permute-start(bf16[2,2,64,512]{3,2,1,0:T(8,128)(2,1)} %get-tuple-element.41), channel_id=1, source_target_pairs={{0,4},{1,5},{2,6},{3,7},{4,0},{5,1},{6,2},{7,3},{8,12},{9,13},{10,... | collective-permute-start | bytes 786440 | tf_op jit(solution)/shard_map/ppermute | solution.py:42
  175.8 1.9 collective-permute-done.6.refs_7_
  177.7 2.4 %collective-permute-start.11 = (bf16[2,2,64,512]{3,2,1,0:T(8,128)(2,1)}, bf16[2,2,64,512]{3,2,1,0:T(8,128)(2,1)}, u32[]{:S(2)}, u32[]{:S(2)}) collective-permute-start(bf16[2,2,64,512]{3,2,1,0:T(8,128)(2,1)} %get-tuple-element.42), channel_id=1, source_target_pairs={{0,5},{1,4},{2,7},{3,6},{4,1},{5,0},{6,3},{7,2},{8,13},{9,12},{10,... | collective-permute-start | bytes 786440 | tf_op jit(solution)/shard_map/ppermute | solution.py:42
  180.1 0.0 collective-permute-done.7.refs_9_
  180.1 1.7 collective-permute-start.12
  181.8 0.0 collective-permute-start.13
  181.9 7.9 %collective-permute-done.9.refs_11_ = bf16[2,2,64,512]{3,2,1,0:T(8,128)(2,1)} collective-permute-done((bf16[2,2,64,512]{3,2,1,0:T(8,128)(2,1)}, bf16[2,2,64,512]{3,2,1,0:T(8,128)(2,1)}, u32[]{:S(2)}, u32[]{:S(2)}) %collective-permute-start.9) | collective-permute-done | bytes 262176 | tf_op jit(solution)/shard_map/ppermute | solution.py:42
  189.8 5.4 %collective-permute-done.12.refs_14_ = bf16[2,2,64,512]{3,2,1,0:T(8,128)(2,1)} collective-permute-done((bf16[2,2,64,512]{3,2,1,0:T(8,128)(2,1)}, bf16[2,2,64,512]{3,2,1,0:T(8,128)(2,1)}, u32[]{:S(2)}, u32[]{:S(2)}) %collective-permute-start.12) | collective-permute-done | bytes 262176 | tf_op jit(solution)/shard_map/ppermute | solution.py:42
  195.2 5.2 %collective-permute-done.13.refs_15_ = bf16[2,2,64,512]{3,2,1,0:T(8,128)(2,1)} collective-permute-done((bf16[2,2,64,512]{3,2,1,0:T(8,128)(2,1)}, bf16[2,2,64,512]{3,2,1,0:T(8,128)(2,1)}, u32[]{:S(2)}, u32[]{:S(2)}) %collective-permute-start.13) | collective-permute-done | bytes 262176 | tf_op jit(solution)/shard_map/ppermute | solution.py:42
  200.3 7.0 %predict.1 = bf16[8,512,512]{2,1,0:T(8,128)(2,1)} custom-call(s32[4]{0:T(128)} %pad_add_fusion.at, s32[256]{0:T(256)} %owners.5, s32[512]{0:T(512)} %reshape.13.octants, bf16[16,2,64,512]{3,2,1,0:T(8,128)(2,1)} %all-to-all-done.slots.refs_0_, bf16[2,2,64,512]{3,2,1,0:T(8,128)(2,1)} %collective-permute-done.refs_1_, ...), custom_call_target="tpu_custom_call" | custom-call | flops 3221225472 | bytes 13631488 | tf_op jit(solution)/shard_map/predict/pallas_call | solution.py:374
  (14 shorter events, 0.1 us)
Async XLA Ops:
  3.7 7.7 %collective-permute-start.14 = (bf16[2,2,64,512]{3,2,1,0:T(8,128)(2,1)}, bf16[2,2,64,512]{3,2,1,0:T(8,128)(2,1)S(1)}, u32[]{:S(2)}, u32[]{:S(2)}) collective-permute-start(bf16[2,2,64,512]{3,2,1,0:T(8,128)(2,1)} %get-tuple-element.45), channel_id=1, source_target_pairs={{0,1},{1,0},{2,3},{3,2},{4,5},{5,4},{6,7},{7,6},{8,9},{9,8},{10,11... | collective-permute-start | bytes 786440 | tf_op jit(solution)/shard_map/ppermute | solution.py:42
  5.2 9.5 %collective-permute-start.15 = (bf16[2,2,64,512]{3,2,1,0:T(8,128)(2,1)}, bf16[2,2,64,512]{3,2,1,0:T(8,128)(2,1)S(1)}, u32[]{:S(2)}, u32[]{:S(2)}) collective-permute-start(bf16[2,2,64,512]{3,2,1,0:T(8,128)(2,1)} %get-tuple-element.46), channel_id=1, source_target_pairs={{0,2},{1,3},{2,4},{3,5},{4,6},{5,7},{6,0},{7,1},{8,10},{9,11},{10,... | collective-permute-start | bytes 786440 | tf_op jit(solution)/shard_map/ppermute | solution.py:42
  6.6 13.9 %collective-permute-start.16 = (bf16[2,2,64,512]{3,2,1,0:T(8,128)(2,1)}, bf16[2,2,64,512]{3,2,1,0:T(8,128)(2,1)}, u32[]{:S(2)}, u32[]{:S(2)}) collective-permute-start(bf16[2,2,64,512]{3,2,1,0:T(8,128)(2,1)} %get-tuple-element.47), channel_id=1, source_target_pairs={{0,3},{1,2},{2,5},{3,4},{4,7},{5,6},{6,1},{7,0},{8,11},{9,10},{10,... | collective-permute-start | bytes 786440 | tf_op jit(solution)/shard_map/ppermute | solution.py:42
  8.2 18.9 %collective-permute-start.17 = (bf16[2,2,64,512]{3,2,1,0:T(8,128)(2,1)}, bf16[2,2,64,512]{3,2,1,0:T(8,128)(2,1)}, u32[]{:S(2)}, u32[]{:S(2)}) collective-permute-start(bf16[2,2,64,512]{3,2,1,0:T(8,128)(2,1)} %get-tuple-element.48), channel_id=1, source_target_pairs={{0,4},{1,5},{2,6},{3,7},{4,0},{5,1},{6,2},{7,3},{8,12},{9,13},{10,... | collective-permute-start | bytes 786440 | tf_op jit(solution)/shard_map/ppermute | solution.py:42
  9.3 23.7 %collective-permute-start.18 = (bf16[2,2,64,512]{3,2,1,0:T(8,128)(2,1)}, bf16[2,2,64,512]{3,2,1,0:T(8,128)(2,1)}, u32[]{:S(2)}, u32[]{:S(2)}) collective-permute-start(bf16[2,2,64,512]{3,2,1,0:T(8,128)(2,1)} %get-tuple-element.49), channel_id=1, source_target_pairs={{0,5},{1,4},{2,7},{3,6},{4,1},{5,0},{6,3},{7,2},{8,13},{9,12},{10,... | collective-permute-start | bytes 786440 | tf_op jit(solution)/shard_map/ppermute | solution.py:42
  11.4 3.3 %copy-start = (bf16[2,2,64,512]{3,2,1,0:T(8,128)(2,1)}, bf16[2,2,64,512]{3,2,1,0:T(8,128)(2,1)S(1)}, u32[]{:S(2)}) copy-start(bf16[2,2,64,512]{3,2,1,0:T(8,128)(2,1)S(1)} %collective-permute-done.14.refs_0_) | copy-start | bytes 786436
  11.4 21.5 %collective-permute-start.19 = (bf16[2,2,64,512]{3,2,1,0:T(8,128)(2,1)}, bf16[2,2,64,512]{3,2,1,0:T(8,128)(2,1)}, u32[]{:S(2)}, u32[]{:S(2)}) collective-permute-start(bf16[2,2,64,512]{3,2,1,0:T(8,128)(2,1)} %get-tuple-element.50), channel_id=1, source_target_pairs={{0,6},{1,7},{2,0},{3,1},{4,2},{5,3},{6,4},{7,5},{8,14},{9,15},{10,... | collective-permute-start | bytes 786440 | tf_op jit(solution)/shard_map/ppermute | solution.py:42
  14.8 0.7 copy-start.1
  15.5 18.4 %collective-permute-start.20 = (bf16[2,2,64,512]{3,2,1,0:T(8,128)(2,1)}, bf16[2,2,64,512]{3,2,1,0:T(8,128)(2,1)}, u32[]{:S(2)}, u32[]{:S(2)}) collective-permute-start(bf16[2,2,64,512]{3,2,1,0:T(8,128)(2,1)} %get-tuple-element.51), channel_id=1, source_target_pairs={{0,7},{1,6},{2,1},{3,0},{4,3},{5,2},{6,5},{7,4},{8,15},{9,14},{10,... | collective-permute-start | bytes 786440 | tf_op jit(solution)/shard_map/ppermute | solution.py:42
  41.4 2.2 %collective-permute-start.21 = (f32[4,256,128]{2,1,0:T(8,128)}, f32[4,256,128]{2,1,0:T(8,128)S(1)}, u32[]{:S(2)}, u32[]{:S(2)}) collective-permute-start(f32[4,256,128]{2,1,0:T(8,128)} %get-tuple-element.53), channel_id=1, source_target_pairs={{0,1},{1,0},{2,3},{3,2},{4,5},{5,4},{6,7},{7,6},{8,9},{9,8},{10,11... | collective-permute-start | bytes 1572872 | tf_op jit(solution)/shard_map/ppermute | solution.py:187
  44.6 5.8 %collective-permute-start.24 = (f32[256,128]{1,0:T(8,128)S(1)}, f32[256,128]{1,0:T(8,128)S(1)}, u32[]{:S(2)}, u32[]{:S(2)}) collective-permute-start(f32[256,128]{1,0:T(8,128)S(1)} %get-tuple-element.57), channel_id=1, source_target_pairs={{0,6},{2,0},{4,2},{6,4},{1,7},{3,1},{5,3},{7,5},{8,14},{10,8},{12,... | collective-permute-start | bytes 393224 | tf_op jit(solution)/shard_map/ppermute | solution.py:190
  47.3 5.9 %collective-permute-start.23 = (f32[256,128]{1,0:T(8,128)S(1)}, f32[256,128]{1,0:T(8,128)S(1)}, u32[]{:S(2)}, u32[]{:S(2)}) collective-permute-start(f32[256,128]{1,0:T(8,128)S(1)} %get-tuple-element.58), channel_id=1, source_target_pairs={{0,4},{2,6},{4,0},{6,2},{1,5},{3,7},{5,1},{7,3},{8,12},{10,14},{12... | collective-permute-start | bytes 393224 | tf_op jit(solution)/shard_map/ppermute | solution.py:190
  48.7 8.0 %collective-permute-start.22 = (f32[256,128]{1,0:T(8,128)S(1)}, f32[256,128]{1,0:T(8,128)S(1)}, u32[]{:S(2)}, u32[]{:S(2)}) collective-permute-start(f32[256,128]{1,0:T(8,128)S(1)} %get-tuple-element.59), channel_id=1, source_target_pairs={{0,2},{2,4},{4,6},{6,0},{1,3},{3,5},{5,7},{7,1},{8,10},{10,12},{12... | collective-permute-start | bytes 393224 | tf_op jit(solution)/shard_map/ppermute | solution.py:190
  72.7 15.2 %all-to-all-start.3 = ((bf16[64,16,128]{2,1,0:T(8,128)(2,1)}), bf16[64,16,128]{2,1,0:T(8,128)(2,1)}, u32[]{:S(2)}, u32[]{:S(2)}) async-start(bf16[64,16,128]{2,1,0:T(8,128)(2,1)} %broadcast_in_dim.2), calls=%async_computation.3 | async-start | bytes 524288 | tf_op jit(solution)/shard_map/all_to_all | solution.py:198
  87.9 29.7 %all-to-all-start = ((bf16[16,2,64,512]{3,2,1,0:T(8,128)(2,1)}), bf16[16,2,64,512]{3,2,1,0:T(8,128)(2,1)}, u32[]{:S(2)}, u32[]{:S(2)}) async-start(bf16[16,2,64,512]{3,2,1,0:T(8,128)(2,1)} %shard_map.55), calls=%async_computation | async-start | bytes 4194304 | tf_op jit(solution)/shard_map/all_to_all | solution.py:405
  117.6 32.8 %all-to-all-start.1 = ((bf16[16,2,64,512]{3,2,1,0:T(8,128)(2,1)}), bf16[16,2,64,512]{3,2,1,0:T(8,128)(2,1)}, u32[]{:S(2)}, u32[]{:S(2)}) async-start(bf16[16,2,64,512]{3,2,1,0:T(8,128)(2,1)} %shard_map.57), calls=%async_computation.1 | async-start | bytes 4194304 | tf_op jit(solution)/shard_map/all_to_all | solution.py:405
  124.9 28.5 %collective-permute-start.25 = (bf16[16,4,16,128]{3,2,1,0:T(8,128)(2,1)}, bf16[16,4,16,128]{3,2,1,0:T(8,128)(2,1)}, u32[]{:S(2)}, u32[]{:S(2)}) collective-permute-start(bf16[16,4,16,128]{3,2,1,0:T(8,128)(2,1)} %bitcast.9.refs_16_), channel_id=1, source_target_pairs={{0,1},{1,0},{2,3},{3,2},{4,5},{5,4},{6,7},{7,6},{8,9},{9,8},{10,11... | collective-permute-start | bytes 786440 | tf_op jit(solution)/shard_map/ppermute | solution.py:200
  130.9 28.9 %collective-permute-start = (bf16[2,2,64,512]{3,2,1,0:T(8,128)(2,1)}, bf16[2,2,64,512]{3,2,1,0:T(8,128)(2,1)}, u32[]{:S(2)}, u32[]{:S(2)}) collective-permute-start(bf16[2,2,64,512]{3,2,1,0:T(8,128)(2,1)} %get-tuple-element.31), channel_id=1, source_target_pairs={{0,1},{1,0},{2,3},{3,2},{4,5},{5,4},{6,7},{7,6},{8,9},{9,8},{10,11... | collective-permute-start | bytes 786440 | tf_op jit(solution)/shard_map/ppermute | solution.py:42
  131.0 30.9 %collective-permute-start.1 = (bf16[2,2,64,512]{3,2,1,0:T(8,128)(2,1)}, bf16[2,2,64,512]{3,2,1,0:T(8,128)(2,1)}, u32[]{:S(2)}, u32[]{:S(2)}) collective-permute-start(bf16[2,2,64,512]{3,2,1,0:T(8,128)(2,1)} %get-tuple-element.32), channel_id=1, source_target_pairs={{0,2},{1,3},{2,4},{3,5},{4,6},{5,7},{6,0},{7,1},{8,10},{9,11},{10,... | collective-permute-start | bytes 786440 | tf_op jit(solution)/shard_map/ppermute | solution.py:42
  131.3 30.6 %collective-permute-start.2 = (bf16[2,2,64,512]{3,2,1,0:T(8,128)(2,1)}, bf16[2,2,64,512]{3,2,1,0:T(8,128)(2,1)}, u32[]{:S(2)}, u32[]{:S(2)}) collective-permute-start(bf16[2,2,64,512]{3,2,1,0:T(8,128)(2,1)} %get-tuple-element.33), channel_id=1, source_target_pairs={{0,3},{1,2},{2,5},{3,4},{4,7},{5,6},{6,1},{7,0},{8,11},{9,10},{10,... | collective-permute-start | bytes 786440 | tf_op jit(solution)/shard_map/ppermute | solution.py:42
  131.9 31.0 %collective-permute-start.3 = (bf16[2,2,64,512]{3,2,1,0:T(8,128)(2,1)}, bf16[2,2,64,512]{3,2,1,0:T(8,128)(2,1)}, u32[]{:S(2)}, u32[]{:S(2)}) collective-permute-start(bf16[2,2,64,512]{3,2,1,0:T(8,128)(2,1)} %get-tuple-element.34), channel_id=1, source_target_pairs={{0,4},{1,5},{2,6},{3,7},{4,0},{5,1},{6,2},{7,3},{8,12},{9,13},{10,... | collective-permute-start | bytes 786440 | tf_op jit(solution)/shard_map/ppermute | solution.py:42
  153.5 12.8 %collective-permute-start.4 = (bf16[2,2,64,512]{3,2,1,0:T(8,128)(2,1)}, bf16[2,2,64,512]{3,2,1,0:T(8,128)(2,1)}, u32[]{:S(2)}, u32[]{:S(2)}) collective-permute-start(bf16[2,2,64,512]{3,2,1,0:T(8,128)(2,1)} %get-tuple-element.35), channel_id=1, source_target_pairs={{0,5},{1,4},{2,7},{3,6},{4,1},{5,0},{6,3},{7,2},{8,13},{9,12},{10,... | collective-permute-start | bytes 786440 | tf_op jit(solution)/shard_map/ppermute | solution.py:42
  159.8 13.2 %collective-permute-start.5 = (bf16[2,2,64,512]{3,2,1,0:T(8,128)(2,1)}, bf16[2,2,64,512]{3,2,1,0:T(8,128)(2,1)}, u32[]{:S(2)}, u32[]{:S(2)}) collective-permute-start(bf16[2,2,64,512]{3,2,1,0:T(8,128)(2,1)} %get-tuple-element.36), channel_id=1, source_target_pairs={{0,6},{1,7},{2,0},{3,1},{4,2},{5,3},{6,4},{7,5},{8,14},{9,15},{10,... | collective-permute-start | bytes 786440 | tf_op jit(solution)/shard_map/ppermute | solution.py:42
  161.8 15.9 %collective-permute-start.6 = (bf16[2,2,64,512]{3,2,1,0:T(8,128)(2,1)}, bf16[2,2,64,512]{3,2,1,0:T(8,128)(2,1)}, u32[]{:S(2)}, u32[]{:S(2)}) collective-permute-start(bf16[2,2,64,512]{3,2,1,0:T(8,128)(2,1)} %get-tuple-element.37), channel_id=1, source_target_pairs={{0,7},{1,6},{2,1},{3,0},{4,3},{5,2},{6,5},{7,4},{8,15},{9,14},{10,... | collective-permute-start | bytes 786440 | tf_op jit(solution)/shard_map/ppermute | solution.py:42
  161.8 18.3 %collective-permute-start.7 = (bf16[2,2,64,512]{3,2,1,0:T(8,128)(2,1)}, bf16[2,2,64,512]{3,2,1,0:T(8,128)(2,1)}, u32[]{:S(2)}, u32[]{:S(2)}) collective-permute-start(bf16[2,2,64,512]{3,2,1,0:T(8,128)(2,1)} %get-tuple-element.38), channel_id=1, source_target_pairs={{0,1},{1,0},{2,3},{3,2},{4,5},{5,4},{6,7},{7,6},{8,9},{9,8},{10,11... | collective-permute-start | bytes 786440 | tf_op jit(solution)/shard_map/ppermute | solution.py:42
  162.9 19.0 %collective-permute-start.8 = (bf16[2,2,64,512]{3,2,1,0:T(8,128)(2,1)}, bf16[2,2,64,512]{3,2,1,0:T(8,128)(2,1)}, u32[]{:S(2)}, u32[]{:S(2)}) collective-permute-start(bf16[2,2,64,512]{3,2,1,0:T(8,128)(2,1)} %get-tuple-element.39), channel_id=1, source_target_pairs={{0,2},{1,3},{2,4},{3,5},{4,6},{5,7},{6,0},{7,1},{8,10},{9,11},{10,... | collective-permute-start | bytes 786440 | tf_op jit(solution)/shard_map/ppermute | solution.py:42
  166.3 23.5 %collective-permute-start.9 = (bf16[2,2,64,512]{3,2,1,0:T(8,128)(2,1)}, bf16[2,2,64,512]{3,2,1,0:T(8,128)(2,1)}, u32[]{:S(2)}, u32[]{:S(2)}) collective-permute-start(bf16[2,2,64,512]{3,2,1,0:T(8,128)(2,1)} %get-tuple-element.40), channel_id=1, source_target_pairs={{0,3},{1,2},{2,5},{3,4},{4,7},{5,6},{6,1},{7,0},{8,11},{9,10},{10,... | collective-permute-start | bytes 786440 | tf_op jit(solution)/shard_map/ppermute | solution.py:42
  173.0 16.8 %collective-permute-start.10 = (bf16[2,2,64,512]{3,2,1,0:T(8,128)(2,1)}, bf16[2,2,64,512]{3,2,1,0:T(8,128)(2,1)}, u32[]{:S(2)}, u32[]{:S(2)}) collective-permute-start(bf16[2,2,64,512]{3,2,1,0:T(8,128)(2,1)} %get-tuple-element.41), channel_id=1, source_target_pairs={{0,4},{1,5},{2,6},{3,7},{4,0},{5,1},{6,2},{7,3},{8,12},{9,13},{10,... | collective-permute-start | bytes 786440 | tf_op jit(solution)/shard_map/ppermute | solution.py:42
  177.7 12.0 %collective-permute-start.11 = (bf16[2,2,64,512]{3,2,1,0:T(8,128)(2,1)}, bf16[2,2,64,512]{3,2,1,0:T(8,128)(2,1)}, u32[]{:S(2)}, u32[]{:S(2)}) collective-permute-start(bf16[2,2,64,512]{3,2,1,0:T(8,128)(2,1)} %get-tuple-element.42), channel_id=1, source_target_pairs={{0,5},{1,4},{2,7},{3,6},{4,1},{5,0},{6,3},{7,2},{8,13},{9,12},{10,... | collective-permute-start | bytes 786440 | tf_op jit(solution)/shard_map/ppermute | solution.py:42
  180.1 15.0 %collective-permute-start.12 = (bf16[2,2,64,512]{3,2,1,0:T(8,128)(2,1)}, bf16[2,2,64,512]{3,2,1,0:T(8,128)(2,1)}, u32[]{:S(2)}, u32[]{:S(2)}) collective-permute-start(bf16[2,2,64,512]{3,2,1,0:T(8,128)(2,1)} %get-tuple-element.43), channel_id=1, source_target_pairs={{0,6},{1,7},{2,0},{3,1},{4,2},{5,3},{6,4},{7,5},{8,14},{9,15},{10,... | collective-permute-start | bytes 786440 | tf_op jit(solution)/shard_map/ppermute | solution.py:42
  181.8 18.5 %collective-permute-start.13 = (bf16[2,2,64,512]{3,2,1,0:T(8,128)(2,1)}, bf16[2,2,64,512]{3,2,1,0:T(8,128)(2,1)}, u32[]{:S(2)}, u32[]{:S(2)}) collective-permute-start(bf16[2,2,64,512]{3,2,1,0:T(8,128)(2,1)} %get-tuple-element.44), channel_id=1, source_target_pairs={{0,7},{1,6},{2,1},{3,0},{4,3},{5,2},{6,5},{7,4},{8,15},{9,14},{10,... | collective-permute-start | bytes 786440 | tf_op jit(solution)/shard_map/ppermute | solution.py:42

commit v2 on v1

--- a/solution.py
+++ b/solution.py
@@ -20,7 +20,8 @@
 F32 = jnp.float32
 RING = 4
 CORES = 2
-OFFSETS = tuple((q, l) for q in range(RING) for l in range(CORES))
+UNIT = 16
+OFFSETS = ((0, 0), (1, 0), (3, 0), (2, 0), (1, 1), (3, 1), (2, 1), (0, 1))
 
 
 WHOLE_VMEM = pltpu.CompilerParams(vmem_limit_bytes=67_043_328)
@@ -96,8 +97,8 @@
 
 
 def product_kernel(at, octants, now, prev, *refs):
-    pieces, interp, mine, other = refs[:7], refs[7], refs[8:12], refs[12]
-    parents, matrices, kids, out, in_sem, mat_sem, out_sem = refs[13:]
+    pieces, interp, mine, other = refs[:7], refs[7], refs[8], refs[9]
+    parents, matrices, kids, out, in_sem, mat_sem, out_sem = refs[10:]
     z, x, y, c = at[0], at[1], at[2], at[3]
     rows = now.shape[1]
     nodes = now.shape[2]
@@ -148,12 +149,10 @@
         part = lax.dot_general(
             kids[1, u, :], kids[0], (((1,), (1,)), ((), ())), preferred_element_type=F32
         )
-        for t in range(RING):
+        for t in range(states // 128):
             out[n, t] = part[:, t * 128 : (t + 1) * 128]
-        for k in range(RING):
-            dst = mine[k] if n else other.at[k]
-            stores.append(pltpu.make_async_copy(out.at[n, (y + k) & 3], dst, out_sem.at[n, k]))
-            stores[-1].start()
+        stores.append(pltpu.make_async_copy(out.at[n], mine if n else other, out_sem.at[n]))
+        stores[-1].start()
     for store in stores:
         store.wait()
 
@@ -161,20 +160,20 @@
 def product_of_cells(at, octants, now, prev, pieces, interp):
     _, rows, nodes = now.shape
     states = rows * RING * CORES
-    block = (states // 2, 128)
+    lanes = (states // 128, states // 2, 128)
     return pl.pallas_call(
         product_kernel,
-        out_shape=[sized(block, F32)] * RING + [sized((RING, *block), F32)],
+        out_shape=[sized(lanes, F32)] * 2,
         in_specs=[SMEM, SMEM] + [HBM] * 10,
-        out_specs=[HBM] * 5,
+        out_specs=[HBM] * 2,
         scratch_shapes=[
             pltpu.VMEM((2, 2, states, nodes), BF16),
             pltpu.VMEM((2, 2, nodes, nodes), BF16),
             pltpu.VMEM((2, states, 4 * nodes), BF16),
-            pltpu.VMEM((2, RING, *block), F32),
+            pltpu.VMEM((2, *lanes), F32),
             pltpu.SemaphoreType.DMA((2, 9)),
             pltpu.SemaphoreType.DMA((2, 2)),
-            pltpu.SemaphoreType.DMA((2, RING)),
+            pltpu.SemaphoreType.DMA((2,)),
         ],
         compiler_params=WHOLE_VMEM,
         cost_estimate=moved(4 << 20, 1 << 20, 24 * states * nodes * nodes),
@@ -184,73 +183,82 @@
 
 def summed_over_all(mine, other, scaling):
     swap = [(0, 1), (1, 0)]
-    other = lax.ppermute(other, C, swap)
-    blocks = [block + other[k] for k, block in enumerate(mine)]
-    blocks[1:] = [
-        lax.ppermute(blocks[k], Y, [(i, (i + k) % RING) for i in range(RING)])
+    half = mine + lax.ppermute(other, C, swap)
+    chips = lax.axis_size(CHIPS)
+    tiles = lax.all_to_all(half.reshape(chips, -1, 128), CHIPS, 0, 0, tiled=True)
+    own = (jnp.sum(tiles, axis=0) * scaling).astype(BF16)
+    own = jnp.stack([own, lax.ppermute(own, C, swap)])
+    own = jnp.broadcast_to(own[None], (chips // RING, *own.shape))
+    own = lax.all_to_all(own, DOM, 0, 0, tiled=True)
+    own = own.reshape(RING, RING, *own.shape[1:])
+    return [own] + [
+        lax.ppermute(own, Y, [(i, (i + k) % RING) for i in range(RING)])
         for k in range(1, RING)
     ]
-    block = (blocks[0] + blocks[1]) + (blocks[2] + blocks[3])
-    doms = lax.axis_size(DOM)
-    tiles = lax.all_to_all(block.reshape(doms, -1, 128), DOM, 0, 0, tiled=True)
-    own = (jnp.sum(tiles, axis=0) * scaling).astype(BF16)
-    own = jnp.broadcast_to(own[None], (doms * RING, *own.shape))
-    own = lax.all_to_all(own, CHIPS, 0, 0, tiled=True)
-    own = own.reshape(doms, RING, -1, 128)
-    return own, lax.ppermute(own, C, swap)
-
-
-def slots_kernel(rank, at, owners, now, prev, out, cells, slot, seen, in_sem, out_sem):
-    z, x = at[0], at[1]
+
+
+def slots_kernel(parts, owners, octants, now, prev, out, cells, slot, seen, in_sem, out_sem):
+    z, x = lax.axis_index(Z), lax.axis_index(X)
     old = now.shape[0]
+    doms = RING * RING
     first = (z * RING + x) * old
     loads = [
         pltpu.make_async_copy(src, cells.at[a], in_sem.at[a]) for a, src in enumerate((now, prev))
     ]
     for load in loads:
         load.start()
-    for d in range(RING * RING):
+    for d in range(doms):
         seen[d] = 0
-        slot[d] = 0
+        for rank in range(2):
+            slot[rank * doms + d] = 0
 
     def place(i, carry):
         owner = owners[first + i]
-        slot[owner] = jnp.where(seen[owner] == rank, i, slot[owner])
-        seen[owner] = seen[owner] + 1
+        rank = jnp.minimum(seen[owner], 1)
+        slot[rank * doms + owner] = i
+        seen[owner] = rank + 1
         return carry
 
     lax.fori_loop(0, old, place, 0)
     stores = []
     for a in range(2):
         loads[a].wait()
-        for d in range(RING * RING):
-            stores.append(
-                pltpu.make_async_copy(cells.at[a, slot[d]], out.at[d, a], out_sem.at[a, d])
-            )
-            stores[-1].start()
+        at_unit = 0
+        for n, (rank, begin, units) in enumerate(parts):
+            for d in range(doms):
+                stores.append(
+                    pltpu.make_async_copy(
+                        cells.at[a, slot[rank * doms + d], pl.ds(begin, units)],
+                        out.at[d, pl.ds(at_unit, units), a],
+                        out_sem.at[n, a, d],
+                    )
+                )
+                stores[-1].start()
+            at_unit += units
     for store in stores:
         store.wait()
 
 
-def slots_for_owners(rank, at, owners, now, prev):
-    old, rows, nodes = now.shape
+def slots_for_owners(parts, owners, octants, now, prev):
+    old, units, _, nodes = now.shape
     doms = RING * RING
-    size = 2 * old * rows * nodes * 2
+    total = sum(n for _, _, n in parts)
+    size = 2 * doms * total * UNIT * nodes * 2
     return pl.pallas_call(
-        functools.partial(slots_kernel, rank),
-        out_shape=sized((doms, 2, rows, nodes)),
+        functools.partial(slots_kernel, parts),
+        out_shape=sized((doms, total, 2, UNIT, nodes)),
         in_specs=[SMEM, SMEM, HBM, HBM],
         out_specs=HBM,
         scratch_shapes=[
-            pltpu.VMEM((2, old, rows, nodes), BF16),
-            pltpu.SMEM((doms,), jnp.int32),
+            pltpu.VMEM((2, old, units, UNIT, nodes), BF16),
+            pltpu.SMEM((2 * doms,), jnp.int32),
             pltpu.SMEM((doms,), jnp.int32),
             pltpu.SemaphoreType.DMA((2,)),
-            pltpu.SemaphoreType.DMA((2, doms)),
+            pltpu.SemaphoreType.DMA((len(parts), 2, doms)),
         ],
         compiler_params=WHOLE_VMEM,
         cost_estimate=moved(size, size),
-    )(at, owners, now, prev)
+    )(owners, octants, now, prev)
 
 
 def route_kernel(at, slots, *refs):
@@ -289,23 +297,19 @@
 
 
 def predict_kernel(old, at, owners, octants, *refs):
-    slots, mine, other, interp, predicted = (refs[0], refs[8]), *refs[16:20]
-    pieces = (refs[1:8], refs[9:16])
-    parents, matrices, mix, out, in_sem, mat_sem, mix_sem, out_sem = refs[20:]
+    slots, pieces = (refs[0], refs[8]), (refs[1:8], refs[9:16])
+    tiles, interp, predicted = refs[16:20], refs[20], refs[21]
+    parents, matrices, planes, mix, out, in_sem, mat_sem, mix_sem, out_sem = refs[22:]
     z, x, y, c = at[0], at[1], at[2], at[3]
-    rows = slots[0].shape[2]
-    states = parents.shape[2]
-    blocks = mine.shape[0]
+    units = parents.shape[1] // (RING * CORES)
+    nodes = parents.shape[4]
+    states = parents.shape[1] * UNIT
     owner = z * RING + x
     mixing = []
-    for n, (side, src) in enumerate(((c, mine), (1 - c, other))):
-        u = pl.ds(side * blocks, blocks)
-        for t in range(RING):
-            mixing.append(
-                pltpu.make_async_copy(
-                    src.at[:, t], mix.at[u, :, pl.ds(t * 128, 128)], mix_sem.at[n, t]
-                )
-            )
+    for n, side in enumerate((c, 1 - c)):
+        for k in range(RING):
+            to = planes.at[:, side, :, (y - k) & 3]
+            mixing.append(pltpu.make_async_copy(tiles[k].at[:, :, n], to, mix_sem.at[n, k]))
     for copy in mixing:
         copy.start()
     loads, filled = [], []
@@ -324,9 +328,9 @@
         copies = []
         for n, (q, l) in enumerate(OFFSETS):
             b = ((y - q) & 3) * CORES + ((c - l) & 1)
-            to = pl.ds(pl.multiple_of(b * rows, rows), rows)
             src = pieces[rank][n - 1].at[e] if n else slots[rank].at[b * 2 + e]
-            copies.append(pltpu.make_async_copy(src, parents.at[k, :, to], in_sem.at[k, n]))
+            to = parents.at[k, pl.ds(b * units, units)]
+            copies.append(pltpu.make_async_copy(src, to, in_sem.at[k, n]))
         for j in range(2):
             o = octants[(first + cell) * 2 + j]
             copies.append(
@@ -337,6 +341,8 @@
         loads.append(copies)
     for copy in mixing:
         copy.wait()
+    for t in range(RING):
+        mix[:, pl.ds(t * 128, 128)] = planes[t].reshape(states, 128)
     stores = []
     for k in range(4):
         rank, e = k // 2, k % 2
@@ -345,10 +351,10 @@
 
         @pl.when(filled[k])
         def _(k=k):
-            mixed = jnp.dot(
-                mix[...].reshape(states, states), parents[k, 0], preferred_element_type=F32
-            )
-            value = (parents[k, 1].astype(F32) + mixed).astype(BF16)
+            now = parents[k, :, 0].reshape(states, nodes)
+            prev = parents[k, :, 1].reshape(states, nodes)
+            mixed = jnp.dot(mix[...], now, preferred_element_type=F32)
+            value = (prev.astype(F32) + mixed).astype(BF16)
             for j in range(2):
                 out[k, j] = lax.dot_general(
                     value, matrices[k, j], (((1,), (1,)), ((), ())), preferred_element_type=F32
@@ -368,18 +374,20 @@
         store.wait()
 
 
-def predict(old, at, owners, octants, slots, pieces, mine, other, interp):
-    _, _, rows, nodes = slots[0].shape
-    states = rows * RING * CORES
+def predict(old, at, owners, octants, slots, pieces, tiles, interp):
+    nodes = interp.shape[2]
+    units = slots[0].shape[1]
+    states = units * UNIT * RING * CORES
     return pl.pallas_call(
         functools.partial(predict_kernel, old),
         out_shape=sized((8, states, nodes)),
-        in_specs=[SMEM] * 3 + [HBM] * 19,
+        in_specs=[SMEM] * 3 + [HBM] * 21,
         out_specs=HBM,
         scratch_shapes=[
-            pltpu.VMEM((4, 2, states, nodes), BF16),
+            pltpu.VMEM((4, states // UNIT, 2, UNIT, nodes), BF16),
             pltpu.VMEM((4, 2, nodes, nodes), BF16),
-            pltpu.VMEM((states // 16, 16, states), BF16),
+            pltpu.VMEM((RING, CORES, RING, RING, 16, 128), BF16),
+            pltpu.VMEM((states, states), BF16),
             pltpu.VMEM((4, 2, states, nodes), BF16),
             pltpu.SemaphoreType.DMA((4, 8)),
             pltpu.SemaphoreType.DMA((4, 2)),
@@ -389,7 +397,7 @@
         compiler_params=WHOLE_VMEM,
         cost_estimate=moved(9 << 20, 4 << 20, 24 * states * nodes * nodes),
         name="predict",
-    )(at, owners, octants, slots[0], *pieces[0], slots[1], *pieces[1], mine, other, interp)
+    )(at, owners, octants, slots[0], *pieces[0], slots[1], *pieces[1], *tiles, interp)
 
 
 def refined(orbitals_now, orbitals_prev, interp, owner_map, child_oct):
@@ -399,19 +407,23 @@
     octants = child_oct.reshape(-1)
     scaling = 1.0 / math.sqrt(2.0 * states * owner_map.shape[0] * nodes)
 
+    units = rows // UNIT
+    by_unit = [a.reshape(old, units, UNIT, nodes) for a in (orbitals_now, orbitals_prev)]
+    parts = (((0, 0, units),), ((1, 0, units),))
     slots, pieces = [], []
-    for rank in range(2):
-        slots.append(slots_for_owners(rank, at, owner_map, orbitals_now, orbitals_prev))
-        slots[rank] = lax.all_to_all(slots[rank], DOM, 0, 0, tiled=True)
-        pieces.append(routed(at, slots[rank]))
-        pieces[rank] = over_band(pieces[rank])
+    for n in range(2):
+        table = octants if n else owner_map
+        slots.append(slots_for_owners(parts[n], owner_map, table, *by_unit))
+        slots[n] = lax.all_to_all(slots[n], DOM, 0, 0, tiled=True)
+        pieces.append(routed(at, slots[n]))
+        pieces[n] = over_band(pieces[n])
 
     cells = cells_for_band(at, orbitals_now, orbitals_prev)
     cells = over_band(cells)
-    *mine, other = product_of_cells(at, octants, orbitals_now, orbitals_prev, cells, interp)
-    mine, other = summed_over_all(mine, other, scaling)
-
-    return predict(old, at, owner_map, octants, slots, pieces, mine, other, interp)
+    mine, other = product_of_cells(at, octants, orbitals_now, orbitals_prev, cells, interp)
+    tiles = summed_over_all(mine, other, scaling)
+
+    return predict(old, at, owner_map, octants, slots, pieces, tiles, interp)
 
 
 def solution(mesh):

time: 208 us -> 195 us (0.938)
  waiting for transfers between devices: 94.6 us -> 71.9 us
  blocking collectives: 14.3 us -> 22.1 us
    ppermute x21, waiting for transfers between devices: 42.2 us -> 26.3 us  [over_band(): lax.ppermute(piece, BAND, band_pairs(q, l))]
    all_to_all x1, blocking collectives: 14.3 us -> 22.1 us  [summed_over_all(): lax.all_to_all(half.reshape(chips, -1, 128), CHIPS, 0, 0, tiled=True)]
    ppermute x5, waiting for transfers between devices: 10 us -> 2.93 us  [the longest x1 2.11 us: summed_over_all(): half = mine + lax.ppermute(other, C, swap)]
    ppermute x21, starting transfers between devices: 37.1 us -> 43.6 us  [over_band(): lax.ppermute(piece, BAND, band_pairs(q, l))]
    all_to_all x3, starting transfers between devices: 17.7 us -> 13.8 us  [the longest x2 9.63 us: refined(): slots[n] = lax.all_to_all(slots[n], DOM, 0, 0, tiled=True)]
  transfers between devices with their start and end apart: 29 -> 29, of which waited for: 18 -> 16; matrix products, arithmetic and copies ran while one was open for 1% -> 1% of each run, Pallas kernels for 6% -> 7%
where the time goes in v2:
time: 195 us; the launch traced here: 193 us
  waiting for transfers between devices  71.9 us (37%)
  starting transfers between devices  63 us (32%)
  Pallas kernels  30.5 us (16%)
  blocking collectives  22.1 us (11%)
  local copies, waits for them, and re-layouts  2.9 us (1%)
    ppermute x21, starting transfers between devices, over_band(): lax.ppermute(piece, BAND, band_pairs(q, l))  43.6 us
    all_to_all x2, waiting for transfers between devices, refined(): slots[n] = lax.all_to_all(slots[n], DOM, 0, 0, tiled=True)  39.4 us
    ppermute x21, waiting for transfers between devices, over_band(): lax.ppermute(piece, BAND, band_pairs(q, l))  26.3 us
    all_to_all x1, blocking collectives, summed_over_all(): lax.all_to_all(half.reshape(chips, -1, 128), CHIPS, 0, 0, tiled=True)  22.1 us
    all_to_all x2, starting transfers between devices, refined(): slots[n] = lax.all_to_all(slots[n], DOM, 0, 0, tiled=True)  9.63 us
    pallas_call x1, Pallas kernels, product_of_cells(): pl.pallas_call(product_kernel, out_shape=[sized(lanes, F32)] * 2, in_spec...  7.38 us
    pallas_call x2, Pallas kernels, slots_for_owners(): pl.pallas_call(functools.partial(slots_kernel, parts), out_shape=sized((d...  7.13 us
    pallas_call x1, Pallas kernels, predict(): pl.pallas_call(functools.partial(predict_kernel, old), out_shape=sized((8...  6.99 us
  transfers between devices with their start and end apart: 29, of which 16 were waited for; matrix products, arithmetic and copies ran while one was open for 1% of the time, Pallas kernels for 7%

profile of v2, /device:TPU:1, one launch (start us, length us, event | category | flops | bytes accessed | tf_op | source)
XLA Modules:
  0.0 192.6 jit_solution(8046195091440577925)
XLA Ops:
  0.0 0.6 pad_add_fusion.at
  0.6 3.1 %cells_for_band.1 = (bf16[2,2,64,512]{3,2,1,0:T(8,128)(2,1)}, bf16[2,2,64,512]{3,2,1,0:T(8,128)(2,1)}, bf16[2,2,64,512]{3,2,1,0:T(8,128)(2,1)}, bf16[2,2,64,512]...) custom-call(s32[4]{0:T(128)} %pad_add_fusion.at, ...), custom_call_target="tpu_custom_call" | custom-call | bytes 3670016 | tf_op jit(solution)/shard_map/cells_for_band/pallas_call | solution.py:83
  3.7 2.2 %collective-permute-start.14 = (bf16[2,2,64,512]{3,2,1,0:T(8,128)(2,1)}, bf16[2,2,64,512]{3,2,1,0:T(8,128)(2,1)S(1)}, u32[]{:S(2)}, u32[]{:S(2)}) collective-permute-start(bf16[2,2,64,512]{3,2,1,0:T(8,128)(2,1)} %get-tuple-element.42), channel_id=1, source_target_pairs={{0,2},{1,3},{2,4},{3,5},{4,6},{5,7},{6,0},{7,1},{8,10},{9,11},{10,... | collective-permute-start | bytes 786440 | tf_op jit(solution)/shard_map/ppermute | solution.py:43
  5.9 1.5 collective-permute-start.15
  7.4 1.6 collective-permute-start.16
  9.0 1.8 collective-permute-start.17
  10.8 1.2 collective-permute-start.18
  12.0 1.5 collective-permute-done.14.refs_0_
  13.5 9.6 %collective-permute-start.19 = (bf16[2,2,64,512]{3,2,1,0:T(8,128)(2,1)}, bf16[2,2,64,512]{3,2,1,0:T(8,128)(2,1)}, u32[]{:S(2)}, u32[]{:S(2)}) collective-permute-start(bf16[2,2,64,512]{3,2,1,0:T(8,128)(2,1)} %get-tuple-element.47), channel_id=1, source_target_pairs={{0,5},{1,4},{2,7},{3,6},{4,1},{5,0},{6,3},{7,2},{8,13},{9,12},{10,... | collective-permute-start | bytes 786440 | tf_op jit(solution)/shard_map/ppermute | solution.py:43
  23.1 0.0 collective-permute-done.15.refs_1_
  23.1 0.7 copy-done.1
  23.8 0.8 copy.6
  24.6 0.7 reshape.29.octants
  25.3 0.0 collective-permute-done.16.refs_2_
  25.3 0.4 collective-permute-done.17.refs_3_
  25.7 1.6 collective-permute-done.18.refs_4_
  27.2 5.1 %collective-permute-done.19.refs_5_ = bf16[2,2,64,512]{3,2,1,0:T(8,128)(2,1)} collective-permute-done((bf16[2,2,64,512]{3,2,1,0:T(8,128)(2,1)}, bf16[2,2,64,512]{3,2,1,0:T(8,128)(2,1)}, u32[]{:S(2)}, u32[]{:S(2)}) %collective-permute-start.19) | collective-permute-done | bytes 262176 | tf_op jit(solution)/shard_map/ppermute | solution.py:43
  32.3 0.0 collective-permute-done.20.refs_6_
  32.3 7.4 %product_of_cells.1 = (f32[4,256,128]{2,1,0:T(8,128)}, f32[4,256,128]{2,1,0:T(8,128)}) custom-call(s32[4]{0:T(128)} %pad_add_fusion.at, s32[512]{0:T(512)} %reshape.29.octants, bf16[16,64,512]{2,1,0:T(8,128)(2,1)} %now.3, bf16[16,64,512]{2,1,0:T(8,128)(2,1)} %prev.3, bf16[2,2,64,512]{3,2,1,0:T(8,128)(2,1)} %copy-done, bf16[2,2,64,512]{3,2,1,0:T(8,128)(2,1)} %copy-done.1, ...), custom_call_target="tpu_custom_call" | custom-call | flops 3221225472 | bytes 5242880 | tf_op jit(solution)/shard_map/product_of_cells/pallas_call | solution.py:164
  39.7 0.1 collective-permute-start.21
  39.8 2.1 %collective-permute-done.21 = f32[4,256,128]{2,1,0:T(8,128)S(1)} collective-permute-done((f32[4,256,128]{2,1,0:T(8,128)}, f32[4,256,128]{2,1,0:T(8,128)S(1)}, u32[]{:S(2)}, u32[]{:S(2)}) %collective-permute-start.21) | collective-permute-done | bytes 524320 | tf_op jit(solution)/shard_map/ppermute | solution.py:186
  41.9 1.1 add.3
  43.0 22.1 %all_to_all.20 = f32[64,16,128]{2,1,0:T(8,128)S(1)} all-to-all(f32[64,16,128]{2,1,0:T(8,128)S(1)} %bitcast.15), channel_id=1, replica_groups=mesh['dom_0'=4,'dom_1'=4,'band_0'=4,'band_1'=2] {'dom_0','dom_1','band_0'}, dimensions={0} | all-to-all | bytes 1048576 | tf_op jit(solution)/shard_map/all_to_all | solution.py:188
  65.1 0.1 reduce_sum.9
  65.2 1.8 collective-permute-start.22
  67.0 0.8 collective-permute-done.22
  67.8 0.7 broadcast_in_dim.2
  68.5 4.2 %all-to-all-start.3 = ((bf16[16,2,16,128]{3,2,1,0:T(8,128)(2,1)}), bf16[16,2,16,128]{3,2,1,0:T(8,128)(2,1)}, u32[]{:S(2)}, u32[]{:S(2)}) async-start(bf16[16,2,16,128]{3,2,1,0:T(8,128)(2,1)} %broadcast_in_dim.2), calls=%async_computation.3 | async-start | bytes 262144 | tf_op jit(solution)/shard_map/all_to_all | solution.py:192
  72.7 3.6 %shard_map.57 = bf16[16,4,2,16,512]{4,3,2,1,0:T(8,128)(2,1)} custom-call(s32[256]{0:T(256)} %owners.5, s32[512]{0:T(512)} %reshape.29.octants, bf16[16,4,16,512]{3,2,1,0:T(8,128)(2,1)} %bitcast.11, bf16[16,4,16,512]{3,2,1,0:T(8,128)(2,1)} %bitcast.13), custom_call_target="tpu_custom_call" | custom-call | bytes 4194304 | tf_op jit(solution)/shard_map/pallas_call | solution.py:247
  76.3 3.2 %all-to-all-done.3 = bf16[16,2,16,128]{3,2,1,0:T(8,128)(2,1)} async-done(((bf16[16,2,16,128]{3,2,1,0:T(8,128)(2,1)}), bf16[16,2,16,128]{3,2,1,0:T(8,128)(2,1)}, u32[]{:S(2)}, u32[]{:S(2)}) %all-to-all-start.3) | async-done | bytes 131104 | tf_op jit(solution)/shard_map/all_to_all | solution.py:192
  79.5 4.4 %all-to-all-start.1 = ((bf16[16,4,2,16,512]{4,3,2,1,0:T(8,128)(2,1)}), bf16[16,4,2,16,512]{4,3,2,1,0:T(8,128)(2,1)}, u32[]{:S(2)}, u32[]{:S(2)}) async-start(bf16[16,4,2,16,512]{4,3,2,1,0:T(8,128)(2,1)} %shard_map.57), calls=%async_computation.1 | async-start | bytes 4194304 | tf_op jit(solution)/shard_map/all_to_all | solution.py:417
  83.9 3.5 %shard_map.55 = bf16[16,4,2,16,512]{4,3,2,1,0:T(8,128)(2,1)} custom-call(s32[256]{0:T(256)} %owners.5, s32[256]{0:T(256)} %owners.5, bf16[16,4,16,512]{3,2,1,0:T(8,128)(2,1)} %bitcast.12, bf16[16,4,16,512]{3,2,1,0:T(8,128)(2,1)} %bitcast.14), custom_call_target="tpu_custom_call" | custom-call | bytes 4194304 | tf_op jit(solution)/shard_map/pallas_call | solution.py:247
  87.5 25.6 %all-to-all-done.1.slots.refs_8_ = bf16[16,4,2,16,512]{4,3,2,1,0:T(8,128)(2,1)} async-done(((bf16[16,4,2,16,512]{4,3,2,1,0:T(8,128)(2,1)}), bf16[16,4,2,16,512]{4,3,2,1,0:T(8,128)(2,1)}, u32[]{:S(2)}, u32[]{:S(2)}) %all-to-all-start.1) | async-done | bytes 2097184 | tf_op jit(solution)/shard_map/all_to_all | solution.py:417
  113.1 5.2 %all-to-all-start = ((bf16[16,4,2,16,512]{4,3,2,1,0:T(8,128)(2,1)}), bf16[16,4,2,16,512]{4,3,2,1,0:T(8,128)(2,1)}, u32[]{:S(2)}, u32[]{:S(2)}) async-start(bf16[16,4,2,16,512]{4,3,2,1,0:T(8,128)(2,1)} %shard_map.55), calls=%async_computation | async-start | bytes 4194304 | tf_op jit(solution)/shard_map/all_to_all | solution.py:417
  118.3 0.4 collective-permute-start.25
  118.7 1.8 collective-permute-start.24
  120.5 3.0 %shard_map.58 = (bf16[2,4,2,16,512]{4,3,2,1,0:T(8,128)(2,1)}, bf16[2,4,2,16,512]{4,3,2,1,0:T(8,128)(2,1)}, bf16[2,4,2,16,512]{4,3,2,1,0:T(8,128)(2,1)}, bf16[2,4...) custom-call(s32[4]{0:T(128)} %pad_add_fusion.at, ...), custom_call_target="tpu_custom_call" | custom-call | bytes 3670016 | tf_op jit(solution)/shard_map/pallas_call | solution.py:284
  123.5 0.1 collective-permute-start.7
  123.6 2.7 %collective-permute-start.8 = (bf16[2,4,2,16,512]{4,3,2,1,0:T(8,128)(2,1)}, bf16[2,4,2,16,512]{4,3,2,1,0:T(8,128)(2,1)}, u32[]{:S(2)}, u32[]{:S(2)}) collective-permute-start(bf16[2,4,2,16,512]{4,3,2,1,0:T(8,128)(2,1)} %get-tuple-element.36), channel_id=1, source_target_pairs={{0,6},{1,7},{2,0},{3,1},{4,2},{5,3},{6,4},{7,5},{8,14},{9,15},{10,... | collective-permute-start | bytes 786440 | tf_op jit(solution)/shard_map/ppermute | solution.py:43
  126.3 0.2 collective-permute-start.9
  126.5 4.1 %collective-permute-start.10 = (bf16[2,4,2,16,512]{4,3,2,1,0:T(8,128)(2,1)}, bf16[2,4,2,16,512]{4,3,2,1,0:T(8,128)(2,1)}, u32[]{:S(2)}, u32[]{:S(2)}) collective-permute-start(bf16[2,4,2,16,512]{4,3,2,1,0:T(8,128)(2,1)} %get-tuple-element.38), channel_id=1, source_target_pairs={{0,3},{1,2},{2,5},{3,4},{4,7},{5,6},{6,1},{7,0},{8,11},{9,10},{10,... | collective-permute-start | bytes 786440 | tf_op jit(solution)/shard_map/ppermute | solution.py:43
  130.6 1.6 collective-permute-start.23
  132.2 13.8 %all-to-all-done.slots.refs_0_ = bf16[16,4,2,16,512]{4,3,2,1,0:T(8,128)(2,1)} async-done(((bf16[16,4,2,16,512]{4,3,2,1,0:T(8,128)(2,1)}), bf16[16,4,2,16,512]{4,3,2,1,0:T(8,128)(2,1)}, u32[]{:S(2)}, u32[]{:S(2)}) %all-to-all-start) | async-done | bytes 2097184 | tf_op jit(solution)/shard_map/all_to_all | solution.py:417
  146.0 2.9 %shard_map.56 = (bf16[2,4,2,16,512]{4,3,2,1,0:T(8,128)(2,1)}, bf16[2,4,2,16,512]{4,3,2,1,0:T(8,128)(2,1)}, bf16[2,4,2,16,512]{4,3,2,1,0:T(8,128)(2,1)}, bf16[2,4...) custom-call(s32[4]{0:T(128)} %pad_add_fusion.at, ...), custom_call_target="tpu_custom_call" | custom-call | bytes 3670016 | tf_op jit(solution)/shard_map/pallas_call | solution.py:284
  149.0 0.0 collective-permute-done.23.refs_17_
  149.0 4.3 %collective-permute-start.11 = (bf16[2,4,2,16,512]{4,3,2,1,0:T(8,128)(2,1)}, bf16[2,4,2,16,512]{4,3,2,1,0:T(8,128)(2,1)}, u32[]{:S(2)}, u32[]{:S(2)}) collective-permute-start(bf16[2,4,2,16,512]{4,3,2,1,0:T(8,128)(2,1)} %get-tuple-element.39), channel_id=1, source_target_pairs={{0,7},{1,6},{2,1},{3,0},{4,3},{5,2},{6,5},{7,4},{8,15},{9,14},{10,... | collective-permute-start | bytes 786440 | tf_op jit(solution)/shard_map/ppermute | solution.py:43
  153.3 0.4 collective-permute-start.12
  153.7 1.8 collective-permute-start.13
  155.5 0.0 collective-permute-done.9.refs_11_
  155.5 0.0 collective-permute-start
  155.5 2.7 %collective-permute-start.1 = (bf16[2,4,2,16,512]{4,3,2,1,0:T(8,128)(2,1)}, bf16[2,4,2,16,512]{4,3,2,1,0:T(8,128)(2,1)}, u32[]{:S(2)}, u32[]{:S(2)}) collective-permute-start(bf16[2,4,2,16,512]{4,3,2,1,0:T(8,128)(2,1)} %get-tuple-element.29), channel_id=1, source_target_pairs={{0,6},{1,7},{2,0},{3,1},{4,2},{5,3},{6,4},{7,5},{8,14},{9,15},{10,... | collective-permute-start | bytes 786440 | tf_op jit(solution)/shard_map/ppermute | solution.py:43
  158.2 2.0 %collective-permute-done.11.refs_13_ = bf16[2,4,2,16,512]{4,3,2,1,0:T(8,128)(2,1)} collective-permute-done((bf16[2,4,2,16,512]{4,3,2,1,0:T(8,128)(2,1)}, bf16[2,4,2,16,512]{4,3,2,1,0:T(8,128)(2,1)}, u32[]{:S(2)}, u32[]{:S(2)}) %collective-permute-start.11) | collective-permute-done | bytes 262176 | tf_op jit(solution)/shard_map/ppermute | solution.py:43
  160.2 1.5 collective-permute-start.2
  161.7 2.1 %collective-permute-done.12.refs_14_ = bf16[2,4,2,16,512]{4,3,2,1,0:T(8,128)(2,1)} collective-permute-done((bf16[2,4,2,16,512]{4,3,2,1,0:T(8,128)(2,1)}, bf16[2,4,2,16,512]{4,3,2,1,0:T(8,128)(2,1)}, u32[]{:S(2)}, u32[]{:S(2)}) %collective-permute-start.12) | collective-permute-done | bytes 262176 | tf_op jit(solution)/shard_map/ppermute | solution.py:43
  163.8 3.8 %collective-permute-start.3 = (bf16[2,4,2,16,512]{4,3,2,1,0:T(8,128)(2,1)}, bf16[2,4,2,16,512]{4,3,2,1,0:T(8,128)(2,1)}, u32[]{:S(2)}, u32[]{:S(2)}) collective-permute-start(bf16[2,4,2,16,512]{4,3,2,1,0:T(8,128)(2,1)} %get-tuple-element.31), channel_id=1, source_target_pairs={{0,3},{1,2},{2,5},{3,4},{4,7},{5,6},{6,1},{7,0},{8,11},{9,10},{10,... | collective-permute-start | bytes 786440 | tf_op jit(solution)/shard_map/ppermute | solution.py:43
  167.6 2.4 %collective-permute-start.4 = (bf16[2,4,2,16,512]{4,3,2,1,0:T(8,128)(2,1)}, bf16[2,4,2,16,512]{4,3,2,1,0:T(8,128)(2,1)}, u32[]{:S(2)}, u32[]{:S(2)}) collective-permute-start(bf16[2,4,2,16,512]{4,3,2,1,0:T(8,128)(2,1)} %get-tuple-element.32), channel_id=1, source_target_pairs={{0,7},{1,6},{2,1},{3,0},{4,3},{5,2},{6,5},{7,4},{8,15},{9,14},{10,... | collective-permute-start | bytes 786440 | tf_op jit(solution)/shard_map/ppermute | solution.py:43
  169.9 0.0 collective-permute-done.refs_1_
  169.9 1.8 collective-permute-start.5
  171.8 1.1 collective-permute-done.1.refs_2_
  172.9 0.8 collective-permute-done.2.refs_3_
  173.7 7.1 %collective-permute-done.3.refs_4_ = bf16[2,4,2,16,512]{4,3,2,1,0:T(8,128)(2,1)} collective-permute-done((bf16[2,4,2,16,512]{4,3,2,1,0:T(8,128)(2,1)}, bf16[2,4,2,16,512]{4,3,2,1,0:T(8,128)(2,1)}, u32[]{:S(2)}, u32[]{:S(2)}) %collective-permute-start.3) | collective-permute-done | bytes 262176 | tf_op jit(solution)/shard_map/ppermute | solution.py:43
  180.8 1.8 collective-permute-done.4.refs_5_
  182.6 2.8 %collective-permute-done.5.refs_6_ = bf16[2,4,2,16,512]{4,3,2,1,0:T(8,128)(2,1)} collective-permute-done((bf16[2,4,2,16,512]{4,3,2,1,0:T(8,128)(2,1)}, bf16[2,4,2,16,512]{4,3,2,1,0:T(8,128)(2,1)}, u32[]{:S(2)}, u32[]{:S(2)}) %collective-permute-start.5) | collective-permute-done | bytes 262176 | tf_op jit(solution)/shard_map/ppermute | solution.py:43
  185.5 7.0 %predict.1 = bf16[8,512,512]{2,1,0:T(8,128)(2,1)} custom-call(s32[4]{0:T(128)} %pad_add_fusion.at, s32[256]{0:T(256)} %owners.5, s32[512]{0:T(512)} %reshape.29.octants, bf16[16,4,2,16,512]{4,3,2,1,0:T(8,128)(2,1)} %all-to-all-done.slots.refs_0_, bf16[2,4,2,16,512]{4,3,2,1,0:T(8,128)(2,1)} %collective-permute-done.refs_1_, ...), custom_call_target="tpu_custom_call" | custom-call | flops 3221225472 | bytes 13631488 | tf_op jit(solution)/shard_map/predict/pallas_call | solution.py:381
  (15 shorter events, 0.0 us)
Async XLA Ops:
  3.7 9.7 %collective-permute-start.14 = (bf16[2,2,64,512]{3,2,1,0:T(8,128)(2,1)}, bf16[2,2,64,512]{3,2,1,0:T(8,128)(2,1)S(1)}, u32[]{:S(2)}, u32[]{:S(2)}) collective-permute-start(bf16[2,2,64,512]{3,2,1,0:T(8,128)(2,1)} %get-tuple-element.42), channel_id=1, source_target_pairs={{0,2},{1,3},{2,4},{3,5},{4,6},{5,7},{6,0},{7,1},{8,10},{9,11},{10,... | collective-permute-start | bytes 786440 | tf_op jit(solution)/shard_map/ppermute | solution.py:43
  5.9 17.2 %collective-permute-start.15 = (bf16[2,2,64,512]{3,2,1,0:T(8,128)(2,1)}, bf16[2,2,64,512]{3,2,1,0:T(8,128)(2,1)S(1)}, u32[]{:S(2)}, u32[]{:S(2)}) collective-permute-start(bf16[2,2,64,512]{3,2,1,0:T(8,128)(2,1)} %get-tuple-element.43), channel_id=1, source_target_pairs={{0,6},{1,7},{2,0},{3,1},{4,2},{5,3},{6,4},{7,5},{8,14},{9,15},{10,... | collective-permute-start | bytes 786440 | tf_op jit(solution)/shard_map/ppermute | solution.py:43
  7.4 17.9 %collective-permute-start.16 = (bf16[2,2,64,512]{3,2,1,0:T(8,128)(2,1)}, bf16[2,2,64,512]{3,2,1,0:T(8,128)(2,1)}, u32[]{:S(2)}, u32[]{:S(2)}) collective-permute-start(bf16[2,2,64,512]{3,2,1,0:T(8,128)(2,1)} %get-tuple-element.44), channel_id=1, source_target_pairs={{0,4},{1,5},{2,6},{3,7},{4,0},{5,1},{6,2},{7,3},{8,12},{9,13},{10,... | collective-permute-start | bytes 786440 | tf_op jit(solution)/shard_map/ppermute | solution.py:43
  9.0 16.7 %collective-permute-start.17 = (bf16[2,2,64,512]{3,2,1,0:T(8,128)(2,1)}, bf16[2,2,64,512]{3,2,1,0:T(8,128)(2,1)}, u32[]{:S(2)}, u32[]{:S(2)}) collective-permute-start(bf16[2,2,64,512]{3,2,1,0:T(8,128)(2,1)} %get-tuple-element.45), channel_id=1, source_target_pairs={{0,3},{1,2},{2,5},{3,4},{4,7},{5,6},{6,1},{7,0},{8,11},{9,10},{10,... | collective-permute-start | bytes 786440 | tf_op jit(solution)/shard_map/ppermute | solution.py:43
  10.8 16.4 %collective-permute-start.18 = (bf16[2,2,64,512]{3,2,1,0:T(8,128)(2,1)}, bf16[2,2,64,512]{3,2,1,0:T(8,128)(2,1)}, u32[]{:S(2)}, u32[]{:S(2)}) collective-permute-start(bf16[2,2,64,512]{3,2,1,0:T(8,128)(2,1)} %get-tuple-element.46), channel_id=1, source_target_pairs={{0,7},{1,6},{2,1},{3,0},{4,3},{5,2},{6,5},{7,4},{8,15},{9,14},{10,... | collective-permute-start | bytes 786440 | tf_op jit(solution)/shard_map/ppermute | solution.py:43
  13.5 9.6 %copy-start = (bf16[2,2,64,512]{3,2,1,0:T(8,128)(2,1)}, bf16[2,2,64,512]{3,2,1,0:T(8,128)(2,1)S(1)}, u32[]{:S(2)}) copy-start(bf16[2,2,64,512]{3,2,1,0:T(8,128)(2,1)S(1)} %collective-permute-done.14.refs_0_) | copy-start | bytes 786436
  13.5 18.8 %collective-permute-start.19 = (bf16[2,2,64,512]{3,2,1,0:T(8,128)(2,1)}, bf16[2,2,64,512]{3,2,1,0:T(8,128)(2,1)}, u32[]{:S(2)}, u32[]{:S(2)}) collective-permute-start(bf16[2,2,64,512]{3,2,1,0:T(8,128)(2,1)} %get-tuple-element.47), channel_id=1, source_target_pairs={{0,5},{1,4},{2,7},{3,6},{4,1},{5,0},{6,3},{7,2},{8,13},{9,12},{10,... | collective-permute-start | bytes 786440 | tf_op jit(solution)/shard_map/ppermute | solution.py:43
  23.1 0.7 copy-start.1
  23.8 8.5 %collective-permute-start.20 = (bf16[2,2,64,512]{3,2,1,0:T(8,128)(2,1)}, bf16[2,2,64,512]{3,2,1,0:T(8,128)(2,1)}, u32[]{:S(2)}, u32[]{:S(2)}) collective-permute-start(bf16[2,2,64,512]{3,2,1,0:T(8,128)(2,1)} %get-tuple-element.48), channel_id=1, source_target_pairs={{0,1},{1,0},{2,3},{3,2},{4,5},{5,4},{6,7},{7,6},{8,9},{9,8},{10,11... | collective-permute-start | bytes 786440 | tf_op jit(solution)/shard_map/ppermute | solution.py:43
  39.7 2.2 %collective-permute-start.21 = (f32[4,256,128]{2,1,0:T(8,128)}, f32[4,256,128]{2,1,0:T(8,128)S(1)}, u32[]{:S(2)}, u32[]{:S(2)}) collective-permute-start(f32[4,256,128]{2,1,0:T(8,128)} %get-tuple-element.50), channel_id=1, source_target_pairs={{0,1},{1,0},{2,3},{3,2},{4,5},{5,4},{6,7},{7,6},{8,9},{9,8},{10,11... | collective-permute-start | bytes 1572872 | tf_op jit(solution)/shard_map/ppermute | solution.py:186
  65.2 2.6 %collective-permute-start.22 = (bf16[16,128]{1,0:T(8,128)(2,1)S(1)}, bf16[16,128]{1,0:T(8,128)(2,1)S(1)}, u32[]{:S(2)}, u32[]{:S(2)}) collective-permute-start(bf16[16,128]{1,0:T(8,128)(2,1)S(1)} %multiply_convert_fusion), channel_id=1, source_target_pairs={{0,1},{1,0},{2,3},{3,2},{4,5},{5,4},{6,7},{7,6},{8,9},{9,8},{10,11... | collective-permute-start | bytes 12296 | tf_op jit(solution)/shard_map/ppermute | solution.py:190
  68.5 11.0 %all-to-all-start.3 = ((bf16[16,2,16,128]{3,2,1,0:T(8,128)(2,1)}), bf16[16,2,16,128]{3,2,1,0:T(8,128)(2,1)}, u32[]{:S(2)}, u32[]{:S(2)}) async-start(bf16[16,2,16,128]{3,2,1,0:T(8,128)(2,1)} %broadcast_in_dim.2), calls=%async_computation.3 | async-start | bytes 262144 | tf_op jit(solution)/shard_map/all_to_all | solution.py:192
  79.5 33.6 %all-to-all-start.1 = ((bf16[16,4,2,16,512]{4,3,2,1,0:T(8,128)(2,1)}), bf16[16,4,2,16,512]{4,3,2,1,0:T(8,128)(2,1)}, u32[]{:S(2)}, u32[]{:S(2)}) async-start(bf16[16,4,2,16,512]{4,3,2,1,0:T(8,128)(2,1)} %shard_map.57), calls=%async_computation.1 | async-start | bytes 4194304 | tf_op jit(solution)/shard_map/all_to_all | solution.py:417
  113.1 32.9 %all-to-all-start = ((bf16[16,4,2,16,512]{4,3,2,1,0:T(8,128)(2,1)}), bf16[16,4,2,16,512]{4,3,2,1,0:T(8,128)(2,1)}, u32[]{:S(2)}, u32[]{:S(2)}) async-start(bf16[16,4,2,16,512]{4,3,2,1,0:T(8,128)(2,1)} %shard_map.55), calls=%async_computation | async-start | bytes 4194304 | tf_op jit(solution)/shard_map/all_to_all | solution.py:417
  118.3 8.2 %collective-permute-start.25 = (bf16[4,4,2,16,128]{4,3,2,1,0:T(8,128)(2,1)}, bf16[4,4,2,16,128]{4,3,2,1,0:T(8,128)(2,1)}, u32[]{:S(2)}, u32[]{:S(2)}) collective-permute-start(bf16[4,4,2,16,128]{4,3,2,1,0:T(8,128)(2,1)} %bitcast.9.refs_16_), channel_id=1, source_target_pairs={{0,6},{2,0},{4,2},{6,4},{1,7},{3,1},{5,3},{7,5},{8,14},{10,8},{12,... | collective-permute-start | bytes 393224 | tf_op jit(solution)/shard_map/ppermute | solution.py:195
  118.7 11.9 %collective-permute-start.24 = (bf16[4,4,2,16,128]{4,3,2,1,0:T(8,128)(2,1)}, bf16[4,4,2,16,128]{4,3,2,1,0:T(8,128)(2,1)}, u32[]{:S(2)}, u32[]{:S(2)}) collective-permute-start(bf16[4,4,2,16,128]{4,3,2,1,0:T(8,128)(2,1)} %bitcast.9.refs_16_), channel_id=1, source_target_pairs={{0,4},{2,6},{4,0},{6,2},{1,5},{3,7},{5,1},{7,3},{8,12},{10,14},{12... | collective-permute-start | bytes 393224 | tf_op jit(solution)/shard_map/ppermute | solution.py:195
  123.5 29.8 %collective-permute-start.7 = (bf16[2,4,2,16,512]{4,3,2,1,0:T(8,128)(2,1)}, bf16[2,4,2,16,512]{4,3,2,1,0:T(8,128)(2,1)}, u32[]{:S(2)}, u32[]{:S(2)}) collective-permute-start(bf16[2,4,2,16,512]{4,3,2,1,0:T(8,128)(2,1)} %get-tuple-element.35), channel_id=1, source_target_pairs={{0,2},{1,3},{2,4},{3,5},{4,6},{5,7},{6,0},{7,1},{8,10},{9,11},{10,... | collective-permute-start | bytes 786440 | tf_op jit(solution)/shard_map/ppermute | solution.py:43
  123.6 30.1 %collective-permute-start.8 = (bf16[2,4,2,16,512]{4,3,2,1,0:T(8,128)(2,1)}, bf16[2,4,2,16,512]{4,3,2,1,0:T(8,128)(2,1)}, u32[]{:S(2)}, u32[]{:S(2)}) collective-permute-start(bf16[2,4,2,16,512]{4,3,2,1,0:T(8,128)(2,1)} %get-tuple-element.36), channel_id=1, source_target_pairs={{0,6},{1,7},{2,0},{3,1},{4,2},{5,3},{6,4},{7,5},{8,14},{9,15},{10,... | collective-permute-start | bytes 786440 | tf_op jit(solution)/shard_map/ppermute | solution.py:43
  126.3 29.2 %collective-permute-start.9 = (bf16[2,4,2,16,512]{4,3,2,1,0:T(8,128)(2,1)}, bf16[2,4,2,16,512]{4,3,2,1,0:T(8,128)(2,1)}, u32[]{:S(2)}, u32[]{:S(2)}) collective-permute-start(bf16[2,4,2,16,512]{4,3,2,1,0:T(8,128)(2,1)} %get-tuple-element.37), channel_id=1, source_target_pairs={{0,4},{1,5},{2,6},{3,7},{4,0},{5,1},{6,2},{7,3},{8,12},{9,13},{10,... | collective-permute-start | bytes 786440 | tf_op jit(solution)/shard_map/ppermute | solution.py:43
  126.5 29.0 %collective-permute-start.10 = (bf16[2,4,2,16,512]{4,3,2,1,0:T(8,128)(2,1)}, bf16[2,4,2,16,512]{4,3,2,1,0:T(8,128)(2,1)}, u32[]{:S(2)}, u32[]{:S(2)}) collective-permute-start(bf16[2,4,2,16,512]{4,3,2,1,0:T(8,128)(2,1)} %get-tuple-element.38), channel_id=1, source_target_pairs={{0,3},{1,2},{2,5},{3,4},{4,7},{5,6},{6,1},{7,0},{8,11},{9,10},{10,... | collective-permute-start | bytes 786440 | tf_op jit(solution)/shard_map/ppermute | solution.py:43
  130.6 18.4 %collective-permute-start.23 = (bf16[4,4,2,16,128]{4,3,2,1,0:T(8,128)(2,1)}, bf16[4,4,2,16,128]{4,3,2,1,0:T(8,128)(2,1)}, u32[]{:S(2)}, u32[]{:S(2)}) collective-permute-start(bf16[4,4,2,16,128]{4,3,2,1,0:T(8,128)(2,1)} %bitcast.9.refs_16_), channel_id=1, source_target_pairs={{0,2},{2,4},{4,6},{6,0},{1,3},{3,5},{5,7},{7,1},{8,10},{10,12},{12... | collective-permute-start | bytes 393224 | tf_op jit(solution)/shard_map/ppermute | solution.py:195
  149.0 11.2 %collective-permute-start.11 = (bf16[2,4,2,16,512]{4,3,2,1,0:T(8,128)(2,1)}, bf16[2,4,2,16,512]{4,3,2,1,0:T(8,128)(2,1)}, u32[]{:S(2)}, u32[]{:S(2)}) collective-permute-start(bf16[2,4,2,16,512]{4,3,2,1,0:T(8,128)(2,1)} %get-tuple-element.39), channel_id=1, source_target_pairs={{0,7},{1,6},{2,1},{3,0},{4,3},{5,2},{6,5},{7,4},{8,15},{9,14},{10,... | collective-permute-start | bytes 786440 | tf_op jit(solution)/shard_map/ppermute | solution.py:43
  153.3 10.5 %collective-permute-start.12 = (bf16[2,4,2,16,512]{4,3,2,1,0:T(8,128)(2,1)}, bf16[2,4,2,16,512]{4,3,2,1,0:T(8,128)(2,1)}, u32[]{:S(2)}, u32[]{:S(2)}) collective-permute-start(bf16[2,4,2,16,512]{4,3,2,1,0:T(8,128)(2,1)} %get-tuple-element.40), channel_id=1, source_target_pairs={{0,5},{1,4},{2,7},{3,6},{4,1},{5,0},{6,3},{7,2},{8,13},{9,12},{10,... | collective-permute-start | bytes 786440 | tf_op jit(solution)/shard_map/ppermute | solution.py:43
  153.7 13.9 %collective-permute-start.13 = (bf16[2,4,2,16,512]{4,3,2,1,0:T(8,128)(2,1)}, bf16[2,4,2,16,512]{4,3,2,1,0:T(8,128)(2,1)}, u32[]{:S(2)}, u32[]{:S(2)}) collective-permute-start(bf16[2,4,2,16,512]{4,3,2,1,0:T(8,128)(2,1)} %get-tuple-element.41), channel_id=1, source_target_pairs={{0,1},{1,0},{2,3},{3,2},{4,5},{5,4},{6,7},{7,6},{8,9},{9,8},{10,11... | collective-permute-start | bytes 786440 | tf_op jit(solution)/shard_map/ppermute | solution.py:43
  155.5 14.4 %collective-permute-start = (bf16[2,4,2,16,512]{4,3,2,1,0:T(8,128)(2,1)}, bf16[2,4,2,16,512]{4,3,2,1,0:T(8,128)(2,1)}, u32[]{:S(2)}, u32[]{:S(2)}) collective-permute-start(bf16[2,4,2,16,512]{4,3,2,1,0:T(8,128)(2,1)} %get-tuple-element.28), channel_id=1, source_target_pairs={{0,2},{1,3},{2,4},{3,5},{4,6},{5,7},{6,0},{7,1},{8,10},{9,11},{10,... | collective-permute-start | bytes 786440 | tf_op jit(solution)/shard_map/ppermute | solution.py:43
  155.5 17.3 %collective-permute-start.1 = (bf16[2,4,2,16,512]{4,3,2,1,0:T(8,128)(2,1)}, bf16[2,4,2,16,512]{4,3,2,1,0:T(8,128)(2,1)}, u32[]{:S(2)}, u32[]{:S(2)}) collective-permute-start(bf16[2,4,2,16,512]{4,3,2,1,0:T(8,128)(2,1)} %get-tuple-element.29), channel_id=1, source_target_pairs={{0,6},{1,7},{2,0},{3,1},{4,2},{5,3},{6,4},{7,5},{8,14},{9,15},{10,... | collective-permute-start | bytes 786440 | tf_op jit(solution)/shard_map/ppermute | solution.py:43
  160.2 13.5 %collective-permute-start.2 = (bf16[2,4,2,16,512]{4,3,2,1,0:T(8,128)(2,1)}, bf16[2,4,2,16,512]{4,3,2,1,0:T(8,128)(2,1)}, u32[]{:S(2)}, u32[]{:S(2)}) collective-permute-start(bf16[2,4,2,16,512]{4,3,2,1,0:T(8,128)(2,1)} %get-tuple-element.30), channel_id=1, source_target_pairs={{0,4},{1,5},{2,6},{3,7},{4,0},{5,1},{6,2},{7,3},{8,12},{9,13},{10,... | collective-permute-start | bytes 786440 | tf_op jit(solution)/shard_map/ppermute | solution.py:43
  163.8 17.0 %collective-permute-start.3 = (bf16[2,4,2,16,512]{4,3,2,1,0:T(8,128)(2,1)}, bf16[2,4,2,16,512]{4,3,2,1,0:T(8,128)(2,1)}, u32[]{:S(2)}, u32[]{:S(2)}) collective-permute-start(bf16[2,4,2,16,512]{4,3,2,1,0:T(8,128)(2,1)} %get-tuple-element.31), channel_id=1, source_target_pairs={{0,3},{1,2},{2,5},{3,4},{4,7},{5,6},{6,1},{7,0},{8,11},{9,10},{10,... | collective-permute-start | bytes 786440 | tf_op jit(solution)/shard_map/ppermute | solution.py:43
  167.6 15.1 %collective-permute-start.4 = (bf16[2,4,2,16,512]{4,3,2,1,0:T(8,128)(2,1)}, bf16[2,4,2,16,512]{4,3,2,1,0:T(8,128)(2,1)}, u32[]{:S(2)}, u32[]{:S(2)}) collective-permute-start(bf16[2,4,2,16,512]{4,3,2,1,0:T(8,128)(2,1)} %get-tuple-element.32), channel_id=1, source_target_pairs={{0,7},{1,6},{2,1},{3,0},{4,3},{5,2},{6,5},{7,4},{8,15},{9,14},{10,... | collective-permute-start | bytes 786440 | tf_op jit(solution)/shard_map/ppermute | solution.py:43
  169.9 15.5 %collective-permute-start.5 = (bf16[2,4,2,16,512]{4,3,2,1,0:T(8,128)(2,1)}, bf16[2,4,2,16,512]{4,3,2,1,0:T(8,128)(2,1)}, u32[]{:S(2)}, u32[]{:S(2)}) collective-permute-start(bf16[2,4,2,16,512]{4,3,2,1,0:T(8,128)(2,1)} %get-tuple-element.33), channel_id=1, source_target_pairs={{0,5},{1,4},{2,7},{3,6},{4,1},{5,0},{6,3},{7,2},{8,13},{9,12},{10,... | collective-permute-start | bytes 786440 | tf_op jit(solution)/shard_map/ppermute | solution.py:43
  172.9 12.6 %collective-permute-start.6 = (bf16[2,4,2,16,512]{4,3,2,1,0:T(8,128)(2,1)}, bf16[2,4,2,16,512]{4,3,2,1,0:T(8,128)(2,1)}, u32[]{:S(2)}, u32[]{:S(2)}) collective-permute-start(bf16[2,4,2,16,512]{4,3,2,1,0:T(8,128)(2,1)} %get-tuple-element.34), channel_id=1, source_target_pairs={{0,1},{1,0},{2,3},{3,2},{4,5},{5,4},{6,7},{7,6},{8,9},{9,8},{10,11... | collective-permute-start | bytes 786440 | tf_op jit(solution)/shard_map/ppermute | solution.py:43

commit v3 on v2

--- a/solution.py
+++ b/solution.py
@@ -21,7 +21,7 @@
 RING = 4
 CORES = 2
 UNIT = 16
-OFFSETS = ((0, 0), (1, 0), (3, 0), (2, 0), (1, 1), (3, 1), (2, 1), (0, 1))
+OFFSETS = ((0, 0), (1, 1), (3, 1), (2, 1), (1, 0), (3, 0), (2, 0), (0, 1))
 
 
 WHOLE_VMEM = pltpu.CompilerParams(vmem_limit_bytes=67_043_328)
@@ -229,7 +229,7 @@
                 stores.append(
                     pltpu.make_async_copy(
                         cells.at[a, slot[rank * doms + d], pl.ds(begin, units)],
-                        out.at[d, pl.ds(at_unit, units), a],
+                        out.at[d % RING, d // RING, pl.ds(at_unit, units), a],
                         out_sem.at[n, a, d],
                     )
                 )
@@ -246,7 +246,7 @@
     size = 2 * doms * total * UNIT * nodes * 2
     return pl.pallas_call(
         functools.partial(slots_kernel, parts),
-        out_shape=sized((doms, total, 2, UNIT, nodes)),
+        out_shape=sized((RING, RING, total, 2, UNIT, nodes)),
         in_specs=[SMEM, SMEM, HBM, HBM],
         out_specs=HBM,
         scratch_shapes=[
@@ -266,8 +266,8 @@
     y, c = at[2], at[3]
     loads, stores = [], []
     for n, (q, l) in enumerate(OFFSETS[1:]):
-        first = (((y + q) & 3) * CORES + ((c + l) & 1)) * 2
-        loads.append(pltpu.make_async_copy(slots.at[pl.ds(first, 2)], buf.at[n], in_sem.at[n]))
+        src = slots.at[pl.ds(((c + l) & 1) * 2, 2), (y + q) & 3]
+        loads.append(pltpu.make_async_copy(src, buf.at[n], in_sem.at[n]))
         stores.append(pltpu.make_async_copy(buf.at[n], outs[n], out_sem.at[n]))
     for load in loads:
         load.start()
@@ -279,7 +279,7 @@
 
 
 def routed(at, slots):
-    piece = (2, *slots.shape[1:])
+    piece = (2, *slots.shape[2:])
     size = 7 * math.prod(piece) * 2
     return pl.pallas_call(
         route_kernel,
@@ -328,7 +328,7 @@
         copies = []
         for n, (q, l) in enumerate(OFFSETS):
             b = ((y - q) & 3) * CORES + ((c - l) & 1)
-            src = pieces[rank][n - 1].at[e] if n else slots[rank].at[b * 2 + e]
+            src = pieces[rank][n - 1].at[e] if n else slots[rank].at[c * 2 + e, y]
             to = parents.at[k, pl.ds(b * units, units)]
             copies.append(pltpu.make_async_copy(src, to, in_sem.at[k, n]))
         for j in range(2):
@@ -376,7 +376,7 @@
 
 def predict(old, at, owners, octants, slots, pieces, tiles, interp):
     nodes = interp.shape[2]
-    units = slots[0].shape[1]
+    units = slots[0].shape[2]
     states = units * UNIT * RING * CORES
     return pl.pallas_call(
         functools.partial(predict_kernel, old),
@@ -414,7 +414,9 @@
     for n in range(2):
         table = octants if n else owner_map
         slots.append(slots_for_owners(parts[n], owner_map, table, *by_unit))
-        slots[n] = lax.all_to_all(slots[n], DOM, 0, 0, tiled=True)
+        by_owner = slots[n].reshape(RING * RING, *slots[n].shape[2:])
+        by_owner = lax.all_to_all(by_owner, (X, Z), 0, 0, tiled=True)
+        slots[n] = by_owner.reshape(slots[n].shape)
         pieces.append(routed(at, slots[n]))
         pieces[n] = over_band(pieces[n])
 

time: 195 us -> 194 us (level)
  the two profiles are of different devices: /device:TPU:1 before, /device:TPU:28 now
where the time goes in v3:
time: 194 us; the launch traced here: 193 us
  waiting for transfers between devices  86.5 us (45%)
  starting transfers between devices  48.5 us (25%)
  Pallas kernels  31.9 us (16%)
  blocking collectives  20.9 us (11%)
  local copies, waits for them, and re-layouts  2.9 us (1%)
    ppermute x21, waiting for transfers between devices, over_band(): lax.ppermute(piece, BAND, band_pairs(q, l))  44.6 us
    all_to_all x2, waiting for transfers between devices, refined(): by_owner = lax.all_to_all(by_owner, (X, Z), 0, 0, tiled=True)  36.2 us
    ppermute x21, starting transfers between devices, over_band(): lax.ppermute(piece, BAND, band_pairs(q, l))  25.1 us
    all_to_all x1, blocking collectives, summed_over_all(): lax.all_to_all(half.reshape(chips, -1, 128), CHIPS, 0, 0, tiled=True)  20.9 us
    all_to_all x2, starting transfers between devices, refined(): by_owner = lax.all_to_all(by_owner, (X, Z), 0, 0, tiled=True)  12.8 us
    pallas_call x1, Pallas kernels, predict(): pl.pallas_call(functools.partial(predict_kernel, old), out_shape=sized((8...  8.31 us
    pallas_call x1, Pallas kernels, product_of_cells(): pl.pallas_call(product_kernel, out_shape=[sized(lanes, F32)] * 2, in_spec...  7.39 us
    pallas_call x2, Pallas kernels, slots_for_owners(): pl.pallas_call(functools.partial(slots_kernel, parts), out_shape=sized((R...  7.12 us
  transfers between devices with their start and end apart: 29, of which 17 were waited for; matrix products, arithmetic and copies ran while one was open for 1% of the time, Pallas kernels for 7%

profile of v3, /device:TPU:28, one launch (start us, length us, event | category | flops | bytes accessed | tf_op | source)
XLA Modules:
  0.0 192.8 jit_solution(3754175432309969772)
XLA Ops:
  0.0 0.6 pad_add_fusion.at
  0.6 3.1 %cells_for_band.1 = (bf16[2,2,64,512]{3,2,1,0:T(8,128)(2,1)}, bf16[2,2,64,512]{3,2,1,0:T(8,128)(2,1)}, bf16[2,2,64,512]{3,2,1,0:T(8,128)(2,1)}, bf16[2,2,64,512]...) custom-call(s32[4]{0:T(128)} %pad_add_fusion.at, ...), custom_call_target="tpu_custom_call" | custom-call | bytes 3670016 | tf_op jit(solution)/shard_map/cells_for_band/pallas_call | solution.py:83
  3.7 0.1 collective-permute-start.14
  3.8 1.7 collective-permute-start.15
  5.5 0.8 collective-permute-start.16
  6.3 2.1 %collective-permute-start.17 = (bf16[2,2,64,512]{3,2,1,0:T(8,128)(2,1)}, bf16[2,2,64,512]{3,2,1,0:T(8,128)(2,1)}, u32[]{:S(2)}, u32[]{:S(2)}) collective-permute-start(bf16[2,2,64,512]{3,2,1,0:T(8,128)(2,1)} %get-tuple-element.45), channel_id=1, source_target_pairs={{0,2},{1,3},{2,4},{3,5},{4,6},{5,7},{6,0},{7,1},{8,10},{9,11},{10,... | collective-permute-start | bytes 786440 | tf_op jit(solution)/shard_map/ppermute | solution.py:43
  8.4 0.0 collective-permute-start.18
  8.4 4.2 %collective-permute-done.14.refs_0_ = bf16[2,2,64,512]{3,2,1,0:T(8,128)(2,1)S(1)} collective-permute-done((bf16[2,2,64,512]{3,2,1,0:T(8,128)(2,1)}, bf16[2,2,64,512]{3,2,1,0:T(8,128)(2,1)S(1)}, u32[]{:S(2)}, u32[]{:S(2)}) %collective-permute-start.14) | collective-permute-done | bytes 262176 | tf_op jit(solution)/shard_map/ppermute | solution.py:43
  12.6 1.2 collective-permute-start.19
  13.8 0.4 collective-permute-done.15.refs_1_
  14.2 0.7 copy-done.1
  14.9 5.6 %collective-permute-start.20 = (bf16[2,2,64,512]{3,2,1,0:T(8,128)(2,1)}, bf16[2,2,64,512]{3,2,1,0:T(8,128)(2,1)}, u32[]{:S(2)}, u32[]{:S(2)}) collective-permute-start(bf16[2,2,64,512]{3,2,1,0:T(8,128)(2,1)} %get-tuple-element.48), channel_id=1, source_target_pairs={{0,1},{1,0},{2,3},{3,2},{4,5},{5,4},{6,7},{7,6},{8,9},{9,8},{10,11... | collective-permute-start | bytes 786440 | tf_op jit(solution)/shard_map/ppermute | solution.py:43
  20.5 0.8 copy.6
  21.3 0.7 reshape.41.octants
  22.0 0.0 collective-permute-done.16.refs_2_
  22.0 2.0 %collective-permute-done.17.refs_3_ = bf16[2,2,64,512]{3,2,1,0:T(8,128)(2,1)} collective-permute-done((bf16[2,2,64,512]{3,2,1,0:T(8,128)(2,1)}, bf16[2,2,64,512]{3,2,1,0:T(8,128)(2,1)}, u32[]{:S(2)}, u32[]{:S(2)}) %collective-permute-start.17) | collective-permute-done | bytes 262176 | tf_op jit(solution)/shard_map/ppermute | solution.py:43
  24.0 6.9 %collective-permute-done.18.refs_4_ = bf16[2,2,64,512]{3,2,1,0:T(8,128)(2,1)} collective-permute-done((bf16[2,2,64,512]{3,2,1,0:T(8,128)(2,1)}, bf16[2,2,64,512]{3,2,1,0:T(8,128)(2,1)}, u32[]{:S(2)}, u32[]{:S(2)}) %collective-permute-start.18) | collective-permute-done | bytes 262176 | tf_op jit(solution)/shard_map/ppermute | solution.py:43
  30.9 0.0 collective-permute-done.19.refs_5_
  30.9 0.0 collective-permute-done.20.refs_6_
  30.9 7.4 %product_of_cells.1 = (f32[4,256,128]{2,1,0:T(8,128)}, f32[4,256,128]{2,1,0:T(8,128)}) custom-call(s32[4]{0:T(128)} %pad_add_fusion.at, s32[512]{0:T(512)} %reshape.41.octants, bf16[16,64,512]{2,1,0:T(8,128)(2,1)} %now.3, bf16[16,64,512]{2,1,0:T(8,128)(2,1)} %prev.3, bf16[2,2,64,512]{3,2,1,0:T(8,128)(2,1)} %copy-done, bf16[2,2,64,512]{3,2,1,0:T(8,128)(2,1)} %copy-done.1, ...), custom_call_target="tpu_custom_call" | custom-call | flops 3221225472 | bytes 5242880 | tf_op jit(solution)/shard_map/product_of_cells/pallas_call | solution.py:164
  38.3 0.1 collective-permute-start.21
  38.4 2.1 %collective-permute-done.21 = f32[4,256,128]{2,1,0:T(8,128)S(1)} collective-permute-done((f32[4,256,128]{2,1,0:T(8,128)}, f32[4,256,128]{2,1,0:T(8,128)S(1)}, u32[]{:S(2)}, u32[]{:S(2)}) %collective-permute-start.21) | collective-permute-done | bytes 524320 | tf_op jit(solution)/shard_map/ppermute | solution.py:186
  40.5 1.1 add.3
  41.6 20.9 %all_to_all.20 = f32[64,16,128]{2,1,0:T(8,128)S(1)} all-to-all(f32[64,16,128]{2,1,0:T(8,128)S(1)} %bitcast.21), channel_id=1, replica_groups=mesh['dom_0'=4,'dom_1'=4,'band_0'=4,'band_1'=2] {'dom_0','dom_1','band_0'}, dimensions={0} | all-to-all | bytes 1048576 | tf_op jit(solution)/shard_map/all_to_all | solution.py:188
  62.5 0.1 reduce_sum.9
  62.6 0.1 collective-permute-start.22
  62.7 1.1 collective-permute-done.22
  63.9 0.7 broadcast_in_dim.2
  64.5 5.7 %all-to-all-start.3 = ((bf16[16,2,16,128]{3,2,1,0:T(8,128)(2,1)}), bf16[16,2,16,128]{3,2,1,0:T(8,128)(2,1)}, u32[]{:S(2)}, u32[]{:S(2)}) async-start(bf16[16,2,16,128]{3,2,1,0:T(8,128)(2,1)} %broadcast_in_dim.2), calls=%async_computation.3 | async-start | bytes 262144 | tf_op jit(solution)/shard_map/all_to_all | solution.py:192
  70.2 3.6 %shard_map.57 = bf16[4,4,4,2,16,512]{5,4,3,2,1,0:T(8,128)(2,1)} custom-call(s32[256]{0:T(256)} %owners.5, s32[512]{0:T(512)} %reshape.41.octants, bf16[16,4,16,512]{3,2,1,0:T(8,128)(2,1)} %bitcast.15, bf16[16,4,16,512]{3,2,1,0:T(8,128)(2,1)} %bitcast.17), custom_call_target="tpu_custom_call" | custom-call | bytes 4194304 | tf_op jit(solution)/shard_map/pallas_call | solution.py:247
  73.8 2.3 %all-to-all-done.3 = bf16[16,2,16,128]{3,2,1,0:T(8,128)(2,1)} async-done(((bf16[16,2,16,128]{3,2,1,0:T(8,128)(2,1)}), bf16[16,2,16,128]{3,2,1,0:T(8,128)(2,1)}, u32[]{:S(2)}, u32[]{:S(2)}) %all-to-all-start.3) | async-done | bytes 131104 | tf_op jit(solution)/shard_map/all_to_all | solution.py:192
  76.2 6.6 %all-to-all-start.1 = ((bf16[16,4,2,16,512]{4,3,2,1,0:T(8,128)(2,1)}), bf16[16,4,2,16,512]{4,3,2,1,0:T(8,128)(2,1)}, u32[]{:S(2)}, u32[]{:S(2)}) async-start(bf16[16,4,2,16,512]{4,3,2,1,0:T(8,128)(2,1)} %bitcast.20), calls=%async_computation.1 | async-start | bytes 4194304 | tf_op jit(solution)/shard_map/all_to_all | solution.py:418
  82.7 3.5 %shard_map.55 = bf16[4,4,4,2,16,512]{5,4,3,2,1,0:T(8,128)(2,1)} custom-call(s32[256]{0:T(256)} %owners.5, s32[256]{0:T(256)} %owners.5, bf16[16,4,16,512]{3,2,1,0:T(8,128)(2,1)} %bitcast.16, bf16[16,4,16,512]{3,2,1,0:T(8,128)(2,1)} %bitcast.18), custom_call_target="tpu_custom_call" | custom-call | bytes 4194304 | tf_op jit(solution)/shard_map/pallas_call | solution.py:247
  86.2 24.0 %all-to-all-done.1 = bf16[16,4,2,16,512]{4,3,2,1,0:T(8,128)(2,1)} async-done(((bf16[16,4,2,16,512]{4,3,2,1,0:T(8,128)(2,1)}), bf16[16,4,2,16,512]{4,3,2,1,0:T(8,128)(2,1)}, u32[]{:S(2)}, u32[]{:S(2)}) %all-to-all-start.1) | async-done | bytes 2097184 | tf_op jit(solution)/shard_map/all_to_all | solution.py:418
  110.3 6.2 %all-to-all-start = ((bf16[16,4,2,16,512]{4,3,2,1,0:T(8,128)(2,1)}), bf16[16,4,2,16,512]{4,3,2,1,0:T(8,128)(2,1)}, u32[]{:S(2)}, u32[]{:S(2)}) async-start(bf16[16,4,2,16,512]{4,3,2,1,0:T(8,128)(2,1)} %bitcast.19), calls=%async_computation | async-start | bytes 4194304 | tf_op jit(solution)/shard_map/all_to_all | solution.py:418
  116.5 0.8 collective-permute-start.25
  117.4 3.2 %collective-permute-start.24 = (bf16[4,4,2,16,128]{4,3,2,1,0:T(8,128)(2,1)}, bf16[4,4,2,16,128]{4,3,2,1,0:T(8,128)(2,1)}, u32[]{:S(2)}, u32[]{:S(2)}) collective-permute-start(bf16[4,4,2,16,128]{4,3,2,1,0:T(8,128)(2,1)} %bitcast.13.refs_16_), channel_id=1, source_target_pairs={{0,4},{2,6},{4,0},{6,2},{1,5},{3,7},{5,1},{7,3},{8,12},{10,14},{12... | collective-permute-start | bytes 393224 | tf_op jit(solution)/shard_map/ppermute | solution.py:195
  120.6 3.0 %shard_map.58 = (bf16[2,4,2,16,512]{4,3,2,1,0:T(8,128)(2,1)}, bf16[2,4,2,16,512]{4,3,2,1,0:T(8,128)(2,1)}, bf16[2,4,2,16,512]{4,3,2,1,0:T(8,128)(2,1)}, bf16[2,4...) custom-call(s32[4]{0:T(128)} %pad_add_fusion.at, ...), custom_call_target="tpu_custom_call" | custom-call | bytes 3670016 | tf_op jit(solution)/shard_map/pallas_call | solution.py:284
  123.6 0.1 collective-permute-start.7
  123.6 1.7 collective-permute-start.8
  125.4 0.8 collective-permute-start.9
  126.2 0.0 collective-permute-done.25.refs_19_
  126.2 1.9 collective-permute-start.10
  128.1 0.7 collective-permute-start.23
  128.7 12.1 %all-to-all-done = bf16[16,4,2,16,512]{4,3,2,1,0:T(8,128)(2,1)} async-done(((bf16[16,4,2,16,512]{4,3,2,1,0:T(8,128)(2,1)}), bf16[16,4,2,16,512]{4,3,2,1,0:T(8,128)(2,1)}, u32[]{:S(2)}, u32[]{:S(2)}) %all-to-all-start) | async-done | bytes 2097184 | tf_op jit(solution)/shard_map/all_to_all | solution.py:418
  140.8 2.9 %shard_map.56 = (bf16[2,4,2,16,512]{4,3,2,1,0:T(8,128)(2,1)}, bf16[2,4,2,16,512]{4,3,2,1,0:T(8,128)(2,1)}, bf16[2,4,2,16,512]{4,3,2,1,0:T(8,128)(2,1)}, bf16[2,4...) custom-call(s32[4]{0:T(128)} %pad_add_fusion.at, ...), custom_call_target="tpu_custom_call" | custom-call | bytes 3670016 | tf_op jit(solution)/shard_map/pallas_call | solution.py:284
  143.8 0.2 collective-permute-done.23.refs_17_
  144.0 1.4 collective-permute-start.11
  145.4 0.0 collective-permute-done.7.refs_9_
  145.4 3.8 %collective-permute-start.12 = (bf16[2,4,2,16,512]{4,3,2,1,0:T(8,128)(2,1)}, bf16[2,4,2,16,512]{4,3,2,1,0:T(8,128)(2,1)}, u32[]{:S(2)}, u32[]{:S(2)}) collective-permute-start(bf16[2,4,2,16,512]{4,3,2,1,0:T(8,128)(2,1)} %get-tuple-element.40), channel_id=1, source_target_pairs={{0,4},{1,5},{2,6},{3,7},{4,0},{5,1},{6,2},{7,3},{8,12},{9,13},{10,... | collective-permute-start | bytes 786440 | tf_op jit(solution)/shard_map/ppermute | solution.py:43
  149.2 0.0 collective-permute-done.8.refs_10_
  149.2 0.0 collective-permute-start.13
  149.2 0.5 collective-permute-start
  149.7 1.3 collective-permute-start.1
  151.0 4.2 %collective-permute-done.11.refs_13_ = bf16[2,4,2,16,512]{4,3,2,1,0:T(8,128)(2,1)} collective-permute-done((bf16[2,4,2,16,512]{4,3,2,1,0:T(8,128)(2,1)}, bf16[2,4,2,16,512]{4,3,2,1,0:T(8,128)(2,1)}, u32[]{:S(2)}, u32[]{:S(2)}) %collective-permute-start.11) | collective-permute-done | bytes 262176 | tf_op jit(solution)/shard_map/ppermute | solution.py:43
  155.2 7.1 %collective-permute-done.12.refs_14_ = bf16[2,4,2,16,512]{4,3,2,1,0:T(8,128)(2,1)} collective-permute-done((bf16[2,4,2,16,512]{4,3,2,1,0:T(8,128)(2,1)}, bf16[2,4,2,16,512]{4,3,2,1,0:T(8,128)(2,1)}, u32[]{:S(2)}, u32[]{:S(2)}) %collective-permute-start.12) | collective-permute-done | bytes 262176 | tf_op jit(solution)/shard_map/ppermute | solution.py:43
  162.3 2.0 %collective-permute-start.4 = (bf16[2,4,2,16,512]{4,3,2,1,0:T(8,128)(2,1)}, bf16[2,4,2,16,512]{4,3,2,1,0:T(8,128)(2,1)}, u32[]{:S(2)}, u32[]{:S(2)}) collective-permute-start(bf16[2,4,2,16,512]{4,3,2,1,0:T(8,128)(2,1)} %get-tuple-element.32), channel_id=1, source_target_pairs={{0,6},{1,7},{2,0},{3,1},{4,2},{5,3},{6,4},{7,5},{8,14},{9,15},{10,... | collective-permute-start | bytes 786440 | tf_op jit(solution)/shard_map/ppermute | solution.py:43
  164.3 1.7 collective-permute-done.1.refs_2_
  166.0 0.2 collective-permute-start.6
  166.2 6.5 %collective-permute-done.2.refs_3_ = bf16[2,4,2,16,512]{4,3,2,1,0:T(8,128)(2,1)} collective-permute-done((bf16[2,4,2,16,512]{4,3,2,1,0:T(8,128)(2,1)}, bf16[2,4,2,16,512]{4,3,2,1,0:T(8,128)(2,1)}, u32[]{:S(2)}, u32[]{:S(2)}) %collective-permute-start.2) | collective-permute-done | bytes 262176 | tf_op jit(solution)/shard_map/ppermute | solution.py:43
  172.7 0.3 collective-permute-done.3.refs_4_
  173.0 4.5 %collective-permute-done.4.refs_5_ = bf16[2,4,2,16,512]{4,3,2,1,0:T(8,128)(2,1)} collective-permute-done((bf16[2,4,2,16,512]{4,3,2,1,0:T(8,128)(2,1)}, bf16[2,4,2,16,512]{4,3,2,1,0:T(8,128)(2,1)}, u32[]{:S(2)}, u32[]{:S(2)}) %collective-permute-start.4) | collective-permute-done | bytes 262176 | tf_op jit(solution)/shard_map/ppermute | solution.py:43
  177.5 6.9 %collective-permute-done.5.refs_6_ = bf16[2,4,2,16,512]{4,3,2,1,0:T(8,128)(2,1)} collective-permute-done((bf16[2,4,2,16,512]{4,3,2,1,0:T(8,128)(2,1)}, bf16[2,4,2,16,512]{4,3,2,1,0:T(8,128)(2,1)}, u32[]{:S(2)}, u32[]{:S(2)}) %collective-permute-start.5) | collective-permute-done | bytes 262176 | tf_op jit(solution)/shard_map/ppermute | solution.py:43
  184.3 8.3 %predict.1 = bf16[8,512,512]{2,1,0:T(8,128)(2,1)} custom-call(s32[4]{0:T(128)} %pad_add_fusion.at, s32[256]{0:T(256)} %owners.5, s32[512]{0:T(512)} %reshape.41.octants, bf16[4,4,4,2,16,512]{5,4,3,2,1,0:T(8,128)(2,1)} %bitcast.7.slots.refs_0_, bf16[2,4,2,16,512]{4,3,2,1,0:T(8,128)(2,1)} %collective-permute-done.refs_1_, ...), custom_call_target="tpu_custom_call" | custom-call | flops 3221225472 | bytes 13631488 | tf_op jit(solution)/shard_map/predict/pallas_call | solution.py:381
  (15 shorter events, 0.0 us)
Async XLA Ops:
  3.7 8.9 %collective-permute-start.14 = (bf16[2,2,64,512]{3,2,1,0:T(8,128)(2,1)}, bf16[2,2,64,512]{3,2,1,0:T(8,128)(2,1)S(1)}, u32[]{:S(2)}, u32[]{:S(2)}) collective-permute-start(bf16[2,2,64,512]{3,2,1,0:T(8,128)(2,1)} %get-tuple-element.42), channel_id=1, source_target_pairs={{0,3},{1,2},{2,5},{3,4},{4,7},{5,6},{6,1},{7,0},{8,11},{9,10},{10,... | collective-permute-start | bytes 786440 | tf_op jit(solution)/shard_map/ppermute | solution.py:43
  3.8 10.4 %collective-permute-start.15 = (bf16[2,2,64,512]{3,2,1,0:T(8,128)(2,1)}, bf16[2,2,64,512]{3,2,1,0:T(8,128)(2,1)S(1)}, u32[]{:S(2)}, u32[]{:S(2)}) collective-permute-start(bf16[2,2,64,512]{3,2,1,0:T(8,128)(2,1)} %get-tuple-element.43), channel_id=1, source_target_pairs={{0,7},{1,6},{2,1},{3,0},{4,3},{5,2},{6,5},{7,4},{8,15},{9,14},{10,... | collective-permute-start | bytes 786440 | tf_op jit(solution)/shard_map/ppermute | solution.py:43
  5.5 16.5 %collective-permute-start.16 = (bf16[2,2,64,512]{3,2,1,0:T(8,128)(2,1)}, bf16[2,2,64,512]{3,2,1,0:T(8,128)(2,1)}, u32[]{:S(2)}, u32[]{:S(2)}) collective-permute-start(bf16[2,2,64,512]{3,2,1,0:T(8,128)(2,1)} %get-tuple-element.44), channel_id=1, source_target_pairs={{0,5},{1,4},{2,7},{3,6},{4,1},{5,0},{6,3},{7,2},{8,13},{9,12},{10,... | collective-permute-start | bytes 786440 | tf_op jit(solution)/shard_map/ppermute | solution.py:43
  6.3 17.7 %collective-permute-start.17 = (bf16[2,2,64,512]{3,2,1,0:T(8,128)(2,1)}, bf16[2,2,64,512]{3,2,1,0:T(8,128)(2,1)}, u32[]{:S(2)}, u32[]{:S(2)}) collective-permute-start(bf16[2,2,64,512]{3,2,1,0:T(8,128)(2,1)} %get-tuple-element.45), channel_id=1, source_target_pairs={{0,2},{1,3},{2,4},{3,5},{4,6},{5,7},{6,0},{7,1},{8,10},{9,11},{10,... | collective-permute-start | bytes 786440 | tf_op jit(solution)/shard_map/ppermute | solution.py:43
  8.4 22.5 %collective-permute-start.18 = (bf16[2,2,64,512]{3,2,1,0:T(8,128)(2,1)}, bf16[2,2,64,512]{3,2,1,0:T(8,128)(2,1)}, u32[]{:S(2)}, u32[]{:S(2)}) collective-permute-start(bf16[2,2,64,512]{3,2,1,0:T(8,128)(2,1)} %get-tuple-element.46), channel_id=1, source_target_pairs={{0,6},{1,7},{2,0},{3,1},{4,2},{5,3},{6,4},{7,5},{8,14},{9,15},{10,... | collective-permute-start | bytes 786440 | tf_op jit(solution)/shard_map/ppermute | solution.py:43
  12.6 1.6 copy-start
  12.6 18.3 %collective-permute-start.19 = (bf16[2,2,64,512]{3,2,1,0:T(8,128)(2,1)}, bf16[2,2,64,512]{3,2,1,0:T(8,128)(2,1)}, u32[]{:S(2)}, u32[]{:S(2)}) collective-permute-start(bf16[2,2,64,512]{3,2,1,0:T(8,128)(2,1)} %get-tuple-element.47), channel_id=1, source_target_pairs={{0,4},{1,5},{2,6},{3,7},{4,0},{5,1},{6,2},{7,3},{8,12},{9,13},{10,... | collective-permute-start | bytes 786440 | tf_op jit(solution)/shard_map/ppermute | solution.py:43
  14.2 0.7 copy-start.1
  14.9 16.0 %collective-permute-start.20 = (bf16[2,2,64,512]{3,2,1,0:T(8,128)(2,1)}, bf16[2,2,64,512]{3,2,1,0:T(8,128)(2,1)}, u32[]{:S(2)}, u32[]{:S(2)}) collective-permute-start(bf16[2,2,64,512]{3,2,1,0:T(8,128)(2,1)} %get-tuple-element.48), channel_id=1, source_target_pairs={{0,1},{1,0},{2,3},{3,2},{4,5},{5,4},{6,7},{7,6},{8,9},{9,8},{10,11... | collective-permute-start | bytes 786440 | tf_op jit(solution)/shard_map/ppermute | solution.py:43
  38.3 2.2 %collective-permute-start.21 = (f32[4,256,128]{2,1,0:T(8,128)}, f32[4,256,128]{2,1,0:T(8,128)S(1)}, u32[]{:S(2)}, u32[]{:S(2)}) collective-permute-start(f32[4,256,128]{2,1,0:T(8,128)} %get-tuple-element.50), channel_id=1, source_target_pairs={{0,1},{1,0},{2,3},{3,2},{4,5},{5,4},{6,7},{7,6},{8,9},{9,8},{10,11... | collective-permute-start | bytes 1572872 | tf_op jit(solution)/shard_map/ppermute | solution.py:186
  62.6 1.2 collective-permute-start.22
  64.5 11.6 %all-to-all-start.3 = ((bf16[16,2,16,128]{3,2,1,0:T(8,128)(2,1)}), bf16[16,2,16,128]{3,2,1,0:T(8,128)(2,1)}, u32[]{:S(2)}, u32[]{:S(2)}) async-start(bf16[16,2,16,128]{3,2,1,0:T(8,128)(2,1)} %broadcast_in_dim.2), calls=%async_computation.3 | async-start | bytes 262144 | tf_op jit(solution)/shard_map/all_to_all | solution.py:192
  76.2 34.1 %all-to-all-start.1 = ((bf16[16,4,2,16,512]{4,3,2,1,0:T(8,128)(2,1)}), bf16[16,4,2,16,512]{4,3,2,1,0:T(8,128)(2,1)}, u32[]{:S(2)}, u32[]{:S(2)}) async-start(bf16[16,4,2,16,512]{4,3,2,1,0:T(8,128)(2,1)} %bitcast.20), calls=%async_computation.1 | async-start | bytes 4194304 | tf_op jit(solution)/shard_map/all_to_all | solution.py:418
  110.3 30.6 %all-to-all-start = ((bf16[16,4,2,16,512]{4,3,2,1,0:T(8,128)(2,1)}), bf16[16,4,2,16,512]{4,3,2,1,0:T(8,128)(2,1)}, u32[]{:S(2)}, u32[]{:S(2)}) async-start(bf16[16,4,2,16,512]{4,3,2,1,0:T(8,128)(2,1)} %bitcast.19), calls=%async_computation | async-start | bytes 4194304 | tf_op jit(solution)/shard_map/all_to_all | solution.py:418
  116.5 9.7 %collective-permute-start.25 = (bf16[4,4,2,16,128]{4,3,2,1,0:T(8,128)(2,1)}, bf16[4,4,2,16,128]{4,3,2,1,0:T(8,128)(2,1)}, u32[]{:S(2)}, u32[]{:S(2)}) collective-permute-start(bf16[4,4,2,16,128]{4,3,2,1,0:T(8,128)(2,1)} %bitcast.13.refs_16_), channel_id=1, source_target_pairs={{0,6},{2,0},{4,2},{6,4},{1,7},{3,1},{5,3},{7,5},{8,14},{10,8},{12,... | collective-permute-start | bytes 393224 | tf_op jit(solution)/shard_map/ppermute | solution.py:195
  117.4 10.7 %collective-permute-start.24 = (bf16[4,4,2,16,128]{4,3,2,1,0:T(8,128)(2,1)}, bf16[4,4,2,16,128]{4,3,2,1,0:T(8,128)(2,1)}, u32[]{:S(2)}, u32[]{:S(2)}) collective-permute-start(bf16[4,4,2,16,128]{4,3,2,1,0:T(8,128)(2,1)} %bitcast.13.refs_16_), channel_id=1, source_target_pairs={{0,4},{2,6},{4,0},{6,2},{1,5},{3,7},{5,1},{7,3},{8,12},{10,14},{12... | collective-permute-start | bytes 393224 | tf_op jit(solution)/shard_map/ppermute | solution.py:195
  123.6 21.8 %collective-permute-start.7 = (bf16[2,4,2,16,512]{4,3,2,1,0:T(8,128)(2,1)}, bf16[2,4,2,16,512]{4,3,2,1,0:T(8,128)(2,1)}, u32[]{:S(2)}, u32[]{:S(2)}) collective-permute-start(bf16[2,4,2,16,512]{4,3,2,1,0:T(8,128)(2,1)} %get-tuple-element.35), channel_id=1, source_target_pairs={{0,3},{1,2},{2,5},{3,4},{4,7},{5,6},{6,1},{7,0},{8,11},{9,10},{10,... | collective-permute-start | bytes 786440 | tf_op jit(solution)/shard_map/ppermute | solution.py:43
  123.6 25.5 %collective-permute-start.8 = (bf16[2,4,2,16,512]{4,3,2,1,0:T(8,128)(2,1)}, bf16[2,4,2,16,512]{4,3,2,1,0:T(8,128)(2,1)}, u32[]{:S(2)}, u32[]{:S(2)}) collective-permute-start(bf16[2,4,2,16,512]{4,3,2,1,0:T(8,128)(2,1)} %get-tuple-element.36), channel_id=1, source_target_pairs={{0,7},{1,6},{2,1},{3,0},{4,3},{5,2},{6,5},{7,4},{8,15},{9,14},{10,... | collective-permute-start | bytes 786440 | tf_op jit(solution)/shard_map/ppermute | solution.py:43
  125.4 23.8 %collective-permute-start.9 = (bf16[2,4,2,16,512]{4,3,2,1,0:T(8,128)(2,1)}, bf16[2,4,2,16,512]{4,3,2,1,0:T(8,128)(2,1)}, u32[]{:S(2)}, u32[]{:S(2)}) collective-permute-start(bf16[2,4,2,16,512]{4,3,2,1,0:T(8,128)(2,1)} %get-tuple-element.37), channel_id=1, source_target_pairs={{0,5},{1,4},{2,7},{3,6},{4,1},{5,0},{6,3},{7,2},{8,13},{9,12},{10,... | collective-permute-start | bytes 786440 | tf_op jit(solution)/shard_map/ppermute | solution.py:43
  126.2 23.6 %collective-permute-start.10 = (bf16[2,4,2,16,512]{4,3,2,1,0:T(8,128)(2,1)}, bf16[2,4,2,16,512]{4,3,2,1,0:T(8,128)(2,1)}, u32[]{:S(2)}, u32[]{:S(2)}) collective-permute-start(bf16[2,4,2,16,512]{4,3,2,1,0:T(8,128)(2,1)} %get-tuple-element.38), channel_id=1, source_target_pairs={{0,2},{1,3},{2,4},{3,5},{4,6},{5,7},{6,0},{7,1},{8,10},{9,11},{10,... | collective-permute-start | bytes 786440 | tf_op jit(solution)/shard_map/ppermute | solution.py:43
  128.1 16.0 %collective-permute-start.23 = (bf16[4,4,2,16,128]{4,3,2,1,0:T(8,128)(2,1)}, bf16[4,4,2,16,128]{4,3,2,1,0:T(8,128)(2,1)}, u32[]{:S(2)}, u32[]{:S(2)}) collective-permute-start(bf16[4,4,2,16,128]{4,3,2,1,0:T(8,128)(2,1)} %bitcast.13.refs_16_), channel_id=1, source_target_pairs={{0,2},{2,4},{4,6},{6,0},{1,3},{3,5},{5,7},{7,1},{8,10},{10,12},{12... | collective-permute-start | bytes 393224 | tf_op jit(solution)/shard_map/ppermute | solution.py:195
  144.0 11.2 %collective-permute-start.11 = (bf16[2,4,2,16,512]{4,3,2,1,0:T(8,128)(2,1)}, bf16[2,4,2,16,512]{4,3,2,1,0:T(8,128)(2,1)}, u32[]{:S(2)}, u32[]{:S(2)}) collective-permute-start(bf16[2,4,2,16,512]{4,3,2,1,0:T(8,128)(2,1)} %get-tuple-element.39), channel_id=1, source_target_pairs={{0,6},{1,7},{2,0},{3,1},{4,2},{5,3},{6,4},{7,5},{8,14},{9,15},{10,... | collective-permute-start | bytes 786440 | tf_op jit(solution)/shard_map/ppermute | solution.py:43
  145.4 16.9 %collective-permute-start.12 = (bf16[2,4,2,16,512]{4,3,2,1,0:T(8,128)(2,1)}, bf16[2,4,2,16,512]{4,3,2,1,0:T(8,128)(2,1)}, u32[]{:S(2)}, u32[]{:S(2)}) collective-permute-start(bf16[2,4,2,16,512]{4,3,2,1,0:T(8,128)(2,1)} %get-tuple-element.40), channel_id=1, source_target_pairs={{0,4},{1,5},{2,6},{3,7},{4,0},{5,1},{6,2},{7,3},{8,12},{9,13},{10,... | collective-permute-start | bytes 786440 | tf_op jit(solution)/shard_map/ppermute | solution.py:43
  149.2 13.1 %collective-permute-start.13 = (bf16[2,4,2,16,512]{4,3,2,1,0:T(8,128)(2,1)}, bf16[2,4,2,16,512]{4,3,2,1,0:T(8,128)(2,1)}, u32[]{:S(2)}, u32[]{:S(2)}) collective-permute-start(bf16[2,4,2,16,512]{4,3,2,1,0:T(8,128)(2,1)} %get-tuple-element.41), channel_id=1, source_target_pairs={{0,1},{1,0},{2,3},{3,2},{4,5},{5,4},{6,7},{7,6},{8,9},{9,8},{10,11... | collective-permute-start | bytes 786440 | tf_op jit(solution)/shard_map/ppermute | solution.py:43
  149.2 15.1 %collective-permute-start = (bf16[2,4,2,16,512]{4,3,2,1,0:T(8,128)(2,1)}, bf16[2,4,2,16,512]{4,3,2,1,0:T(8,128)(2,1)}, u32[]{:S(2)}, u32[]{:S(2)}) collective-permute-start(bf16[2,4,2,16,512]{4,3,2,1,0:T(8,128)(2,1)} %get-tuple-element.28), channel_id=1, source_target_pairs={{0,3},{1,2},{2,5},{3,4},{4,7},{5,6},{6,1},{7,0},{8,11},{9,10},{10,... | collective-permute-start | bytes 786440 | tf_op jit(solution)/shard_map/ppermute | solution.py:43
  149.7 16.3 %collective-permute-start.1 = (bf16[2,4,2,16,512]{4,3,2,1,0:T(8,128)(2,1)}, bf16[2,4,2,16,512]{4,3,2,1,0:T(8,128)(2,1)}, u32[]{:S(2)}, u32[]{:S(2)}) collective-permute-start(bf16[2,4,2,16,512]{4,3,2,1,0:T(8,128)(2,1)} %get-tuple-element.29), channel_id=1, source_target_pairs={{0,7},{1,6},{2,1},{3,0},{4,3},{5,2},{6,5},{7,4},{8,15},{9,14},{10,... | collective-permute-start | bytes 786440 | tf_op jit(solution)/shard_map/ppermute | solution.py:43
  155.2 17.5 %collective-permute-start.2 = (bf16[2,4,2,16,512]{4,3,2,1,0:T(8,128)(2,1)}, bf16[2,4,2,16,512]{4,3,2,1,0:T(8,128)(2,1)}, u32[]{:S(2)}, u32[]{:S(2)}) collective-permute-start(bf16[2,4,2,16,512]{4,3,2,1,0:T(8,128)(2,1)} %get-tuple-element.30), channel_id=1, source_target_pairs={{0,5},{1,4},{2,7},{3,6},{4,1},{5,0},{6,3},{7,2},{8,13},{9,12},{10,... | collective-permute-start | bytes 786440 | tf_op jit(solution)/shard_map/ppermute | solution.py:43
  162.3 10.7 %collective-permute-start.3 = (bf16[2,4,2,16,512]{4,3,2,1,0:T(8,128)(2,1)}, bf16[2,4,2,16,512]{4,3,2,1,0:T(8,128)(2,1)}, u32[]{:S(2)}, u32[]{:S(2)}) collective-permute-start(bf16[2,4,2,16,512]{4,3,2,1,0:T(8,128)(2,1)} %get-tuple-element.31), channel_id=1, source_target_pairs={{0,2},{1,3},{2,4},{3,5},{4,6},{5,7},{6,0},{7,1},{8,10},{9,11},{10,... | collective-permute-start | bytes 786440 | tf_op jit(solution)/shard_map/ppermute | solution.py:43
  162.3 15.2 %collective-permute-start.4 = (bf16[2,4,2,16,512]{4,3,2,1,0:T(8,128)(2,1)}, bf16[2,4,2,16,512]{4,3,2,1,0:T(8,128)(2,1)}, u32[]{:S(2)}, u32[]{:S(2)}) collective-permute-start(bf16[2,4,2,16,512]{4,3,2,1,0:T(8,128)(2,1)} %get-tuple-element.32), channel_id=1, source_target_pairs={{0,6},{1,7},{2,0},{3,1},{4,2},{5,3},{6,4},{7,5},{8,14},{9,15},{10,... | collective-permute-start | bytes 786440 | tf_op jit(solution)/shard_map/ppermute | solution.py:43
  164.3 20.0 %collective-permute-start.5 = (bf16[2,4,2,16,512]{4,3,2,1,0:T(8,128)(2,1)}, bf16[2,4,2,16,512]{4,3,2,1,0:T(8,128)(2,1)}, u32[]{:S(2)}, u32[]{:S(2)}) collective-permute-start(bf16[2,4,2,16,512]{4,3,2,1,0:T(8,128)(2,1)} %get-tuple-element.33), channel_id=1, source_target_pairs={{0,4},{1,5},{2,6},{3,7},{4,0},{5,1},{6,2},{7,3},{8,12},{9,13},{10,... | collective-permute-start | bytes 786440 | tf_op jit(solution)/shard_map/ppermute | solution.py:43
  166.0 18.3 %collective-permute-start.6 = (bf16[2,4,2,16,512]{4,3,2,1,0:T(8,128)(2,1)}, bf16[2,4,2,16,512]{4,3,2,1,0:T(8,128)(2,1)}, u32[]{:S(2)}, u32[]{:S(2)}) collective-permute-start(bf16[2,4,2,16,512]{4,3,2,1,0:T(8,128)(2,1)} %get-tuple-element.34), channel_id=1, source_target_pairs={{0,1},{1,0},{2,3},{3,2},{4,5},{5,4},{6,7},{7,6},{8,9},{9,8},{10,11... | collective-permute-start | bytes 786440 | tf_op jit(solution)/shard_map/ppermute | solution.py:43
